TPU v7x, 32 devices: a whole 2x2x4 slice. The times are simulated.
32 devices in a mesh: grp: 2 (over y), tgt: 4 (over z), src: 4 (over x, core).
Axes of the slice: x: 2, y: 2, z: 4, core: 2. Of those that a mesh axis runs over, the one named last changes fastest.
Arguments:
- target_rows: bfloat16 [2048, 4608], P(('grp', 'tgt', 'src')), parts along dimension 0, may hold values from -6 to 6
- target_pos: int32 [2048], P(('grp', 'tgt')), parts along dimension 0, may hold values from 0 to 255
- decoder_rows: bfloat16 [512, 4608], P(('grp', 'tgt', 'src')), parts along dimension 0, may hold values from -0.09375 to 0.09375
- source_pos: int32 [512], P('grp'), parts along dimension 0, may hold values from 0 to 255
- out_proj: bfloat16 [32, 4608, 128], P('src', 'tgt'), may hold values from -0.09375 to 0.09375
- value_proj: bfloat16 [16, 4608, 128], P('src'), may hold values from -1 to 1
- attention: bfloat16 [64, 256, 256], P(('grp', 'src'), 'tgt'), parts along dimension 0, may hold values from 0 to 1, as said below
- tile_pattern: int32 [8, 4], P('grp'), parts along dimension 0, may hold values from 0 to 1, as said below
Outputs:
- edges: bfloat16 [512, 1024], P(('grp', 'src'), 'tgt'), parts along dimension 0
There are 2 independent parts, one for each index of `grp`. A program takes and returns all parts, laid end to end along the dimension named above; an argument that names none is the same for every part. Nothing has to cross between parts.
Inputs may be any that keep to these rules, and one draw needn't show every extreme that they name: Each row attention[h, p, :] is a probability distribution over the keys 0 to p: zero beyond p, summing to one. tile_pattern[b, c] is 1 where the tile of edges between source block b and target block c is kept, else 0.
All inputs are finite; a program needn't handle non-finite values.
Results may differ from a plain program's by a relative error of at most 0.0057.
Values may be sent and summed in bfloat16 or wider, within the bound.
No kernel may reach another device: no remote copies, remote signals or barrier semaphores. Data moves between devices by JAX's collectives and lax.ppermute only.
A program may use at most 64 MiB of HBM per device.

v0:
```python
import functools

import jax
import jax.numpy as jnp
from jax import lax
from jax.experimental import pallas as pl
from jax.experimental.pallas import tpu as pltpu
from jax.sharding import PartitionSpec as P


F32 = jnp.float32
BF16 = jnp.bfloat16
VMEM_BYTES = 24 << 20


def passed_along(value, axis, steps):
    count = lax.axis_size(axis)
    pairs = [(source, (source + steps) % count) for source in range(count)]
    return lax.ppermute(value, axis, pairs)


def swapped(value, axis, bit):
    pairs = [(source, source ^ bit) for source in range(lax.axis_size(axis))]
    return lax.ppermute(value, axis, pairs)


def kernel_call(body, outs, args, flops, moved, scratch=(), smem=(), hbm=()):
    return pl.pallas_call(
        body,
        out_shape=outs,
        in_specs=[
            pl.BlockSpec(
                memory_space=pltpu.SMEM if i in smem else pltpu.HBM if i in hbm else pltpu.VMEM
            )
            for i in range(len(args))
        ],
        out_specs=jax.tree.map(lambda _: pl.BlockSpec(memory_space=pltpu.VMEM), outs),
        scratch_shapes=scratch,
        compiler_params=pltpu.CompilerParams(vmem_limit_bytes=VMEM_BYTES),
        cost_estimate=pl.CostEstimate(flops=flops, bytes_accessed=moved, transcendentals=0),
    )(*args)


def aligned(start, size):
    return pl.ds(pl.multiple_of(start, size), size)


def pair_of(ref, first, rows=slice(None)):
    return jnp.concatenate([ref[first, rows, :], ref[first + 1, rows, :]], axis=-1)


def origin_of(z, k):
    return jnp.where(z >= k, z - k, z - k + 4)


def source_row(z, k, block):
    b = origin_of(z, k)
    return (b % 2) * (2 * block) + (b // 2) * block


def cut_kernel(targets, sources, own, first, second, third, done):
    z = lax.axis_index("tgt")
    rows, sub = targets.shape[0], sources.shape[0]
    part = own.shape[1]

    def columns(index):
        return pl.ds(pl.multiple_of(index * part, 128), part)

    moves = [(targets.at[:, columns(z)], own.at[pl.ds(0, rows)])]
    for k, out in enumerate((first, second, third), 1):
        at = columns(jnp.where(z + k >= 4, z + k - 4, z + k))
        moves.append((targets.at[:, at], out.at[pl.ds(0, rows)]))
        moves.append((sources.at[:, at], out.at[pl.ds(rows, sub)]))
    for i in range(4):
        moves.append((sources.at[:, pl.ds(i * part, part)], own.at[pl.ds(rows + i * sub, sub)]))
    copies = [pltpu.make_async_copy(*ends, done.at[i]) for i, ends in enumerate(moves)]
    for copy in copies:
        copy.start()
    for copy in copies:
        copy.wait()


def by_core(positions):
    quarter = positions.shape[1] // 4
    return jnp.concatenate(
        [positions[:, b * quarter : (b + 1) * quarter] for b in (0, 2, 1, 3)], axis=1
    )


def table_kernel(attn, spos, tpos, out):
    heads, queries, keys = attn.shape
    base = heads * queries
    picks = lax.broadcasted_iota(jnp.int32, (keys, spos.shape[1]), 0) == by_core(spos[...])
    picks = picks.astype(F32).astype(BF16)
    table = attn[...].reshape(base, keys)
    out[0:base, :] = jnp.dot(table, picks, preferred_element_type=F32).astype(BF16)
    out[base:, :] = jnp.broadcast_to(
        tpos[...].astype(F32), (out.shape[0] - base, tpos.shape[1])
    ).astype(BF16)


def values_kernel(rows, own, core, far, cross, value, out):
    s = lax.axis_index("src")
    sub = (own.shape[0] - rows) // 4
    part = own.shape[1]
    for pair in range(value.shape[0] // 2):
        total = None
        for i in range(4):
            at = slice(rows + i * sub, rows + (i + 1) * sub)
            left = jnp.concatenate([ref[at, :] for ref in (own, core, far, cross)], axis=0)
            got = jnp.dot(
                left,
                pair_of(value, 2 * pair, slice(i * part, (i + 1) * part)),
                preferred_element_type=F32,
            )
            total = got if total is None else total + got
        width = total.shape[1]
        for j in range(4):
            out[aligned((s ^ j) * sub, sub), pair * width : (pair + 1) * width] = total[
                j * sub : (j + 1) * sub, :
            ].astype(BF16)


def reads_kernel(rows, *refs):
    pieces, weight, reads, direct, dec = refs[:16], refs[16], refs[17], refs[18], refs[19]
    z, s = lax.axis_index("tgt"), lax.axis_index("src")
    sub = pieces[4].shape[0] - rows
    block = 4 * sub
    dec[...] = jnp.zeros_like(dec)
    for k in range(4):
        if k:
            piece = pieces[4 * k][rows:, :]
        else:
            piece = pieces[0][aligned(rows + sub * z, sub), :]
        dec[aligned(source_row(z, k, block) + sub * s, sub), :] = piece
    width = 2 * weight.shape[2]
    group = 4 * rows

    def put(k, target, cols, value):
        for j in range(4):
            target[aligned(k * group + (s ^ j) * rows, rows), cols] = value[
                j * rows : (j + 1) * rows
            ].astype(target.dtype)

    lefts = [
        jnp.concatenate([ref[0:rows, :] for ref in pieces[4 * k : 4 * k + 4]], axis=0)
        for k in range(4)
    ]
    for pair in range(weight.shape[0] // 2):
        right = pair_of(weight, 2 * pair)
        for k in range(4):
            got = jnp.dot(lefts[k], right, preferred_element_type=F32)
            put(k, reads, slice(pair * width, (pair + 1) * width), got)
    for k in range(4):
        got = lax.dot_general(
            lefts[k], dec[...], (((1,), (1,)), ((), ())), preferred_element_type=F32
        )
        put(k, direct, slice(0, direct.shape[1]), got)


def edges_kernel(heads, queries, flip, *refs):
    home, right1, right2, right3, left1, left2, left3 = refs[:7]
    blocks_of_values = refs[7:11]
    reads, direct, spos, out, table, values = refs[11:]
    z, s = lax.axis_index("tgt"), lax.axis_index("src")
    side = (s % 2) ^ flip
    sources = spos.shape[1]
    half = sources // 2
    block = sources // 4
    ordered = by_core(spos[...])
    wide = 2 * (reads.shape[1] // heads)
    dim = wide // 2
    pairs = heads // 2
    table[0] = home[...]
    for k, (near, other) in enumerate(((right1, left3), (right2, left2), (right3, left1)), 1):

        @pl.when(z >= k)
        def _(k=k, near=near):
            table[k] = near[...]

        @pl.when(z < k)
        def _(k=k, other=other):
            table[k] = other[...]

    for k in range(4):
        values[aligned(source_row(z, k, block), block), :] = blocks_of_values[k][...]
    lanes = aligned(side * half, half)
    grid_q = jnp.concatenate(
        [
            lax.broadcasted_iota(jnp.int32, (queries, sources), 0) + origin_of(z, k) * queries
            for k in range(4)
        ],
        axis=0,
    )
    near = ordered[:, :half]
    near = jnp.where(side == 0, near, ordered[:, half:])
    picks = (grid_q[:, :half] == near).astype(F32).astype(BF16)
    blank = jnp.zeros((dim, half), BF16)
    scorers, tables = [], []
    for pair in range(pairs):
        turned = values[lanes, pair * dim : (pair + 1) * dim].astype(F32).T.astype(BF16)
        scorers.append(
            jnp.concatenate(
                [
                    jnp.concatenate([turned, blank], axis=1),
                    jnp.concatenate([blank, turned], axis=1),
                ],
                axis=0,
            )
        )
        tables.append(
            jnp.concatenate(
                [
                    jnp.concatenate(
                        [table[k, h * queries : (h + 1) * queries, lanes] for k in range(4)], axis=0
                    )
                    for h in (2 * pair, 2 * pair + 1)
                ],
                axis=1,
            )
        )
    for k in range(4):
        tpos = table[k, table.shape[1] - 16 : table.shape[1], :].astype(F32)[0:1].astype(jnp.int32)
        hot = (grid_q == tpos).astype(F32).T.astype(BF16)
        here = slice(k * sources, (k + 1) * sources)
        running = None
        for pair in range(pairs):
            weights = jnp.dot(hot, tables[pair], preferred_element_type=F32)
            scores = jnp.dot(
                reads[here, pair * wide : (pair + 1) * wide],
                scorers[pair],
                preferred_element_type=F32,
            )
            term = weights * scores
            running = term if running is None else running + term
        mixed = running[:, :half] + running[:, half:]
        same = jnp.dot(hot, picks, preferred_element_type=F32)
        turned = (mixed + same * direct[here, lanes]).T
        for x in range(2):
            row = jnp.where(s // 2 == x, block, 0)
            out[aligned(row, block), here] = turned[x * block : (x + 1) * block, :]


def finish_kernel(pattern, mine, first, second, third, out):
    kept = pattern[lax.axis_index("src"), lax.axis_index("tgt")].astype(F32)
    total = mine[...]
    for ref in (first, second, third):
        total = total + ref[...].astype(F32)
    out[...] = (total * kept).astype(BF16)


def resident(
    target_rows, target_pos, decoder_rows, source_pos, out_proj, value_proj, attention, tile_pattern
):
    blocks = lax.axis_size("tgt")
    rows, depth = target_rows.shape
    sub = decoder_rows.shape[0]
    part = depth // blocks
    heads, _, head_dim = out_proj.shape
    groups = value_proj.shape[0]
    queries = attention.shape[1]
    sources = source_pos.shape[0]
    targets = target_pos.shape[0]
    block = sources // blocks

    def shape(*dims, dtype=BF16):
        return jax.ShapeDtypeStruct(dims, dtype)

    cut = kernel_call(
        cut_kernel,
        (shape(rows + 4 * sub, part),) + (shape(rows + sub, part),) * 3,
        [target_rows, decoder_rows],
        0,
        target_rows.size * 4,
        [pltpu.SemaphoreType.DMA((11,))],
        hbm=(0, 1),
    )
    own, far, core, cross = [cut[0]], [], [], []
    for k in range(1, blocks):
        own.append(passed_along(cut[k], "tgt", k))
    for k in range(blocks):
        far.append(swapped(own[k], "src", 2))
        core.append(swapped(own[k], "src", 1))
        cross.append(swapped(far[k], "src", 1))

    spots = source_pos[None, :]
    home = kernel_call(
        table_kernel,
        shape(heads * queries + 16, sources),
        [attention, spots, target_pos[None, :]],
        2 * attention.size * sources,
        attention.size * 4,
    )
    rightward, leftward = [home], [home]
    for step in range(1, blocks):
        up = [(i, i + 1) for i in range(step - 1, blocks - 1)]
        down = [(blocks - 1 - i, blocks - 2 - i) for i in range(step - 1, blocks - 1)]
        rightward.append(lax.ppermute(rightward[-1], "tgt", up))
        leftward.append(lax.ppermute(leftward[-1], "tgt", down))
    values = [
        kernel_call(
            functools.partial(values_kernel, rows),
            shape(block, groups * head_dim),
            [own[0], core[0], far[0], cross[0], value_proj],
            2 * block * depth * groups * head_dim,
            value_proj.size * 2,
        )
    ]
    for k in range(1, blocks):
        values.append(passed_along(values[0], "tgt", k))

    reads, direct = kernel_call(
        functools.partial(reads_kernel, rows),
        (
            shape(blocks * targets, heads * head_dim),
            shape(blocks * targets, sources, dtype=F32),
        ),
        [a[k] for k in range(blocks) for a in (own, core, far, cross)] + [out_proj],
        2 * blocks * targets * part * (heads * head_dim + sources),
        out_proj.size * 2,
        [pltpu.VMEM((sources, part), BF16)],
    )

    def edges(flip):
        return kernel_call(
            functools.partial(edges_kernel, heads, queries, flip),
            shape(sources // 2, blocks * targets, dtype=F32),
            [home, *rightward[1:], *leftward[1:], *values, reads, direct, spots],
            2 * 2 * blocks * targets * sources * heads * head_dim,
            1 << 22,
            [pltpu.VMEM((4,) + home.shape, BF16), pltpu.VMEM((sources, groups * head_dim), BF16)],
        )

    away = swapped(edges(1), "src", 1)
    kept = edges(0)
    back = swapped((kept[:block] + away[:block]).astype(BF16), "src", 2)
    mine = kept[block:] + away[block:] + back.astype(F32)
    parts = [mine[:, k * targets : (k + 1) * targets] for k in range(blocks)]
    landed = [passed_along(parts[k].astype(BF16), "tgt", -k) for k in range(1, blocks)]
    return kernel_call(
        finish_kernel,
        shape(block, targets),
        [tile_pattern, parts[0], *landed],
        4 * block * targets,
        block * targets * 12,
        smem=(0,),
    )


def ring(
    target_rows, target_pos, decoder_rows, source_pos, out_proj, value_proj, attention, tile_pattern
):
    blocks = lax.axis_size("tgt")
    column = lax.axis_index("tgt")
    src_lane = lax.axis_index("src")
    full_targets, full_sources = (
        lax.all_gather(target_rows, "src", axis=0, tiled=True),
        lax.all_gather(decoder_rows, "src", axis=0, tiled=True),
    )
    tgt_dev = full_targets.shape[0]
    src_dev = full_sources.shape[0]
    sub_rows = decoder_rows.shape[0]
    heads_here = out_proj.shape[0]
    head_dim = out_proj.shape[2]
    groups_here = value_proj.shape[0]
    repeat = heads_here // groups_here
    read_sum = jnp.einsum(
        "td,hde->the",
        full_targets,
        lax.all_gather(out_proj, "tgt", axis=1, tiled=True),
        preferred_element_type=jnp.float32,
    )
    head_reads = read_sum.astype(jnp.bfloat16).reshape(tgt_dev, groups_here, repeat, head_dim)
    values = jnp.einsum("sd,gde->sge", full_sources, value_proj, preferred_element_type=jnp.float32)
    values = values.astype(jnp.bfloat16).reshape(src_dev, groups_here * head_dim)
    attn_table = lax.all_gather(attention, "tgt", axis=1, tiled=True)
    target_attn = jnp.take(attn_table, target_pos, axis=1)
    keyed_attn = jnp.transpose(target_attn, (0, 2, 1))

    def edge_tile(payload, block_index):
        decoder_part, value_part = payload
        key_positions = lax.dynamic_slice_in_dim(source_pos, block_index * src_dev, src_dev)
        weights = jnp.take(keyed_attn, key_positions, axis=1).astype(jnp.float32)
        scores = jnp.einsum(
            "sgd,tgrd->grst",
            value_part.reshape(src_dev, groups_here, head_dim),
            head_reads,
            preferred_element_type=jnp.float32,
        )
        scores = scores.reshape(heads_here, src_dev, tgt_dev)
        mixed_term = jnp.sum(weights * scores, axis=0)
        own_positions = lax.dynamic_slice_in_dim(key_positions, src_lane * sub_rows, sub_rows)
        same_place = (own_positions[:, None] == target_pos[None, :]).astype(jnp.float32)
        direct = (
            jnp.einsum("sd,td->st", decoder_part, full_targets, preferred_element_type=jnp.float32)
            * same_place
        )
        own_rows = lax.dynamic_slice_in_dim(mixed_term, src_lane * sub_rows, sub_rows, 0)
        return lax.dynamic_update_slice_in_dim(
            mixed_term, own_rows + direct, src_lane * sub_rows, 0
        )

    def place_tile(partial_value, payload, block_index):
        kept_flag = tile_pattern[block_index, column]
        piece_tile = edge_tile(payload, block_index) * kept_flag.astype(jnp.float32)
        return lax.dynamic_update_slice_in_dim(partial_value, piece_tile, block_index * src_dev, 0)

    own_block = (decoder_rows, values)
    partial_value = jnp.zeros((blocks * src_dev, tgt_dev), jnp.float32)
    partial_value = place_tile(partial_value, own_block, column)

    def cycle_turn(turn_index, state_carry):
        forward_block, backward_block, running = state_carry
        forward_block = passed_along((forward_block[0], forward_block[1]), "tgt", 1)
        backward_block = passed_along((backward_block[0], backward_block[1]), "tgt", -1)
        running = place_tile(running, forward_block, (column - turn_index) % blocks)
        running = place_tile(running, backward_block, (column + turn_index) % blocks)
        return (forward_block, backward_block, running)

    forward_block, _, partial_value = lax.fori_loop(
        1, blocks // 2, cycle_turn, (own_block, own_block, partial_value)
    )
    forward_block = passed_along((forward_block[0], forward_block[1]), "tgt", 1)
    partial_value = place_tile(partial_value, forward_block, (column - blocks // 2) % blocks)
    summed = lax.psum_scatter(partial_value, "src", scatter_dimension=0, tiled=True)
    return summed.astype(jnp.bfloat16)


def shards(*args):
    target_rows, target_pos, decoder_rows, source_pos, out_proj, value_proj, attention, _ = args
    blocks, lanes = lax.axis_size("tgt"), lax.axis_size("src")
    heads, groups = out_proj.shape[0], value_proj.shape[0]
    fits = (
        blocks == 4
        and lanes == 4
        and out_proj.shape[1] % 128 == 0
        and out_proj.shape[2] == 128
        and heads == 2 * groups
        and groups % 2 == 0
        and source_pos.shape[0] == target_pos.shape[0] == attention.shape[2] == 256
        and target_rows.shape[0] % 16 == 0
        and decoder_rows.shape[0] % 16 == 0
        and attention.shape[1] % 16 == 0
    )
    if not fits:
        return ring(*args)
    return resident(*args)


def solution(mesh):
    return jax.shard_map(
        shards,
        mesh=mesh,
        in_specs=(
            P(("grp", "tgt", "src"), None),
            P(("grp", "tgt")),
            P(("grp", "tgt", "src"), None),
            P("grp"),
            P("src", "tgt", None),
            P("src", None, None),
            P(("grp", "src"), "tgt", None),
            P("grp", None),
        ),
        out_specs=P(("grp", "src"), "tgt"),
        check_vma=False,
    )
```

profile of v0, /device:TPU:0, one launch (start us, length us, event | category | flops | bytes accessed | tf_op | source)
XLA Modules:
  0.0 80.6 jit_solution(9737306170798730275)
XLA Ops:
  0.0 1.1 %copy-done.1 = bf16[64,4608]{1,0:T(8,128)(2,1)S(1)} copy-done((bf16[64,4608]{1,0:T(8,128)(2,1)S(1)}, bf16[64,4608]{1,0:T(8,128)(2,1)}, u32[]{:S(2)}) %copy-start.1) | copy-done | bytes 589848
  1.1 0.9 %copy-done.3 = bf16[16,4608]{1,0:T(8,128)(2,1)S(1)} copy-done((bf16[16,4608]{1,0:T(8,128)(2,1)S(1)}, bf16[16,4608]{1,0:T(8,128)(2,1)}, u32[]{:S(2)}) %copy-start.3) | copy-done | bytes 147480
  2.3 3.1 %collective-permute-start.12 = (bf16[80,1152]{1,0:T(8,128)(2,1)S(1)}, bf16[80,1152]{1,0:T(8,128)(2,1)S(1)}, u32[]{:S(2)}, u32[]{:S(2)}) collective-permute-start(bf16[80,1152]{1,0:T(8,128)(2,1)S(1)} %get-tuple-element.12), channel_id=1, source_target_pairs={{0,4},{4,8},{8,12},{12,0},{1,5},{5,9},{9,13},{13,1},{2,6},{6,10},{... | collective-permute-start | bytes 552968 | tf_op jit(solution)/shard_map/ppermute | solution.py:19
  5.4 2.6 %collective-permute-start.16 = (bf16[80,1152]{1,0:T(8,128)(2,1)S(1)}, bf16[80,1152]{1,0:T(8,128)(2,1)S(1)}, u32[]{:S(2)}, u32[]{:S(2)}) collective-permute-start(bf16[80,1152]{1,0:T(8,128)(2,1)S(1)} %get-tuple-element.13), channel_id=1, source_target_pairs={{0,8},{4,12},{8,0},{12,4},{1,9},{5,13},{9,1},{13,5},{2,10},{6,14},... | collective-permute-start | bytes 552968 | tf_op jit(solution)/shard_map/ppermute | solution.py:19
  8.0 0.9 %copy-done.2 = bf16[8,64,256]{2,1,0:T(8,128)(2,1)S(1)} copy-done((bf16[8,64,256]{2,1,0:T(8,128)(2,1)S(1)}, bf16[8,64,256]{2,1,0:T(8,128)(2,1)}, u32[]{:S(2)}) %copy-start.2) | copy-done | bytes 262168
  10.6 2.0 %collective-permute-start = (bf16[528,256]{1,0:T(8,128)(2,1)S(1)}, bf16[528,256]{1,0:T(8,128)(2,1)S(1)}, u32[]{:S(2)}, u32[]{:S(2)}) collective-permute-start(bf16[528,256]{1,0:T(8,128)(2,1)S(1)} %shard_map.82.refs_0_), channel_id=1, source_target_pairs={{0,4},{4,8},{8,12},{1,5},{5,9},{9,13},{2,6},{6,10},{10,14},{3,7},{... | collective-permute-start | bytes 811016 | tf_op jit(solution)/shard_map/ppermute | solution.py:298
  12.6 1.7 %collective-permute-start.7 = (bf16[128,1152]{1,0:T(8,128)(2,1)S(1)}, bf16[128,1152]{1,0:T(8,128)(2,1)S(1)}, u32[]{:S(2)}, u32[]{:S(2)}) collective-permute-start(bf16[128,1152]{1,0:T(8,128)(2,1)S(1)} %get-tuple-element.11.own.refs_0_), channel_id=1, source_target_pairs={{0,2},{1,3},{2,0},{3,1},{4,6},{5,7},{6,4},{7,5},{8,10},{9,11},{10,... | collective-permute-start | bytes 884744 | tf_op jit(solution)/shard_map/ppermute | solution.py:24
  14.8 5.3 %collective-permute-done.16.refs_8_ = bf16[80,1152]{1,0:T(8,128)(2,1)S(1)} collective-permute-done((bf16[80,1152]{1,0:T(8,128)(2,1)S(1)}, bf16[80,1152]{1,0:T(8,128)(2,1)S(1)}, u32[]{:S(2)}, u32[]{:S(2)}) %collective-permute-start.16) | collective-permute-done | bytes 184352 | tf_op jit(solution)/shard_map/ppermute | solution.py:19
  20.1 1.3 %collective-permute-start.3 = (bf16[528,256]{1,0:T(8,128)(2,1)S(1)}, bf16[528,256]{1,0:T(8,128)(2,1)S(1)}, u32[]{:S(2)}, u32[]{:S(2)}) collective-permute-start(bf16[528,256]{1,0:T(8,128)(2,1)S(1)} %shard_map.82.refs_0_), channel_id=1, source_target_pairs={{12,8},{8,4},{4,0},{13,9},{9,5},{5,1},{14,10},{10,6},{6,2},{15,11}... | collective-permute-start | bytes 811016 | tf_op jit(solution)/shard_map/ppermute | solution.py:299
  21.4 2.5 %collective-permute-done.20.refs_12_ = bf16[80,1152]{1,0:T(8,128)(2,1)S(1)} collective-permute-done((bf16[80,1152]{1,0:T(8,128)(2,1)S(1)}, bf16[80,1152]{1,0:T(8,128)(2,1)S(1)}, u32[]{:S(2)}, u32[]{:S(2)}) %collective-permute-start.20) | collective-permute-done | bytes 184352 | tf_op jit(solution)/shard_map/ppermute | solution.py:19
  24.0 1.5 %collective-permute-start.14 = (bf16[80,1152]{1,0:T(8,128)(2,1)S(1)}, bf16[80,1152]{1,0:T(8,128)(2,1)S(1)}, u32[]{:S(2)}, u32[]{:S(2)}) collective-permute-start(bf16[80,1152]{1,0:T(8,128)(2,1)S(1)} %collective-permute-done.12.refs_4_), channel_id=1, source_target_pairs={{0,2},{1,3},{2,0},{3,1},{4,6},{5,7},{6,4},{7,5},{8,10},{9,11},{10,... | collective-permute-start | bytes 552968 | tf_op jit(solution)/shard_map/ppermute | solution.py:24
  26.0 4.3 %collective-permute-done.3.refs_4_ = bf16[528,256]{1,0:T(8,128)(2,1)S(1)} collective-permute-done((bf16[528,256]{1,0:T(8,128)(2,1)S(1)}, bf16[528,256]{1,0:T(8,128)(2,1)S(1)}, u32[]{:S(2)}, u32[]{:S(2)}) %collective-permute-start.3) | collective-permute-done | bytes 270368 | tf_op jit(solution)/shard_map/ppermute | solution.py:299
  30.3 1.5 %collective-permute-start.22 = (bf16[80,1152]{1,0:T(8,128)(2,1)S(1)}, bf16[80,1152]{1,0:T(8,128)(2,1)S(1)}, u32[]{:S(2)}, u32[]{:S(2)}) collective-permute-start(bf16[80,1152]{1,0:T(8,128)(2,1)S(1)} %collective-permute-done.20.refs_12_), channel_id=1, source_target_pairs={{0,2},{1,3},{2,0},{3,1},{4,6},{5,7},{6,4},{7,5},{8,10},{9,11},{10,... | collective-permute-start | bytes 552968 | tf_op jit(solution)/shard_map/ppermute | solution.py:24
  32.3 3.1 %collective-permute-done.18.refs_10_ = bf16[80,1152]{1,0:T(8,128)(2,1)S(1)} collective-permute-done((bf16[80,1152]{1,0:T(8,128)(2,1)S(1)}, bf16[80,1152]{1,0:T(8,128)(2,1)S(1)}, u32[]{:S(2)}, u32[]{:S(2)}) %collective-permute-start.18) | collective-permute-done | bytes 184352 | tf_op jit(solution)/shard_map/ppermute | solution.py:24
  35.4 3.1 %collective-permute-done.22.refs_14_ = bf16[80,1152]{1,0:T(8,128)(2,1)S(1)} collective-permute-done((bf16[80,1152]{1,0:T(8,128)(2,1)S(1)}, bf16[80,1152]{1,0:T(8,128)(2,1)S(1)}, u32[]{:S(2)}, u32[]{:S(2)}) %collective-permute-start.22) | collective-permute-done | bytes 184352 | tf_op jit(solution)/shard_map/ppermute | solution.py:24
  39.2 1.3 %collective-permute-start.4 = (bf16[528,256]{1,0:T(8,128)(2,1)S(1)}, bf16[528,256]{1,0:T(8,128)(2,1)S(1)}, u32[]{:S(2)}, u32[]{:S(2)}) collective-permute-start(bf16[528,256]{1,0:T(8,128)(2,1)S(1)} %collective-permute-done.3.refs_4_), channel_id=1, source_target_pairs={{8,4},{4,0},{9,5},{5,1},{10,6},{6,2},{11,7},{7,3},{24,20},{20,16},... | collective-permute-start | bytes 811016 | tf_op jit(solution)/shard_map/ppermute | solution.py:299
  41.1 2.3 %copy-done = bf16[4,4608,128]{2,1,0:T(8,128)(2,1)S(1)} copy-done((bf16[4,4608,128]{2,1,0:T(8,128)(2,1)S(1)}, bf16[4,4608,128]{2,1,0:T(8,128)(2,1)}, u32[]{:S(2)}) %copy-start) | copy-done | bytes 4718616
  43.5 0.9 %shard_map.84.refs_7_ = bf16[64,512]{1,0:T(8,128)(2,1)S(1)} custom-call(bf16[128,1152]{1,0:T(8,128)(2,1)S(1)} %get-tuple-element.11.own.refs_0_, bf16[128,1152]{1,0:T(8,128)(2,1)S(1)} %collective-permute-done.6.core.refs_1_, bf16[128,1152]{1,0:T(8,128)(2,1)S(1)} %collective-permute-done.7.far.refs_2_, ...), custom_call_target="tpu_custom_call" | custom-call | flops 301989888 | bytes 4718592 | tf_op jit(solution)/shard_map/pallas_call | solution.py:28
  45.1 4.8 %collective-permute-done.4.refs_5_ = bf16[528,256]{1,0:T(8,128)(2,1)S(1)} collective-permute-done((bf16[528,256]{1,0:T(8,128)(2,1)S(1)}, bf16[528,256]{1,0:T(8,128)(2,1)S(1)}, u32[]{:S(2)}, u32[]{:S(2)}) %collective-permute-start.4) | collective-permute-done | bytes 270368 | tf_op jit(solution)/shard_map/ppermute | solution.py:299
  49.9 1.3 %collective-permute-start.5 = (bf16[528,256]{1,0:T(8,128)(2,1)S(1)}, bf16[528,256]{1,0:T(8,128)(2,1)S(1)}, u32[]{:S(2)}, u32[]{:S(2)}) collective-permute-start(bf16[528,256]{1,0:T(8,128)(2,1)S(1)} %collective-permute-done.4.refs_5_), channel_id=1, source_target_pairs={{4,0},{5,1},{6,2},{7,3},{20,16},{21,17},{22,18},{23,19}} | collective-permute-start | bytes 811016 | tf_op jit(solution)/shard_map/ppermute | solution.py:299
  51.2 1.7 %collective-permute-start.10 = (bf16[64,512]{1,0:T(8,128)(2,1)S(1)}, bf16[64,512]{1,0:T(8,128)(2,1)S(1)}, u32[]{:S(2)}, u32[]{:S(2)}) collective-permute-start(bf16[64,512]{1,0:T(8,128)(2,1)S(1)} %shard_map.84.refs_7_), channel_id=1, source_target_pairs={{0,8},{4,12},{8,0},{12,4},{1,9},{5,13},{9,1},{13,5},{2,10},{6,14},... | collective-permute-start | bytes 196616 | tf_op jit(solution)/shard_map/ppermute | solution.py:19
  53.0 3.4 %collective-permute-start.11 = (bf16[64,512]{1,0:T(8,128)(2,1)S(1)}, bf16[64,512]{1,0:T(8,128)(2,1)S(1)}, u32[]{:S(2)}, u32[]{:S(2)}) collective-permute-start(bf16[64,512]{1,0:T(8,128)(2,1)S(1)} %shard_map.84.refs_7_), channel_id=1, source_target_pairs={{0,12},{4,0},{8,4},{12,8},{1,13},{5,1},{9,5},{13,9},{2,14},{6,2},{... | collective-permute-start | bytes 196616 | tf_op jit(solution)/shard_map/ppermute | solution.py:19
  56.3 3.8 %shard_map.85 = (bf16[1024,1024]{1,0:T(8,128)(2,1)S(1)}, f32[1024,256]{1,0:T(8,128)S(1)}) custom-call(bf16[128,1152]{1,0:T(8,128)(2,1)S(1)} %get-tuple-element.11.own.refs_0_, bf16[128,1152]{1,0:T(8,128)(2,1)S(1)} %collective-permute-done.6.core.refs_1_, bf16[128,1152]{1,0:T(8,128)(2,1)S(1)} %collective-permute-done.7.far.refs_2_, ...), custom_call_target="tpu_custom_call" | custom-call | flops 3019898880 | bytes 2359296 | tf_op jit(solution)/shard_map/pallas_call | solution.py:28
  60.1 2.6 %collective-permute-done.11.refs_10_ = bf16[64,512]{1,0:T(8,128)(2,1)S(1)} collective-permute-done((bf16[64,512]{1,0:T(8,128)(2,1)S(1)}, bf16[64,512]{1,0:T(8,128)(2,1)S(1)}, u32[]{:S(2)}, u32[]{:S(2)}) %collective-permute-start.11) | collective-permute-done | bytes 65568 | tf_op jit(solution)/shard_map/ppermute | solution.py:19
  62.8 1.7 %shard_map.87 = f32[128,1024]{1,0:T(8,128)S(1)} custom-call(bf16[528,256]{1,0:T(8,128)(2,1)S(1)} %shard_map.82.refs_0_, bf16[528,256]{1,0:T(8,128)(2,1)S(1)} %collective-permute-done.refs_1_, bf16[528,256]{1,0:T(8,128)(2,1)S(1)} %collective-permute-done.1.refs_2_, bf16[528,256]{1,0:T(8,128)(2,1)S(1)} %collective-permute-done.2.refs_3_, ...), custom_call_target="tpu_custom_call" | custom-call | flops 1073741824 | bytes 4194304 | tf_op jit(solution)/shard_map/pallas_call | solution.py:28
  64.6 1.7 %shard_map.86 = f32[128,1024]{1,0:T(8,128)S(1)} custom-call(bf16[528,256]{1,0:T(8,128)(2,1)S(1)} %shard_map.82.refs_0_, bf16[528,256]{1,0:T(8,128)(2,1)S(1)} %collective-permute-done.refs_1_, bf16[528,256]{1,0:T(8,128)(2,1)S(1)} %collective-permute-done.1.refs_2_, bf16[528,256]{1,0:T(8,128)(2,1)S(1)} %collective-permute-done.2.refs_3_, ...), custom_call_target="tpu_custom_call" | custom-call | flops 1073741824 | bytes 4194304 | tf_op jit(solution)/shard_map/pallas_call | solution.py:28
  67.0 5.3 %collective-permute-done.25 = bf16[64,1024]{1,0:T(8,128)(2,1)S(1)} collective-permute-done((bf16[64,1024]{1,0:T(8,128)(2,1)S(1)}, bf16[64,1024]{1,0:T(8,128)(2,1)S(1)}, u32[]{:S(2)}, u32[]{:S(2)}) %collective-permute-start.25) | collective-permute-done | bytes 131104 | tf_op jit(solution)/shard_map/ppermute | solution.py:24
  72.4 1.3 %collective-permute-start.26 = (bf16[64,256]{1,0:T(8,128)(2,1)S(1)}, bf16[64,256]{1,0:T(8,128)(2,1)S(1)}, u32[]{:S(2)}, u32[]{:S(2)}) collective-permute-start(bf16[64,256]{1,0:T(8,128)(2,1)S(1)} %get-tuple-element.21), channel_id=1, source_target_pairs={{0,12},{4,0},{8,4},{12,8},{1,13},{5,1},{9,5},{13,9},{2,14},{6,2},{... | collective-permute-start | bytes 98312 | tf_op jit(solution)/shard_map/ppermute | solution.py:19
  74.5 1.9 %collective-permute-done.26.first = bf16[64,256]{1,0:T(8,128)(2,1)S(1)} collective-permute-done((bf16[64,256]{1,0:T(8,128)(2,1)S(1)}, bf16[64,256]{1,0:T(8,128)(2,1)S(1)}, u32[]{:S(2)}, u32[]{:S(2)}) %collective-permute-start.26) | collective-permute-done | bytes 32800 | tf_op jit(solution)/shard_map/ppermute | solution.py:19
  76.4 2.1 %collective-permute-done.27.second = bf16[64,256]{1,0:T(8,128)(2,1)S(1)} collective-permute-done((bf16[64,256]{1,0:T(8,128)(2,1)S(1)}, bf16[64,256]{1,0:T(8,128)(2,1)S(1)}, u32[]{:S(2)}, u32[]{:S(2)}) %collective-permute-start.27) | collective-permute-done | bytes 32800 | tf_op jit(solution)/shard_map/ppermute | solution.py:19
  78.5 0.9 %collective-permute-done.28.third = bf16[64,256]{1,0:T(8,128)(2,1)S(1)} collective-permute-done((bf16[64,256]{1,0:T(8,128)(2,1)S(1)}, bf16[64,256]{1,0:T(8,128)(2,1)S(1)}, u32[]{:S(2)}, u32[]{:S(2)}) %collective-permute-start.28) | collective-permute-done | bytes 32800 | tf_op jit(solution)/shard_map/ppermute | solution.py:19
  79.4 1.2 %shard_map.88 = bf16[64,256]{1,0:T(8,128)(2,1)} custom-call(s32[4,4]{1,0:T(4,128)S(1)} %copy-done.6, f32[64,256]{1,0:T(8,128)S(1)} %slice.39.mine, bf16[64,256]{1,0:T(8,128)(2,1)S(1)} %collective-permute-done.26.first, bf16[64,256]{1,0:T(8,128)(2,1)S(1)} %collective-permute-done.27.second, bf16[64,256]{1,0:T(8,128)(2,1)S(1)} %collective-permute-done.28.third), custom_call_target="tpu_custom_call" | custom-call | flops 65536 | bytes 196608 | tf_op jit(solution)/shard_map/pallas_call | solution.py:28
  (55 shorter events, 7.3 us)
Async XLA Ops:
  2.3 12.0 %collective-permute-start.12 = (bf16[80,1152]{1,0:T(8,128)(2,1)S(1)}, bf16[80,1152]{1,0:T(8,128)(2,1)S(1)}, u32[]{:S(2)}, u32[]{:S(2)}) collective-permute-start(bf16[80,1152]{1,0:T(8,128)(2,1)S(1)} %get-tuple-element.12), channel_id=1, source_target_pairs={{0,4},{4,8},{8,12},{12,0},{1,5},{5,9},{9,13},{13,1},{2,6},{6,10},{... | collective-permute-start | bytes 552968 | tf_op jit(solution)/shard_map/ppermute | solution.py:19
  5.4 14.7 %collective-permute-start.16 = (bf16[80,1152]{1,0:T(8,128)(2,1)S(1)}, bf16[80,1152]{1,0:T(8,128)(2,1)S(1)}, u32[]{:S(2)}, u32[]{:S(2)}) collective-permute-start(bf16[80,1152]{1,0:T(8,128)(2,1)S(1)} %get-tuple-element.13), channel_id=1, source_target_pairs={{0,8},{4,12},{8,0},{12,4},{1,9},{5,13},{9,1},{13,5},{2,10},{6,14},... | collective-permute-start | bytes 552968 | tf_op jit(solution)/shard_map/ppermute | solution.py:19
  10.6 14.8 %collective-permute-start = (bf16[528,256]{1,0:T(8,128)(2,1)S(1)}, bf16[528,256]{1,0:T(8,128)(2,1)S(1)}, u32[]{:S(2)}, u32[]{:S(2)}) collective-permute-start(bf16[528,256]{1,0:T(8,128)(2,1)S(1)} %shard_map.82.refs_0_), channel_id=1, source_target_pairs={{0,4},{4,8},{8,12},{1,5},{5,9},{9,13},{2,6},{6,10},{10,14},{3,7},{... | collective-permute-start | bytes 811016 | tf_op jit(solution)/shard_map/ppermute | solution.py:298
  12.6 13.3 %collective-permute-start.7 = (bf16[128,1152]{1,0:T(8,128)(2,1)S(1)}, bf16[128,1152]{1,0:T(8,128)(2,1)S(1)}, u32[]{:S(2)}, u32[]{:S(2)}) collective-permute-start(bf16[128,1152]{1,0:T(8,128)(2,1)S(1)} %get-tuple-element.11.own.refs_0_), channel_id=1, source_target_pairs={{0,2},{1,3},{2,0},{3,1},{4,6},{5,7},{6,4},{7,5},{8,10},{9,11},{10,... | collective-permute-start | bytes 884744 | tf_op jit(solution)/shard_map/ppermute | solution.py:24
  14.3 17.5 %collective-permute-start.6 = (bf16[128,1152]{1,0:T(8,128)(2,1)S(1)}, bf16[128,1152]{1,0:T(8,128)(2,1)S(1)}, u32[]{:S(2)}, u32[]{:S(2)}) collective-permute-start(bf16[128,1152]{1,0:T(8,128)(2,1)S(1)} %get-tuple-element.11.own.refs_0_), channel_id=1, source_target_pairs={{0,1},{1,0},{2,3},{3,2},{4,5},{5,4},{6,7},{7,6},{8,9},{9,8},{10,11... | collective-permute-start | bytes 884744 | tf_op jit(solution)/shard_map/ppermute | solution.py:24
  14.3 9.6 %collective-permute-start.20 = (bf16[80,1152]{1,0:T(8,128)(2,1)S(1)}, bf16[80,1152]{1,0:T(8,128)(2,1)S(1)}, u32[]{:S(2)}, u32[]{:S(2)}) collective-permute-start(bf16[80,1152]{1,0:T(8,128)(2,1)S(1)} %get-tuple-element.14), channel_id=1, source_target_pairs={{0,12},{4,0},{8,4},{12,8},{1,13},{5,1},{9,5},{13,9},{2,14},{6,2},{... | collective-permute-start | bytes 552968 | tf_op jit(solution)/shard_map/ppermute | solution.py:19
  20.1 10.2 %collective-permute-start.3 = (bf16[528,256]{1,0:T(8,128)(2,1)S(1)}, bf16[528,256]{1,0:T(8,128)(2,1)S(1)}, u32[]{:S(2)}, u32[]{:S(2)}) collective-permute-start(bf16[528,256]{1,0:T(8,128)(2,1)S(1)} %shard_map.82.refs_0_), channel_id=1, source_target_pairs={{12,8},{8,4},{4,0},{13,9},{9,5},{5,1},{14,10},{10,6},{6,2},{15,11}... | collective-permute-start | bytes 811016 | tf_op jit(solution)/shard_map/ppermute | solution.py:299
  24.0 7.9 %collective-permute-start.14 = (bf16[80,1152]{1,0:T(8,128)(2,1)S(1)}, bf16[80,1152]{1,0:T(8,128)(2,1)S(1)}, u32[]{:S(2)}, u32[]{:S(2)}) collective-permute-start(bf16[80,1152]{1,0:T(8,128)(2,1)S(1)} %collective-permute-done.12.refs_4_), channel_id=1, source_target_pairs={{0,2},{1,3},{2,0},{3,1},{4,6},{5,7},{6,4},{7,5},{8,10},{9,11},{10,... | collective-permute-start | bytes 552968 | tf_op jit(solution)/shard_map/ppermute | solution.py:24
  25.4 10.0 %collective-permute-start.18 = (bf16[80,1152]{1,0:T(8,128)(2,1)S(1)}, bf16[80,1152]{1,0:T(8,128)(2,1)S(1)}, u32[]{:S(2)}, u32[]{:S(2)}) collective-permute-start(bf16[80,1152]{1,0:T(8,128)(2,1)S(1)} %collective-permute-done.16.refs_8_), channel_id=1, source_target_pairs={{0,2},{1,3},{2,0},{3,1},{4,6},{5,7},{6,4},{7,5},{8,10},{9,11},{10,... | collective-permute-start | bytes 552968 | tf_op jit(solution)/shard_map/ppermute | solution.py:24
  26.0 15.1 %collective-permute-start.8 = (bf16[128,1152]{1,0:T(8,128)(2,1)S(1)}, bf16[128,1152]{1,0:T(8,128)(2,1)S(1)}, u32[]{:S(2)}, u32[]{:S(2)}) collective-permute-start(bf16[128,1152]{1,0:T(8,128)(2,1)S(1)} %collective-permute-done.7.far.refs_2_), channel_id=1, source_target_pairs={{0,1},{1,0},{2,3},{3,2},{4,5},{5,4},{6,7},{7,6},{8,9},{9,8},{10,11... | collective-permute-start | bytes 884744 | tf_op jit(solution)/shard_map/ppermute | solution.py:24
  30.3 8.1 %collective-permute-start.22 = (bf16[80,1152]{1,0:T(8,128)(2,1)S(1)}, bf16[80,1152]{1,0:T(8,128)(2,1)S(1)}, u32[]{:S(2)}, u32[]{:S(2)}) collective-permute-start(bf16[80,1152]{1,0:T(8,128)(2,1)S(1)} %collective-permute-done.20.refs_12_), channel_id=1, source_target_pairs={{0,2},{1,3},{2,0},{3,1},{4,6},{5,7},{6,4},{7,5},{8,10},{9,11},{10,... | collective-permute-start | bytes 552968 | tf_op jit(solution)/shard_map/ppermute | solution.py:24
  31.8 7.3 %collective-permute-start.13 = (bf16[80,1152]{1,0:T(8,128)(2,1)S(1)}, bf16[80,1152]{1,0:T(8,128)(2,1)S(1)}, u32[]{:S(2)}, u32[]{:S(2)}) collective-permute-start(bf16[80,1152]{1,0:T(8,128)(2,1)S(1)} %collective-permute-done.12.refs_4_), channel_id=1, source_target_pairs={{0,1},{1,0},{2,3},{3,2},{4,5},{5,4},{6,7},{7,6},{8,9},{9,8},{10,11... | collective-permute-start | bytes 552968 | tf_op jit(solution)/shard_map/ppermute | solution.py:24
  31.8 8.6 %collective-permute-start.17 = (bf16[80,1152]{1,0:T(8,128)(2,1)S(1)}, bf16[80,1152]{1,0:T(8,128)(2,1)S(1)}, u32[]{:S(2)}, u32[]{:S(2)}) collective-permute-start(bf16[80,1152]{1,0:T(8,128)(2,1)S(1)} %collective-permute-done.16.refs_8_), channel_id=1, source_target_pairs={{0,1},{1,0},{2,3},{3,2},{4,5},{5,4},{6,7},{7,6},{8,9},{9,8},{10,11... | collective-permute-start | bytes 552968 | tf_op jit(solution)/shard_map/ppermute | solution.py:24
  35.4 5.1 %collective-permute-start.21 = (bf16[80,1152]{1,0:T(8,128)(2,1)S(1)}, bf16[80,1152]{1,0:T(8,128)(2,1)S(1)}, u32[]{:S(2)}, u32[]{:S(2)}) collective-permute-start(bf16[80,1152]{1,0:T(8,128)(2,1)S(1)} %collective-permute-done.20.refs_12_), channel_id=1, source_target_pairs={{0,1},{1,0},{2,3},{3,2},{4,5},{5,4},{6,7},{7,6},{8,9},{9,8},{10,11... | collective-permute-start | bytes 552968 | tf_op jit(solution)/shard_map/ppermute | solution.py:24
  38.5 6.0 %collective-permute-start.1 = (bf16[528,256]{1,0:T(8,128)(2,1)S(1)}, bf16[528,256]{1,0:T(8,128)(2,1)S(1)}, u32[]{:S(2)}, u32[]{:S(2)}) collective-permute-start(bf16[528,256]{1,0:T(8,128)(2,1)S(1)} %collective-permute-done.refs_1_), channel_id=1, source_target_pairs={{4,8},{8,12},{5,9},{9,13},{6,10},{10,14},{7,11},{11,15},{20,24},{2... | collective-permute-start | bytes 811016 | tf_op jit(solution)/shard_map/ppermute | solution.py:298
  39.2 10.8 %collective-permute-start.4 = (bf16[528,256]{1,0:T(8,128)(2,1)S(1)}, bf16[528,256]{1,0:T(8,128)(2,1)S(1)}, u32[]{:S(2)}, u32[]{:S(2)}) collective-permute-start(bf16[528,256]{1,0:T(8,128)(2,1)S(1)} %collective-permute-done.3.refs_4_), channel_id=1, source_target_pairs={{8,4},{4,0},{9,5},{5,1},{10,6},{6,2},{11,7},{7,3},{24,20},{20,16},... | collective-permute-start | bytes 811016 | tf_op jit(solution)/shard_map/ppermute | solution.py:299
  40.5 10.8 %collective-permute-start.15 = (bf16[80,1152]{1,0:T(8,128)(2,1)S(1)}, bf16[80,1152]{1,0:T(8,128)(2,1)S(1)}, u32[]{:S(2)}, u32[]{:S(2)}) collective-permute-start(bf16[80,1152]{1,0:T(8,128)(2,1)S(1)} %collective-permute-done.14.refs_6_), channel_id=1, source_target_pairs={{0,1},{1,0},{2,3},{3,2},{4,5},{5,4},{6,7},{7,6},{8,9},{9,8},{10,11... | collective-permute-start | bytes 552968 | tf_op jit(solution)/shard_map/ppermute | solution.py:24
  40.6 12.4 %collective-permute-start.19 = (bf16[80,1152]{1,0:T(8,128)(2,1)S(1)}, bf16[80,1152]{1,0:T(8,128)(2,1)S(1)}, u32[]{:S(2)}, u32[]{:S(2)}) collective-permute-start(bf16[80,1152]{1,0:T(8,128)(2,1)S(1)} %collective-permute-done.18.refs_10_), channel_id=1, source_target_pairs={{0,1},{1,0},{2,3},{3,2},{4,5},{5,4},{6,7},{7,6},{8,9},{9,8},{10,11... | collective-permute-start | bytes 552968 | tf_op jit(solution)/shard_map/ppermute | solution.py:24
  41.0 15.3 %collective-permute-start.23 = (bf16[80,1152]{1,0:T(8,128)(2,1)S(1)}, bf16[80,1152]{1,0:T(8,128)(2,1)S(1)}, u32[]{:S(2)}, u32[]{:S(2)}) collective-permute-start(bf16[80,1152]{1,0:T(8,128)(2,1)S(1)} %collective-permute-done.22.refs_14_), channel_id=1, source_target_pairs={{0,1},{1,0},{2,3},{3,2},{4,5},{5,4},{6,7},{7,6},{8,9},{9,8},{10,11... | collective-permute-start | bytes 552968 | tf_op jit(solution)/shard_map/ppermute | solution.py:24
  43.5 12.9 %copy-start.8 = (bf16[8,1152,128]{2,1,0:T(8,128)(2,1)S(1)}, bf16[8,1152,128]{2,1,0:T(8,128)(2,1)}, u32[]{:S(2)}) copy-start(bf16[8,1152,128]{2,1,0:T(8,128)(2,1)} %refs_16_.1) | copy-start | bytes 7077892
  44.4 18.3 %copy-start.5 = (s32[256]{0:T(256)S(1)}, s32[256]{0:T(256)}, u32[]{:S(2)}) copy-start(s32[256]{0:T(256)} %param.11) | copy-start | bytes 3076
  44.4 18.3 %collective-permute-start.2 = (bf16[528,256]{1,0:T(8,128)(2,1)S(1)}, bf16[528,256]{1,0:T(8,128)(2,1)S(1)}, u32[]{:S(2)}, u32[]{:S(2)}) collective-permute-start(bf16[528,256]{1,0:T(8,128)(2,1)S(1)} %collective-permute-done.1.refs_2_), channel_id=1, source_target_pairs={{8,12},{9,13},{10,14},{11,15},{24,28},{25,29},{26,30},{27,31}} | collective-permute-start | bytes 811016 | tf_op jit(solution)/shard_map/ppermute | solution.py:298
  49.9 12.8 %collective-permute-start.5 = (bf16[528,256]{1,0:T(8,128)(2,1)S(1)}, bf16[528,256]{1,0:T(8,128)(2,1)S(1)}, u32[]{:S(2)}, u32[]{:S(2)}) collective-permute-start(bf16[528,256]{1,0:T(8,128)(2,1)S(1)} %collective-permute-done.4.refs_5_), channel_id=1, source_target_pairs={{4,0},{5,1},{6,2},{7,3},{20,16},{21,17},{22,18},{23,19}} | collective-permute-start | bytes 811016 | tf_op jit(solution)/shard_map/ppermute | solution.py:299
  51.2 8.9 %collective-permute-start.10 = (bf16[64,512]{1,0:T(8,128)(2,1)S(1)}, bf16[64,512]{1,0:T(8,128)(2,1)S(1)}, u32[]{:S(2)}, u32[]{:S(2)}) collective-permute-start(bf16[64,512]{1,0:T(8,128)(2,1)S(1)} %shard_map.84.refs_7_), channel_id=1, source_target_pairs={{0,8},{4,12},{8,0},{12,4},{1,9},{5,13},{9,1},{13,5},{2,10},{6,14},... | collective-permute-start | bytes 196616 | tf_op jit(solution)/shard_map/ppermute | solution.py:19
  53.0 9.8 %collective-permute-start.11 = (bf16[64,512]{1,0:T(8,128)(2,1)S(1)}, bf16[64,512]{1,0:T(8,128)(2,1)S(1)}, u32[]{:S(2)}, u32[]{:S(2)}) collective-permute-start(bf16[64,512]{1,0:T(8,128)(2,1)S(1)} %shard_map.84.refs_7_), channel_id=1, source_target_pairs={{0,12},{4,0},{8,4},{12,8},{1,13},{5,1},{9,5},{13,9},{2,14},{6,2},{... | collective-permute-start | bytes 196616 | tf_op jit(solution)/shard_map/ppermute | solution.py:19
  56.3 6.4 %collective-permute-start.9 = (bf16[64,512]{1,0:T(8,128)(2,1)S(1)}, bf16[64,512]{1,0:T(8,128)(2,1)S(1)}, u32[]{:S(2)}, u32[]{:S(2)}) collective-permute-start(bf16[64,512]{1,0:T(8,128)(2,1)S(1)} %shard_map.84.refs_7_), channel_id=1, source_target_pairs={{0,4},{4,8},{8,12},{12,0},{1,5},{5,9},{9,13},{13,1},{2,6},{6,10},{... | collective-permute-start | bytes 196616 | tf_op jit(solution)/shard_map/ppermute | solution.py:19
  64.5 14.9 %copy-start.6 = (s32[4,4]{1,0:T(4,128)S(1)}, s32[4,4]{1,0:T(4,128)}, u32[]{:S(2)}) copy-start(s32[4,4]{1,0:T(4,128)} %pattern.1) | copy-start | bytes 196
  64.5 2.0 %collective-permute-start.24 = (f32[128,1024]{1,0:T(8,128)S(1)}, f32[128,1024]{1,0:T(8,128)S(1)}, u32[]{:S(2)}, u32[]{:S(2)}) collective-permute-start(f32[128,1024]{1,0:T(8,128)S(1)} %shard_map.87), channel_id=1, source_target_pairs={{0,1},{1,0},{2,3},{3,2},{4,5},{5,4},{6,7},{7,6},{8,9},{9,8},{10,11... | collective-permute-start | bytes 1572872 | tf_op jit(solution)/shard_map/ppermute | solution.py:24
  66.5 5.8 %collective-permute-start.25 = (bf16[64,1024]{1,0:T(8,128)(2,1)S(1)}, bf16[64,1024]{1,0:T(8,128)(2,1)S(1)}, u32[]{:S(2)}, u32[]{:S(2)}) collective-permute-start(bf16[64,1024]{1,0:T(8,128)(2,1)S(1)} %fusion), channel_id=1, source_target_pairs={{0,2},{1,3},{2,0},{3,1},{4,6},{5,7},{6,4},{7,5},{8,10},{9,11},{10,... | collective-permute-start | bytes 393224 | tf_op jit(solution)/shard_map/ppermute | solution.py:24
  72.4 4.0 %collective-permute-start.26 = (bf16[64,256]{1,0:T(8,128)(2,1)S(1)}, bf16[64,256]{1,0:T(8,128)(2,1)S(1)}, u32[]{:S(2)}, u32[]{:S(2)}) collective-permute-start(bf16[64,256]{1,0:T(8,128)(2,1)S(1)} %get-tuple-element.21), channel_id=1, source_target_pairs={{0,12},{4,0},{8,4},{12,8},{1,13},{5,1},{9,5},{13,9},{2,14},{6,2},{... | collective-permute-start | bytes 98312 | tf_op jit(solution)/shard_map/ppermute | solution.py:19
  73.6 4.8 %collective-permute-start.27 = (bf16[64,256]{1,0:T(8,128)(2,1)S(1)}, bf16[64,256]{1,0:T(8,128)(2,1)S(1)}, u32[]{:S(2)}, u32[]{:S(2)}) collective-permute-start(bf16[64,256]{1,0:T(8,128)(2,1)S(1)} %get-tuple-element.20), channel_id=1, source_target_pairs={{0,8},{4,12},{8,0},{12,4},{1,9},{5,13},{9,1},{13,5},{2,10},{6,14},... | collective-permute-start | bytes 98312 | tf_op jit(solution)/shard_map/ppermute | solution.py:19
  73.6 5.7 %collective-permute-start.28 = (bf16[64,256]{1,0:T(8,128)(2,1)S(1)}, bf16[64,256]{1,0:T(8,128)(2,1)S(1)}, u32[]{:S(2)}, u32[]{:S(2)}) collective-permute-start(bf16[64,256]{1,0:T(8,128)(2,1)S(1)} %get-tuple-element.19), channel_id=1, source_target_pairs={{0,4},{4,8},{8,12},{12,0},{1,5},{5,9},{9,13},{13,1},{2,6},{6,10},{... | collective-permute-start | bytes 98312 | tf_op jit(solution)/shard_map/ppermute | solution.py:19
  (6 other events, 6.6 us)
where the time goes:
time: 80.9 us; the launch traced here: 80.6 us
  waiting for transfers between devices  36.1 us (45%)
  starting transfers between devices  27.5 us (34%)
  Pallas kernels  10 us (12%)
  local copies, waits for them, and re-layouts  6.65 us (8%)
    ppermute x9, waiting for transfers between devices, passed_along(): return lax.ppermute(value, axis, pairs)  15.3 us
    ppermute x9, starting transfers between devices, passed_along(): return lax.ppermute(value, axis, pairs)  13.4 us
    ppermute x14, waiting for transfers between devices, swapped(): return lax.ppermute(value, axis, pairs)  11.6 us
    pallas_call x7, Pallas kernels, kernel_call(): pl.pallas_call(body, out_shape=outs, in_specs=[pl.BlockSpec(memory_space=...  10 us
    ppermute x3, waiting for transfers between devices, resident(): leftward.append(lax.ppermute(leftward[-1], 'tgt', down))  9.16 us
    ppermute x14, starting transfers between devices, swapped(): return lax.ppermute(value, axis, pairs)  6.92 us
    unnamed x18, local copies, waits for them, and re-layouts  6.63 us
    ppermute x3, starting transfers between devices, resident(): leftward.append(lax.ppermute(leftward[-1], 'tgt', down))  3.85 us
  transfers between devices with their start and end apart: 29, of which 12 were waited for; matrix products, arithmetic and copies ran while one was open for 0% of the time, Pallas kernels for 8%

commit v1 on v0

--- a/solution.py
+++ b/solution.py
@@ -38,7 +38,12 @@
         scratch_shapes=scratch,
         compiler_params=pltpu.CompilerParams(vmem_limit_bytes=VMEM_BYTES),
         cost_estimate=pl.CostEstimate(flops=flops, bytes_accessed=moved, transcendentals=0),
-    )(*args)
+    )(
+        *[
+            pltpu.with_memory_space_constraint(arg, pltpu.HBM) if i in hbm else arg
+            for i, arg in enumerate(args)
+        ]
+    )
 
 
 def aligned(start, size):
@@ -58,62 +63,74 @@
     return (b % 2) * (2 * block) + (b // 2) * block
 
 
-def cut_kernel(targets, sources, own, first, second, third, done):
+def by_core(positions):
+    quarter = positions.shape[1] // 4
+    return jnp.concatenate(
+        [positions[:, b * quarter : (b + 1) * quarter] for b in (0, 2, 1, 3)], axis=1
+    )
+
+
+def front_kernel(targets, sources, attn, spos, tpos, own, first, second, third, table, held, spots, done):
     z = lax.axis_index("tgt")
     rows, sub = targets.shape[0], sources.shape[0]
     part = own.shape[1]
+    heads, queries, keys = attn.shape
+    base = heads * queries
 
     def columns(index):
         return pl.ds(pl.multiple_of(index * part, 128), part)
 
-    moves = [(targets.at[:, columns(z)], own.at[pl.ds(0, rows)])]
+    moves = [(attn, held), (spos, spots.at[0]), (tpos, spots.at[1])]
     for k, out in enumerate((first, second, third), 1):
         at = columns(jnp.where(z + k >= 4, z + k - 4, z + k))
         moves.append((targets.at[:, at], out.at[pl.ds(0, rows)]))
         moves.append((sources.at[:, at], out.at[pl.ds(rows, sub)]))
+    moves.append((targets.at[:, columns(z)], own.at[pl.ds(0, rows)]))
     for i in range(4):
         moves.append((sources.at[:, pl.ds(i * part, part)], own.at[pl.ds(rows + i * sub, sub)]))
     copies = [pltpu.make_async_copy(*ends, done.at[i]) for i, ends in enumerate(moves)]
     for copy in copies:
         copy.start()
-    for copy in copies:
+    for copy in copies[:3]:
         copy.wait()
-
-
-def by_core(positions):
-    quarter = positions.shape[1] // 4
-    return jnp.concatenate(
-        [positions[:, b * quarter : (b + 1) * quarter] for b in (0, 2, 1, 3)], axis=1
-    )
-
-
-def table_kernel(attn, spos, tpos, out):
-    heads, queries, keys = attn.shape
-    base = heads * queries
-    picks = lax.broadcasted_iota(jnp.int32, (keys, spos.shape[1]), 0) == by_core(spos[...])
+    picks = lax.broadcasted_iota(jnp.int32, (keys, spos.shape[1]), 0) == by_core(spots[0])
     picks = picks.astype(F32).astype(BF16)
-    table = attn[...].reshape(base, keys)
-    out[0:base, :] = jnp.dot(table, picks, preferred_element_type=F32).astype(BF16)
-    out[base:, :] = jnp.broadcast_to(
-        tpos[...].astype(F32), (out.shape[0] - base, tpos.shape[1])
+    table[0:base, :] = jnp.dot(
+        held[...].reshape(base, keys), picks, preferred_element_type=F32
     ).astype(BF16)
-
-
-def values_kernel(rows, own, core, far, cross, value, out):
+    table[base:, :] = jnp.broadcast_to(
+        spots[1].astype(F32), (table.shape[0] - base, tpos.shape[1])
+    ).astype(BF16)
+    for copy in copies[3:]:
+        copy.wait()
+
+
+def values_kernel(rows, own, core, far, cross, value, out, held, done):
     s = lax.axis_index("src")
     sub = (own.shape[0] - rows) // 4
     part = own.shape[1]
-    for pair in range(value.shape[0] // 2):
-        total = None
-        for i in range(4):
-            at = slice(rows + i * sub, rows + (i + 1) * sub)
-            left = jnp.concatenate([ref[at, :] for ref in (own, core, far, cross)], axis=0)
+    pairs = value.shape[0] // 2
+    copies = [
+        pltpu.make_async_copy(
+            value.at[:, pl.ds(i * part, part), :], held.at[:, pl.ds(i * part, part), :], done.at[i]
+        )
+        for i in range(4)
+    ]
+    for copy in copies:
+        copy.start()
+    totals = [None] * pairs
+    for i in range(4):
+        copies[i].wait()
+        at = slice(rows + i * sub, rows + (i + 1) * sub)
+        left = jnp.concatenate([ref[at, :] for ref in (own, core, far, cross)], axis=0)
+        for pair in range(pairs):
             got = jnp.dot(
                 left,
-                pair_of(value, 2 * pair, slice(i * part, (i + 1) * part)),
+                pair_of(held, 2 * pair, slice(i * part, (i + 1) * part)),
                 preferred_element_type=F32,
             )
-            total = got if total is None else total + got
+            totals[pair] = got if i == 0 else totals[pair] + got
+    for pair, total in enumerate(totals):
         width = total.shape[1]
         for j in range(4):
             out[aligned((s ^ j) * sub, sub), pair * width : (pair + 1) * width] = total[
@@ -161,7 +178,7 @@
 def edges_kernel(heads, queries, flip, *refs):
     home, right1, right2, right3, left1, left2, left3 = refs[:7]
     blocks_of_values = refs[7:11]
-    reads, direct, spos, out, table, values = refs[11:]
+    reads, direct, spos, pattern, out, table, values = refs[11:]
     z, s = lax.axis_index("tgt"), lax.axis_index("src")
     side = (s % 2) ^ flip
     sources = spos.shape[1]
@@ -238,15 +255,8 @@
         turned = (mixed + same * direct[here, lanes]).T
         for x in range(2):
             row = jnp.where(s // 2 == x, block, 0)
-            out[aligned(row, block), here] = turned[x * block : (x + 1) * block, :]
-
-
-def finish_kernel(pattern, mine, first, second, third, out):
-    kept = pattern[lax.axis_index("src"), lax.axis_index("tgt")].astype(F32)
-    total = mine[...]
-    for ref in (first, second, third):
-        total = total + ref[...].astype(F32)
-    out[...] = (total * kept).astype(BF16)
+            kept = pattern[2 * x + side, origin_of(z, k)].astype(F32)
+            out[aligned(row, block), here] = turned[x * block : (x + 1) * block, :] * kept
 
 
 def resident(
@@ -266,14 +276,21 @@
     def shape(*dims, dtype=BF16):
         return jax.ShapeDtypeStruct(dims, dtype)
 
+    spots = source_pos[None, :]
     cut = kernel_call(
-        cut_kernel,
-        (shape(rows + 4 * sub, part),) + (shape(rows + sub, part),) * 3,
-        [target_rows, decoder_rows],
-        0,
+        front_kernel,
+        (shape(rows + 4 * sub, part),)
+        + (shape(rows + sub, part),) * 3
+        + (shape(heads * queries + 16, sources),),
+        [target_rows, decoder_rows, attention, spots, target_pos[None, :]],
+        2 * attention.size * sources,
         target_rows.size * 4,
-        [pltpu.SemaphoreType.DMA((11,))],
-        hbm=(0, 1),
+        [
+            pltpu.VMEM(attention.shape, BF16),
+            pltpu.VMEM((2, 1, sources), jnp.int32),
+            pltpu.SemaphoreType.DMA((14,)),
+        ],
+        hbm=(0, 1, 2, 3, 4),
     )
     own, far, core, cross = [cut[0]], [], [], []
     for k in range(1, blocks):
@@ -283,14 +300,7 @@
         core.append(swapped(own[k], "src", 1))
         cross.append(swapped(far[k], "src", 1))
 
-    spots = source_pos[None, :]
-    home = kernel_call(
-        table_kernel,
-        shape(heads * queries + 16, sources),
-        [attention, spots, target_pos[None, :]],
-        2 * attention.size * sources,
-        attention.size * 4,
-    )
+    home = cut[4]
     rightward, leftward = [home], [home]
     for step in range(1, blocks):
         up = [(i, i + 1) for i in range(step - 1, blocks - 1)]
@@ -304,6 +314,8 @@
             [own[0], core[0], far[0], cross[0], value_proj],
             2 * block * depth * groups * head_dim,
             value_proj.size * 2,
+            [pltpu.VMEM(value_proj.shape, BF16), pltpu.SemaphoreType.DMA((4,))],
+            hbm=(4,),
         )
     ]
     for k in range(1, blocks):
@@ -325,10 +337,11 @@
         return kernel_call(
             functools.partial(edges_kernel, heads, queries, flip),
             shape(sources // 2, blocks * targets, dtype=F32),
-            [home, *rightward[1:], *leftward[1:], *values, reads, direct, spots],
+            [home, *rightward[1:], *leftward[1:], *values, reads, direct, spots, tile_pattern],
             2 * 2 * blocks * targets * sources * heads * head_dim,
             1 << 22,
             [pltpu.VMEM((4,) + home.shape, BF16), pltpu.VMEM((sources, groups * head_dim), BF16)],
+            smem=(14,),
         )
 
     away = swapped(edges(1), "src", 1)
@@ -337,14 +350,10 @@
     mine = kept[block:] + away[block:] + back.astype(F32)
     parts = [mine[:, k * targets : (k + 1) * targets] for k in range(blocks)]
     landed = [passed_along(parts[k].astype(BF16), "tgt", -k) for k in range(1, blocks)]
-    return kernel_call(
-        finish_kernel,
-        shape(block, targets),
-        [tile_pattern, parts[0], *landed],
-        4 * block * targets,
-        block * targets * 12,
-        smem=(0,),
-    )
+    result = parts[0]
+    for value in landed:
+        result = result + value.astype(F32)
+    return result.astype(BF16)
 
 
 def ring(

time: 80.9 us -> 80.4 us (level)
  local copies, waits for them, and re-layouts: 6.65 us -> 0.03 us
  Pallas kernels: 10 us -> 12.4 us
  starting transfers between devices: 27.5 us -> 29.1 us
  waiting for transfers between devices: 36.1 us -> 37.6 us
    unnamed x18 -> x6, local copies, waits for them, and re-layouts: 6.63 us -> 0.02 us
    ppermute x3, waiting for transfers between devices: 9.16 us -> 12.5 us  [resident(): leftward.append(lax.ppermute(leftward[-1], 'tgt', down))]
    pallas_call x7 -> x5, Pallas kernels: 10 us -> 12.4 us  [kernel_call(): pl.pallas_call(body, out_shape=outs, in_specs=[pl.BlockSpec(memory_space=...]
    ppermute x14, waiting for transfers between devices: 11.6 us -> 9.74 us  [swapped(): return lax.ppermute(value, axis, pairs)]
    ppermute x9, starting transfers between devices: 13.4 us -> 15 us  [passed_along(): return lax.ppermute(value, axis, pairs)]
  transfers between devices with their start and end apart: 29 -> 29, of which waited for: 12 -> 12; matrix products, arithmetic and copies ran while one was open for 0% -> 0% of each run, Pallas kernels for 8% -> 11%
where the time goes in v1:
time: 80.4 us; the launch traced here: 80.2 us
  waiting for transfers between devices  37.6 us (47%)
  starting transfers between devices  29.1 us (36%)
  Pallas kernels  12.4 us (15%)
    ppermute x9, waiting for transfers between devices, passed_along(): return lax.ppermute(value, axis, pairs)  15.4 us
    ppermute x9, starting transfers between devices, passed_along(): return lax.ppermute(value, axis, pairs)  15 us
    ppermute x3, waiting for transfers between devices, resident(): leftward.append(lax.ppermute(leftward[-1], 'tgt', down))  12.5 us
    pallas_call x5, Pallas kernels, kernel_call(): pl.pallas_call(body, out_shape=outs, in_specs=[pl.BlockSpec(memory_space=...  12.4 us
    ppermute x14, waiting for transfers between devices, swapped(): return lax.ppermute(value, axis, pairs)  9.74 us
    ppermute x14, starting transfers between devices, swapped(): return lax.ppermute(value, axis, pairs)  6.92 us
    ppermute x3, starting transfers between devices, resident(): leftward.append(lax.ppermute(leftward[-1], 'tgt', down))  3.85 us
    ppermute x3, starting transfers between devices, resident(): rightward.append(lax.ppermute(rightward[-1], 'tgt', up))  3.33 us
  transfers between devices with their start and end apart: 29, of which 12 were waited for; matrix products, arithmetic and copies ran while one was open for 0% of the time, Pallas kernels for 11%

profile of v1, /device:TPU:0, one launch (start us, length us, event | category | flops | bytes accessed | tf_op | source)
XLA Modules:
  0.0 80.2 jit_solution(10276332260146640368)
XLA Ops:
  0.0 1.4 %shard_map.82 = (bf16[128,1152]{1,0:T(8,128)(2,1)S(1)}, bf16[80,1152]{1,0:T(8,128)(2,1)S(1)}, bf16[80,1152]{1,0:T(8,128)(2,1)S(1)}, bf16[80,1152]{1,0:T(8,128)(2,1)S(1)}, bf16[528,256]{1,0:T(8,128)(2,1)S(1)}) custom-call(bf16[64,4608]{1,0:T(8,128)(2,1)} %targets.1, bf16[16,4608]{1,0:T(8,128)(2,1)} %sources.1, bf16[8,64,256]{2,1,0:T(8,128)(2,1)} %attn.1, ...), custom_call_target="tpu_custom_call" | custom-call | flops 67108864 | bytes 1179648 | tf_op jit(solution)/shard_map/pallas_call | solution.py:28
  1.4 3.1 %collective-permute-start.12 = (bf16[80,1152]{1,0:T(8,128)(2,1)S(1)}, bf16[80,1152]{1,0:T(8,128)(2,1)S(1)}, u32[]{:S(2)}, u32[]{:S(2)}) collective-permute-start(bf16[80,1152]{1,0:T(8,128)(2,1)S(1)} %get-tuple-element.14), channel_id=1, source_target_pairs={{0,4},{4,8},{8,12},{12,0},{1,5},{5,9},{9,13},{13,1},{2,6},{6,10},{... | collective-permute-start | bytes 552968 | tf_op jit(solution)/shard_map/ppermute | solution.py:19
  4.5 2.6 %collective-permute-start.16 = (bf16[80,1152]{1,0:T(8,128)(2,1)S(1)}, bf16[80,1152]{1,0:T(8,128)(2,1)S(1)}, u32[]{:S(2)}, u32[]{:S(2)}) collective-permute-start(bf16[80,1152]{1,0:T(8,128)(2,1)S(1)} %get-tuple-element.15), channel_id=1, source_target_pairs={{0,8},{4,12},{8,0},{12,4},{1,9},{5,13},{9,1},{13,5},{2,10},{6,14},... | collective-permute-start | bytes 552968 | tf_op jit(solution)/shard_map/ppermute | solution.py:19
  7.1 2.0 %collective-permute-start = (bf16[528,256]{1,0:T(8,128)(2,1)S(1)}, bf16[528,256]{1,0:T(8,128)(2,1)S(1)}, u32[]{:S(2)}, u32[]{:S(2)}) collective-permute-start(bf16[528,256]{1,0:T(8,128)(2,1)S(1)} %get-tuple-element.12.refs_0_), channel_id=1, source_target_pairs={{0,4},{4,8},{8,12},{1,5},{5,9},{9,13},{2,6},{6,10},{10,14},{3,7},{... | collective-permute-start | bytes 811016 | tf_op jit(solution)/shard_map/ppermute | solution.py:308
  9.1 1.7 %collective-permute-start.7 = (bf16[128,1152]{1,0:T(8,128)(2,1)S(1)}, bf16[128,1152]{1,0:T(8,128)(2,1)S(1)}, u32[]{:S(2)}, u32[]{:S(2)}) collective-permute-start(bf16[128,1152]{1,0:T(8,128)(2,1)S(1)} %get-tuple-element.13.own.refs_0_), channel_id=1, source_target_pairs={{0,2},{1,3},{2,0},{3,1},{4,6},{5,7},{6,4},{7,5},{8,10},{9,11},{10,... | collective-permute-start | bytes 884744 | tf_op jit(solution)/shard_map/ppermute | solution.py:24
  10.8 1.3 %collective-permute-done.12.refs_4_ = bf16[80,1152]{1,0:T(8,128)(2,1)S(1)} collective-permute-done((bf16[80,1152]{1,0:T(8,128)(2,1)S(1)}, bf16[80,1152]{1,0:T(8,128)(2,1)S(1)}, u32[]{:S(2)}, u32[]{:S(2)}) %collective-permute-start.12) | collective-permute-done | bytes 184352 | tf_op jit(solution)/shard_map/ppermute | solution.py:19
  12.1 2.2 %collective-permute-start.20 = (bf16[80,1152]{1,0:T(8,128)(2,1)S(1)}, bf16[80,1152]{1,0:T(8,128)(2,1)S(1)}, u32[]{:S(2)}, u32[]{:S(2)}) collective-permute-start(bf16[80,1152]{1,0:T(8,128)(2,1)S(1)} %get-tuple-element.16), channel_id=1, source_target_pairs={{0,12},{4,0},{8,4},{12,8},{1,13},{5,1},{9,5},{13,9},{2,14},{6,2},{... | collective-permute-start | bytes 552968 | tf_op jit(solution)/shard_map/ppermute | solution.py:19
  14.3 4.9 %collective-permute-done.16.refs_8_ = bf16[80,1152]{1,0:T(8,128)(2,1)S(1)} collective-permute-done((bf16[80,1152]{1,0:T(8,128)(2,1)S(1)}, bf16[80,1152]{1,0:T(8,128)(2,1)S(1)}, u32[]{:S(2)}, u32[]{:S(2)}) %collective-permute-start.16) | collective-permute-done | bytes 184352 | tf_op jit(solution)/shard_map/ppermute | solution.py:19
  19.2 1.3 %collective-permute-start.3 = (bf16[528,256]{1,0:T(8,128)(2,1)S(1)}, bf16[528,256]{1,0:T(8,128)(2,1)S(1)}, u32[]{:S(2)}, u32[]{:S(2)}) collective-permute-start(bf16[528,256]{1,0:T(8,128)(2,1)S(1)} %get-tuple-element.12.refs_0_), channel_id=1, source_target_pairs={{12,8},{8,4},{4,0},{13,9},{9,5},{5,1},{14,10},{10,6},{6,2},{15,11}... | collective-permute-start | bytes 811016 | tf_op jit(solution)/shard_map/ppermute | solution.py:309
  20.5 1.7 %collective-permute-done.20.refs_12_ = bf16[80,1152]{1,0:T(8,128)(2,1)S(1)} collective-permute-done((bf16[80,1152]{1,0:T(8,128)(2,1)S(1)}, bf16[80,1152]{1,0:T(8,128)(2,1)S(1)}, u32[]{:S(2)}, u32[]{:S(2)}) %collective-permute-start.20) | collective-permute-done | bytes 184352 | tf_op jit(solution)/shard_map/ppermute | solution.py:19
  22.2 1.5 %collective-permute-start.14 = (bf16[80,1152]{1,0:T(8,128)(2,1)S(1)}, bf16[80,1152]{1,0:T(8,128)(2,1)S(1)}, u32[]{:S(2)}, u32[]{:S(2)}) collective-permute-start(bf16[80,1152]{1,0:T(8,128)(2,1)S(1)} %collective-permute-done.12.refs_4_), channel_id=1, source_target_pairs={{0,2},{1,3},{2,0},{3,1},{4,6},{5,7},{6,4},{7,5},{8,10},{9,11},{10,... | collective-permute-start | bytes 552968 | tf_op jit(solution)/shard_map/ppermute | solution.py:24
  24.2 5.2 %collective-permute-done.3.refs_4_ = bf16[528,256]{1,0:T(8,128)(2,1)S(1)} collective-permute-done((bf16[528,256]{1,0:T(8,128)(2,1)S(1)}, bf16[528,256]{1,0:T(8,128)(2,1)S(1)}, u32[]{:S(2)}, u32[]{:S(2)}) %collective-permute-start.3) | collective-permute-done | bytes 270368 | tf_op jit(solution)/shard_map/ppermute | solution.py:309
  29.4 1.5 %collective-permute-start.22 = (bf16[80,1152]{1,0:T(8,128)(2,1)S(1)}, bf16[80,1152]{1,0:T(8,128)(2,1)S(1)}, u32[]{:S(2)}, u32[]{:S(2)}) collective-permute-start(bf16[80,1152]{1,0:T(8,128)(2,1)S(1)} %collective-permute-done.20.refs_12_), channel_id=1, source_target_pairs={{0,2},{1,3},{2,0},{3,1},{4,6},{5,7},{6,4},{7,5},{8,10},{9,11},{10,... | collective-permute-start | bytes 552968 | tf_op jit(solution)/shard_map/ppermute | solution.py:24
  31.4 0.8 %collective-permute-done.18.refs_10_ = bf16[80,1152]{1,0:T(8,128)(2,1)S(1)} collective-permute-done((bf16[80,1152]{1,0:T(8,128)(2,1)S(1)}, bf16[80,1152]{1,0:T(8,128)(2,1)S(1)}, u32[]{:S(2)}, u32[]{:S(2)}) %collective-permute-start.18) | collective-permute-done | bytes 184352 | tf_op jit(solution)/shard_map/ppermute | solution.py:24
  32.3 3.4 %collective-permute-done.22.refs_14_ = bf16[80,1152]{1,0:T(8,128)(2,1)S(1)} collective-permute-done((bf16[80,1152]{1,0:T(8,128)(2,1)S(1)}, bf16[80,1152]{1,0:T(8,128)(2,1)S(1)}, u32[]{:S(2)}, u32[]{:S(2)}) %collective-permute-start.22) | collective-permute-done | bytes 184352 | tf_op jit(solution)/shard_map/ppermute | solution.py:24
  36.3 1.3 %collective-permute-start.4 = (bf16[528,256]{1,0:T(8,128)(2,1)S(1)}, bf16[528,256]{1,0:T(8,128)(2,1)S(1)}, u32[]{:S(2)}, u32[]{:S(2)}) collective-permute-start(bf16[528,256]{1,0:T(8,128)(2,1)S(1)} %collective-permute-done.3.refs_4_), channel_id=1, source_target_pairs={{8,4},{4,0},{9,5},{5,1},{10,6},{6,2},{11,7},{7,3},{24,20},{20,16},... | collective-permute-start | bytes 811016 | tf_op jit(solution)/shard_map/ppermute | solution.py:309
  38.3 2.7 %shard_map.83.refs_7_ = bf16[64,512]{1,0:T(8,128)(2,1)S(1)} custom-call(bf16[128,1152]{1,0:T(8,128)(2,1)S(1)} %get-tuple-element.13.own.refs_0_, bf16[128,1152]{1,0:T(8,128)(2,1)S(1)} %collective-permute-done.6.core.refs_1_, bf16[128,1152]{1,0:T(8,128)(2,1)S(1)} %collective-permute-done.7.far.refs_2_, ...), custom_call_target="tpu_custom_call" | custom-call | flops 301989888 | bytes 4718592 | tf_op jit(solution)/shard_map/pallas_call | solution.py:28
  41.0 0.7 collective-permute-start.2
  41.7 7.3 %collective-permute-done.4.refs_5_ = bf16[528,256]{1,0:T(8,128)(2,1)S(1)} collective-permute-done((bf16[528,256]{1,0:T(8,128)(2,1)S(1)}, bf16[528,256]{1,0:T(8,128)(2,1)S(1)}, u32[]{:S(2)}, u32[]{:S(2)}) %collective-permute-start.4) | collective-permute-done | bytes 270368 | tf_op jit(solution)/shard_map/ppermute | solution.py:309
  49.0 1.3 %collective-permute-start.5 = (bf16[528,256]{1,0:T(8,128)(2,1)S(1)}, bf16[528,256]{1,0:T(8,128)(2,1)S(1)}, u32[]{:S(2)}, u32[]{:S(2)}) collective-permute-start(bf16[528,256]{1,0:T(8,128)(2,1)S(1)} %collective-permute-done.4.refs_5_), channel_id=1, source_target_pairs={{4,0},{5,1},{6,2},{7,3},{20,16},{21,17},{22,18},{23,19}} | collective-permute-start | bytes 811016 | tf_op jit(solution)/shard_map/ppermute | solution.py:309
  50.3 1.6 %collective-permute-start.10 = (bf16[64,512]{1,0:T(8,128)(2,1)S(1)}, bf16[64,512]{1,0:T(8,128)(2,1)S(1)}, u32[]{:S(2)}, u32[]{:S(2)}) collective-permute-start(bf16[64,512]{1,0:T(8,128)(2,1)S(1)} %shard_map.83.refs_7_), channel_id=1, source_target_pairs={{0,8},{4,12},{8,0},{12,4},{1,9},{5,13},{9,1},{13,5},{2,10},{6,14},... | collective-permute-start | bytes 196616 | tf_op jit(solution)/shard_map/ppermute | solution.py:19
  52.0 3.4 %collective-permute-start.11 = (bf16[64,512]{1,0:T(8,128)(2,1)S(1)}, bf16[64,512]{1,0:T(8,128)(2,1)S(1)}, u32[]{:S(2)}, u32[]{:S(2)}) collective-permute-start(bf16[64,512]{1,0:T(8,128)(2,1)S(1)} %shard_map.83.refs_7_), channel_id=1, source_target_pairs={{0,12},{4,0},{8,4},{12,8},{1,13},{5,1},{9,5},{13,9},{2,14},{6,2},{... | collective-permute-start | bytes 196616 | tf_op jit(solution)/shard_map/ppermute | solution.py:19
  55.4 3.7 %shard_map.84 = (bf16[1024,1024]{1,0:T(8,128)(2,1)S(1)}, f32[1024,256]{1,0:T(8,128)S(1)}) custom-call(bf16[128,1152]{1,0:T(8,128)(2,1)S(1)} %get-tuple-element.13.own.refs_0_, bf16[128,1152]{1,0:T(8,128)(2,1)S(1)} %collective-permute-done.6.core.refs_1_, bf16[128,1152]{1,0:T(8,128)(2,1)S(1)} %collective-permute-done.7.far.refs_2_, ...), custom_call_target="tpu_custom_call" | custom-call | flops 3019898880 | bytes 2359296 | tf_op jit(solution)/shard_map/pallas_call | solution.py:28
  59.2 2.6 %collective-permute-done.11.refs_10_ = bf16[64,512]{1,0:T(8,128)(2,1)S(1)} collective-permute-done((bf16[64,512]{1,0:T(8,128)(2,1)S(1)}, bf16[64,512]{1,0:T(8,128)(2,1)S(1)}, u32[]{:S(2)}, u32[]{:S(2)}) %collective-permute-start.11) | collective-permute-done | bytes 65568 | tf_op jit(solution)/shard_map/ppermute | solution.py:19
  61.8 2.3 %shard_map.86 = f32[128,1024]{1,0:T(8,128)S(1)} custom-call(bf16[528,256]{1,0:T(8,128)(2,1)S(1)} %get-tuple-element.12.refs_0_, bf16[528,256]{1,0:T(8,128)(2,1)S(1)} %collective-permute-done.refs_1_, bf16[528,256]{1,0:T(8,128)(2,1)S(1)} %collective-permute-done.1.refs_2_, bf16[528,256]{1,0:T(8,128)(2,1)S(1)} %collective-permute-done.2.refs_3_, ...), custom_call_target="tpu_custom_call" | custom-call | flops 1073741824 | bytes 4194304 | tf_op jit(solution)/shard_map/pallas_call | solution.py:28
  64.2 2.3 %shard_map.85 = f32[128,1024]{1,0:T(8,128)S(1)} custom-call(bf16[528,256]{1,0:T(8,128)(2,1)S(1)} %get-tuple-element.12.refs_0_, bf16[528,256]{1,0:T(8,128)(2,1)S(1)} %collective-permute-done.refs_1_, bf16[528,256]{1,0:T(8,128)(2,1)S(1)} %collective-permute-done.1.refs_2_, bf16[528,256]{1,0:T(8,128)(2,1)S(1)} %collective-permute-done.2.refs_3_, ...), custom_call_target="tpu_custom_call" | custom-call | flops 1073741824 | bytes 4194304 | tf_op jit(solution)/shard_map/pallas_call | solution.py:28
  67.0 5.5 %collective-permute-done.25 = bf16[64,1024]{1,0:T(8,128)(2,1)S(1)} collective-permute-done((bf16[64,1024]{1,0:T(8,128)(2,1)S(1)}, bf16[64,1024]{1,0:T(8,128)(2,1)S(1)}, u32[]{:S(2)}, u32[]{:S(2)}) %collective-permute-start.25) | collective-permute-done | bytes 131104 | tf_op jit(solution)/shard_map/ppermute | solution.py:24
  72.6 1.2 %collective-permute-start.26 = (bf16[64,256]{1,0:T(8,128)(2,1)S(1)}, bf16[64,256]{1,0:T(8,128)(2,1)S(1)}, u32[]{:S(2)}, u32[]{:S(2)}) collective-permute-start(bf16[64,256]{1,0:T(8,128)(2,1)S(1)} %get-tuple-element.21), channel_id=1, source_target_pairs={{0,12},{4,0},{8,4},{12,8},{1,13},{5,1},{9,5},{13,9},{2,14},{6,2},{... | collective-permute-start | bytes 98312 | tf_op jit(solution)/shard_map/ppermute | solution.py:19
  73.8 0.9 %collective-permute-start.28 = (bf16[64,256]{1,0:T(8,128)(2,1)S(1)}, bf16[64,256]{1,0:T(8,128)(2,1)S(1)}, u32[]{:S(2)}, u32[]{:S(2)}) collective-permute-start(bf16[64,256]{1,0:T(8,128)(2,1)S(1)} %get-tuple-element.22), channel_id=1, source_target_pairs={{0,4},{4,8},{8,12},{12,0},{1,5},{5,9},{9,13},{13,1},{2,6},{6,10},{... | collective-permute-start | bytes 98312 | tf_op jit(solution)/shard_map/ppermute | solution.py:19
  74.7 1.9 %collective-permute-done.26 = bf16[64,256]{1,0:T(8,128)(2,1)S(1)} collective-permute-done((bf16[64,256]{1,0:T(8,128)(2,1)S(1)}, bf16[64,256]{1,0:T(8,128)(2,1)S(1)}, u32[]{:S(2)}, u32[]{:S(2)}) %collective-permute-start.26) | collective-permute-done | bytes 32800 | tf_op jit(solution)/shard_map/ppermute | solution.py:19
  76.6 2.1 %collective-permute-done.27 = bf16[64,256]{1,0:T(8,128)(2,1)S(1)} collective-permute-done((bf16[64,256]{1,0:T(8,128)(2,1)S(1)}, bf16[64,256]{1,0:T(8,128)(2,1)S(1)}, u32[]{:S(2)}, u32[]{:S(2)}) %collective-permute-start.27) | collective-permute-done | bytes 32800 | tf_op jit(solution)/shard_map/ppermute | solution.py:19
  78.6 0.9 %collective-permute-done.28 = bf16[64,256]{1,0:T(8,128)(2,1)S(1)} collective-permute-done((bf16[64,256]{1,0:T(8,128)(2,1)S(1)}, bf16[64,256]{1,0:T(8,128)(2,1)S(1)}, u32[]{:S(2)}, u32[]{:S(2)}) %collective-permute-start.28) | collective-permute-done | bytes 32800 | tf_op jit(solution)/shard_map/ppermute | solution.py:19
  (41 shorter events, 3.7 us)
Async XLA Ops:
  1.4 10.7 %collective-permute-start.12 = (bf16[80,1152]{1,0:T(8,128)(2,1)S(1)}, bf16[80,1152]{1,0:T(8,128)(2,1)S(1)}, u32[]{:S(2)}, u32[]{:S(2)}) collective-permute-start(bf16[80,1152]{1,0:T(8,128)(2,1)S(1)} %get-tuple-element.14), channel_id=1, source_target_pairs={{0,4},{4,8},{8,12},{12,0},{1,5},{5,9},{9,13},{13,1},{2,6},{6,10},{... | collective-permute-start | bytes 552968 | tf_op jit(solution)/shard_map/ppermute | solution.py:19
  4.5 14.7 %collective-permute-start.16 = (bf16[80,1152]{1,0:T(8,128)(2,1)S(1)}, bf16[80,1152]{1,0:T(8,128)(2,1)S(1)}, u32[]{:S(2)}, u32[]{:S(2)}) collective-permute-start(bf16[80,1152]{1,0:T(8,128)(2,1)S(1)} %get-tuple-element.15), channel_id=1, source_target_pairs={{0,8},{4,12},{8,0},{12,4},{1,9},{5,13},{9,1},{13,5},{2,10},{6,14},... | collective-permute-start | bytes 552968 | tf_op jit(solution)/shard_map/ppermute | solution.py:19
  7.1 16.6 %collective-permute-start = (bf16[528,256]{1,0:T(8,128)(2,1)S(1)}, bf16[528,256]{1,0:T(8,128)(2,1)S(1)}, u32[]{:S(2)}, u32[]{:S(2)}) collective-permute-start(bf16[528,256]{1,0:T(8,128)(2,1)S(1)} %get-tuple-element.12.refs_0_), channel_id=1, source_target_pairs={{0,4},{4,8},{8,12},{1,5},{5,9},{9,13},{2,6},{6,10},{10,14},{3,7},{... | collective-permute-start | bytes 811016 | tf_op jit(solution)/shard_map/ppermute | solution.py:308
  9.1 15.1 %collective-permute-start.7 = (bf16[128,1152]{1,0:T(8,128)(2,1)S(1)}, bf16[128,1152]{1,0:T(8,128)(2,1)S(1)}, u32[]{:S(2)}, u32[]{:S(2)}) collective-permute-start(bf16[128,1152]{1,0:T(8,128)(2,1)S(1)} %get-tuple-element.13.own.refs_0_), channel_id=1, source_target_pairs={{0,2},{1,3},{2,0},{3,1},{4,6},{5,7},{6,4},{7,5},{8,10},{9,11},{10,... | collective-permute-start | bytes 884744 | tf_op jit(solution)/shard_map/ppermute | solution.py:24
  10.8 20.1 %collective-permute-start.6 = (bf16[128,1152]{1,0:T(8,128)(2,1)S(1)}, bf16[128,1152]{1,0:T(8,128)(2,1)S(1)}, u32[]{:S(2)}, u32[]{:S(2)}) collective-permute-start(bf16[128,1152]{1,0:T(8,128)(2,1)S(1)} %get-tuple-element.13.own.refs_0_), channel_id=1, source_target_pairs={{0,1},{1,0},{2,3},{3,2},{4,5},{5,4},{6,7},{7,6},{8,9},{9,8},{10,11... | collective-permute-start | bytes 884744 | tf_op jit(solution)/shard_map/ppermute | solution.py:24
  12.1 43.3 %copy-start.2 = (bf16[8,1152,128]{2,1,0:T(8,128)(2,1)S(1)}, bf16[8,1152,128]{2,1,0:T(8,128)(2,1)}, u32[]{:S(2)}) copy-start(bf16[8,1152,128]{2,1,0:T(8,128)(2,1)} %refs_16_.1) | copy-start | bytes 7077892
  12.1 10.1 %collective-permute-start.20 = (bf16[80,1152]{1,0:T(8,128)(2,1)S(1)}, bf16[80,1152]{1,0:T(8,128)(2,1)S(1)}, u32[]{:S(2)}, u32[]{:S(2)}) collective-permute-start(bf16[80,1152]{1,0:T(8,128)(2,1)S(1)} %get-tuple-element.16), channel_id=1, source_target_pairs={{0,12},{4,0},{8,4},{12,8},{1,13},{5,1},{9,5},{13,9},{2,14},{6,2},{... | collective-permute-start | bytes 552968 | tf_op jit(solution)/shard_map/ppermute | solution.py:19
  19.2 10.2 %collective-permute-start.3 = (bf16[528,256]{1,0:T(8,128)(2,1)S(1)}, bf16[528,256]{1,0:T(8,128)(2,1)S(1)}, u32[]{:S(2)}, u32[]{:S(2)}) collective-permute-start(bf16[528,256]{1,0:T(8,128)(2,1)S(1)} %get-tuple-element.12.refs_0_), channel_id=1, source_target_pairs={{12,8},{8,4},{4,0},{13,9},{9,5},{5,1},{14,10},{10,6},{6,2},{15,11}... | collective-permute-start | bytes 811016 | tf_op jit(solution)/shard_map/ppermute | solution.py:309
  22.2 8.7 %collective-permute-start.14 = (bf16[80,1152]{1,0:T(8,128)(2,1)S(1)}, bf16[80,1152]{1,0:T(8,128)(2,1)S(1)}, u32[]{:S(2)}, u32[]{:S(2)}) collective-permute-start(bf16[80,1152]{1,0:T(8,128)(2,1)S(1)} %collective-permute-done.12.refs_4_), channel_id=1, source_target_pairs={{0,2},{1,3},{2,0},{3,1},{4,6},{5,7},{6,4},{7,5},{8,10},{9,11},{10,... | collective-permute-start | bytes 552968 | tf_op jit(solution)/shard_map/ppermute | solution.py:24
  23.7 8.6 %collective-permute-start.18 = (bf16[80,1152]{1,0:T(8,128)(2,1)S(1)}, bf16[80,1152]{1,0:T(8,128)(2,1)S(1)}, u32[]{:S(2)}, u32[]{:S(2)}) collective-permute-start(bf16[80,1152]{1,0:T(8,128)(2,1)S(1)} %collective-permute-done.16.refs_8_), channel_id=1, source_target_pairs={{0,2},{1,3},{2,0},{3,1},{4,6},{5,7},{6,4},{7,5},{8,10},{9,11},{10,... | collective-permute-start | bytes 552968 | tf_op jit(solution)/shard_map/ppermute | solution.py:24
  24.2 14.0 %collective-permute-start.8 = (bf16[128,1152]{1,0:T(8,128)(2,1)S(1)}, bf16[128,1152]{1,0:T(8,128)(2,1)S(1)}, u32[]{:S(2)}, u32[]{:S(2)}) collective-permute-start(bf16[128,1152]{1,0:T(8,128)(2,1)S(1)} %collective-permute-done.7.far.refs_2_), channel_id=1, source_target_pairs={{0,1},{1,0},{2,3},{3,2},{4,5},{5,4},{6,7},{7,6},{8,9},{9,8},{10,11... | collective-permute-start | bytes 884744 | tf_op jit(solution)/shard_map/ppermute | solution.py:24
  29.4 6.2 %collective-permute-start.22 = (bf16[80,1152]{1,0:T(8,128)(2,1)S(1)}, bf16[80,1152]{1,0:T(8,128)(2,1)S(1)}, u32[]{:S(2)}, u32[]{:S(2)}) collective-permute-start(bf16[80,1152]{1,0:T(8,128)(2,1)S(1)} %collective-permute-done.20.refs_12_), channel_id=1, source_target_pairs={{0,2},{1,3},{2,0},{3,1},{4,6},{5,7},{6,4},{7,5},{8,10},{9,11},{10,... | collective-permute-start | bytes 552968 | tf_op jit(solution)/shard_map/ppermute | solution.py:24
  30.9 5.4 %collective-permute-start.13 = (bf16[80,1152]{1,0:T(8,128)(2,1)S(1)}, bf16[80,1152]{1,0:T(8,128)(2,1)S(1)}, u32[]{:S(2)}, u32[]{:S(2)}) collective-permute-start(bf16[80,1152]{1,0:T(8,128)(2,1)S(1)} %collective-permute-done.12.refs_4_), channel_id=1, source_target_pairs={{0,1},{1,0},{2,3},{3,2},{4,5},{5,4},{6,7},{7,6},{8,9},{9,8},{10,11... | collective-permute-start | bytes 552968 | tf_op jit(solution)/shard_map/ppermute | solution.py:24
  30.9 6.7 %collective-permute-start.17 = (bf16[80,1152]{1,0:T(8,128)(2,1)S(1)}, bf16[80,1152]{1,0:T(8,128)(2,1)S(1)}, u32[]{:S(2)}, u32[]{:S(2)}) collective-permute-start(bf16[80,1152]{1,0:T(8,128)(2,1)S(1)} %collective-permute-done.16.refs_8_), channel_id=1, source_target_pairs={{0,1},{1,0},{2,3},{3,2},{4,5},{5,4},{6,7},{7,6},{8,9},{9,8},{10,11... | collective-permute-start | bytes 552968 | tf_op jit(solution)/shard_map/ppermute | solution.py:24
  32.3 5.4 %collective-permute-start.21 = (bf16[80,1152]{1,0:T(8,128)(2,1)S(1)}, bf16[80,1152]{1,0:T(8,128)(2,1)S(1)}, u32[]{:S(2)}, u32[]{:S(2)}) collective-permute-start(bf16[80,1152]{1,0:T(8,128)(2,1)S(1)} %collective-permute-done.20.refs_12_), channel_id=1, source_target_pairs={{0,1},{1,0},{2,3},{3,2},{4,5},{5,4},{6,7},{7,6},{8,9},{9,8},{10,11... | collective-permute-start | bytes 552968 | tf_op jit(solution)/shard_map/ppermute | solution.py:24
  35.6 5.4 %collective-permute-start.1 = (bf16[528,256]{1,0:T(8,128)(2,1)S(1)}, bf16[528,256]{1,0:T(8,128)(2,1)S(1)}, u32[]{:S(2)}, u32[]{:S(2)}) collective-permute-start(bf16[528,256]{1,0:T(8,128)(2,1)S(1)} %collective-permute-done.refs_1_), channel_id=1, source_target_pairs={{4,8},{8,12},{5,9},{9,13},{6,10},{10,14},{7,11},{11,15},{20,24},{2... | collective-permute-start | bytes 811016 | tf_op jit(solution)/shard_map/ppermute | solution.py:308
  36.3 12.7 %collective-permute-start.4 = (bf16[528,256]{1,0:T(8,128)(2,1)S(1)}, bf16[528,256]{1,0:T(8,128)(2,1)S(1)}, u32[]{:S(2)}, u32[]{:S(2)}) collective-permute-start(bf16[528,256]{1,0:T(8,128)(2,1)S(1)} %collective-permute-done.3.refs_4_), channel_id=1, source_target_pairs={{8,4},{4,0},{9,5},{5,1},{10,6},{6,2},{11,7},{7,3},{24,20},{20,16},... | collective-permute-start | bytes 811016 | tf_op jit(solution)/shard_map/ppermute | solution.py:309
  37.6 12.7 %collective-permute-start.15 = (bf16[80,1152]{1,0:T(8,128)(2,1)S(1)}, bf16[80,1152]{1,0:T(8,128)(2,1)S(1)}, u32[]{:S(2)}, u32[]{:S(2)}) collective-permute-start(bf16[80,1152]{1,0:T(8,128)(2,1)S(1)} %collective-permute-done.14.refs_6_), channel_id=1, source_target_pairs={{0,1},{1,0},{2,3},{3,2},{4,5},{5,4},{6,7},{7,6},{8,9},{9,8},{10,11... | collective-permute-start | bytes 552968 | tf_op jit(solution)/shard_map/ppermute | solution.py:24
  37.7 14.3 %collective-permute-start.19 = (bf16[80,1152]{1,0:T(8,128)(2,1)S(1)}, bf16[80,1152]{1,0:T(8,128)(2,1)S(1)}, u32[]{:S(2)}, u32[]{:S(2)}) collective-permute-start(bf16[80,1152]{1,0:T(8,128)(2,1)S(1)} %collective-permute-done.18.refs_10_), channel_id=1, source_target_pairs={{0,1},{1,0},{2,3},{3,2},{4,5},{5,4},{6,7},{7,6},{8,9},{9,8},{10,11... | collective-permute-start | bytes 552968 | tf_op jit(solution)/shard_map/ppermute | solution.py:24
  38.2 17.2 %collective-permute-start.23 = (bf16[80,1152]{1,0:T(8,128)(2,1)S(1)}, bf16[80,1152]{1,0:T(8,128)(2,1)S(1)}, u32[]{:S(2)}, u32[]{:S(2)}) collective-permute-start(bf16[80,1152]{1,0:T(8,128)(2,1)S(1)} %collective-permute-done.22.refs_14_), channel_id=1, source_target_pairs={{0,1},{1,0},{2,3},{3,2},{4,5},{5,4},{6,7},{7,6},{8,9},{9,8},{10,11... | collective-permute-start | bytes 552968 | tf_op jit(solution)/shard_map/ppermute | solution.py:24
  41.0 20.8 %copy-start = (s32[256]{0:T(256)S(1)}, s32[256]{0:T(256)}, u32[]{:S(2)}) copy-start(s32[256]{0:T(256)} %param.11) | copy-start | bytes 3076
  41.0 20.8 %copy-start.1 = (s32[4,4]{1,0:T(4,128)S(1)}, s32[4,4]{1,0:T(4,128)}, u32[]{:S(2)}) copy-start(s32[4,4]{1,0:T(4,128)} %refs_14_.3) | copy-start | bytes 196
  41.0 20.8 %collective-permute-start.2 = (bf16[528,256]{1,0:T(8,128)(2,1)S(1)}, bf16[528,256]{1,0:T(8,128)(2,1)S(1)}, u32[]{:S(2)}, u32[]{:S(2)}) collective-permute-start(bf16[528,256]{1,0:T(8,128)(2,1)S(1)} %collective-permute-done.1.refs_2_), channel_id=1, source_target_pairs={{8,12},{9,13},{10,14},{11,15},{24,28},{25,29},{26,30},{27,31}} | collective-permute-start | bytes 811016 | tf_op jit(solution)/shard_map/ppermute | solution.py:308
  49.0 12.8 %collective-permute-start.5 = (bf16[528,256]{1,0:T(8,128)(2,1)S(1)}, bf16[528,256]{1,0:T(8,128)(2,1)S(1)}, u32[]{:S(2)}, u32[]{:S(2)}) collective-permute-start(bf16[528,256]{1,0:T(8,128)(2,1)S(1)} %collective-permute-done.4.refs_5_), channel_id=1, source_target_pairs={{4,0},{5,1},{6,2},{7,3},{20,16},{21,17},{22,18},{23,19}} | collective-permute-start | bytes 811016 | tf_op jit(solution)/shard_map/ppermute | solution.py:309
  50.3 8.8 %collective-permute-start.10 = (bf16[64,512]{1,0:T(8,128)(2,1)S(1)}, bf16[64,512]{1,0:T(8,128)(2,1)S(1)}, u32[]{:S(2)}, u32[]{:S(2)}) collective-permute-start(bf16[64,512]{1,0:T(8,128)(2,1)S(1)} %shard_map.83.refs_7_), channel_id=1, source_target_pairs={{0,8},{4,12},{8,0},{12,4},{1,9},{5,13},{9,1},{13,5},{2,10},{6,14},... | collective-permute-start | bytes 196616 | tf_op jit(solution)/shard_map/ppermute | solution.py:19
  52.0 9.9 %collective-permute-start.11 = (bf16[64,512]{1,0:T(8,128)(2,1)S(1)}, bf16[64,512]{1,0:T(8,128)(2,1)S(1)}, u32[]{:S(2)}, u32[]{:S(2)}) collective-permute-start(bf16[64,512]{1,0:T(8,128)(2,1)S(1)} %shard_map.83.refs_7_), channel_id=1, source_target_pairs={{0,12},{4,0},{8,4},{12,8},{1,13},{5,1},{9,5},{13,9},{2,14},{6,2},{... | collective-permute-start | bytes 196616 | tf_op jit(solution)/shard_map/ppermute | solution.py:19
  55.4 6.4 %collective-permute-start.9 = (bf16[64,512]{1,0:T(8,128)(2,1)S(1)}, bf16[64,512]{1,0:T(8,128)(2,1)S(1)}, u32[]{:S(2)}, u32[]{:S(2)}) collective-permute-start(bf16[64,512]{1,0:T(8,128)(2,1)S(1)} %shard_map.83.refs_7_), channel_id=1, source_target_pairs={{0,4},{4,8},{8,12},{12,0},{1,5},{5,9},{9,13},{13,1},{2,6},{6,10},{... | collective-permute-start | bytes 196616 | tf_op jit(solution)/shard_map/ppermute | solution.py:19
  64.1 2.4 %collective-permute-start.24 = (f32[128,1024]{1,0:T(8,128)S(1)}, f32[128,1024]{1,0:T(8,128)S(1)}, u32[]{:S(2)}, u32[]{:S(2)}) collective-permute-start(f32[128,1024]{1,0:T(8,128)S(1)} %shard_map.86), channel_id=1, source_target_pairs={{0,1},{1,0},{2,3},{3,2},{4,5},{5,4},{6,7},{7,6},{8,9},{9,8},{10,11... | collective-permute-start | bytes 1572872 | tf_op jit(solution)/shard_map/ppermute | solution.py:24
  66.6 6.0 %collective-permute-start.25 = (bf16[64,1024]{1,0:T(8,128)(2,1)S(1)}, bf16[64,1024]{1,0:T(8,128)(2,1)S(1)}, u32[]{:S(2)}, u32[]{:S(2)}) collective-permute-start(bf16[64,1024]{1,0:T(8,128)(2,1)S(1)} %fusion), channel_id=1, source_target_pairs={{0,2},{1,3},{2,0},{3,1},{4,6},{5,7},{6,4},{7,5},{8,10},{9,11},{10,... | collective-permute-start | bytes 393224 | tf_op jit(solution)/shard_map/ppermute | solution.py:24
  72.6 4.0 %collective-permute-start.26 = (bf16[64,256]{1,0:T(8,128)(2,1)S(1)}, bf16[64,256]{1,0:T(8,128)(2,1)S(1)}, u32[]{:S(2)}, u32[]{:S(2)}) collective-permute-start(bf16[64,256]{1,0:T(8,128)(2,1)S(1)} %get-tuple-element.21), channel_id=1, source_target_pairs={{0,12},{4,0},{8,4},{12,8},{1,13},{5,1},{9,5},{13,9},{2,14},{6,2},{... | collective-permute-start | bytes 98312 | tf_op jit(solution)/shard_map/ppermute | solution.py:19
  73.8 4.8 %collective-permute-start.27 = (bf16[64,256]{1,0:T(8,128)(2,1)S(1)}, bf16[64,256]{1,0:T(8,128)(2,1)S(1)}, u32[]{:S(2)}, u32[]{:S(2)}) collective-permute-start(bf16[64,256]{1,0:T(8,128)(2,1)S(1)} %get-tuple-element.23), channel_id=1, source_target_pairs={{0,8},{4,12},{8,0},{12,4},{1,9},{5,13},{9,1},{13,5},{2,10},{6,14},... | collective-permute-start | bytes 98312 | tf_op jit(solution)/shard_map/ppermute | solution.py:19
  73.8 5.7 %collective-permute-start.28 = (bf16[64,256]{1,0:T(8,128)(2,1)S(1)}, bf16[64,256]{1,0:T(8,128)(2,1)S(1)}, u32[]{:S(2)}, u32[]{:S(2)}) collective-permute-start(bf16[64,256]{1,0:T(8,128)(2,1)S(1)} %get-tuple-element.22), channel_id=1, source_target_pairs={{0,4},{4,8},{8,12},{12,0},{1,5},{5,9},{9,13},{13,1},{2,6},{6,10},{... | collective-permute-start | bytes 98312 | tf_op jit(solution)/shard_map/ppermute | solution.py:19

commit v2 on v1

--- a/solution.py
+++ b/solution.py
@@ -70,7 +70,9 @@
     )
 
 
-def front_kernel(targets, sources, attn, spos, tpos, own, first, second, third, table, held, spots, done):
+def front_kernel(
+    targets, sources, attn, spos, tpos, pattern, own, first, second, third, table, kept, held, spots, flags, done
+):
     z = lax.axis_index("tgt")
     rows, sub = targets.shape[0], sources.shape[0]
     part = own.shape[1]
@@ -80,7 +82,7 @@
     def columns(index):
         return pl.ds(pl.multiple_of(index * part, 128), part)
 
-    moves = [(attn, held), (spos, spots.at[0]), (tpos, spots.at[1])]
+    moves = [(attn, held), (spos, spots.at[0]), (tpos, spots.at[1]), (pattern, flags)]
     for k, out in enumerate((first, second, third), 1):
         at = columns(jnp.where(z + k >= 4, z + k - 4, z + k))
         moves.append((targets.at[:, at], out.at[pl.ds(0, rows)]))
@@ -91,7 +93,7 @@
     copies = [pltpu.make_async_copy(*ends, done.at[i]) for i, ends in enumerate(moves)]
     for copy in copies:
         copy.start()
-    for copy in copies[:3]:
+    for copy in copies[:4]:
         copy.wait()
     picks = lax.broadcasted_iota(jnp.int32, (keys, spos.shape[1]), 0) == by_core(spots[0])
     picks = picks.astype(F32).astype(BF16)
@@ -101,7 +103,11 @@
     table[base:, :] = jnp.broadcast_to(
         spots[1].astype(F32), (table.shape[0] - base, tpos.shape[1])
     ).astype(BF16)
-    for copy in copies[3:]:
+    across = lax.broadcasted_iota(jnp.int32, pattern.shape, 0) == lax.axis_index("src")
+    down = lax.broadcasted_iota(jnp.int32, pattern.shape, 1) == z
+    flag = jnp.where(across & down, flags[...], 0).astype(F32)
+    kept[...] = jnp.broadcast_to(jnp.sum(flag, keepdims=True), kept.shape)
+    for copy in copies[4:]:
         copy.wait()
 
 
@@ -178,7 +184,7 @@
 def edges_kernel(heads, queries, flip, *refs):
     home, right1, right2, right3, left1, left2, left3 = refs[:7]
     blocks_of_values = refs[7:11]
-    reads, direct, spos, pattern, out, table, values = refs[11:]
+    reads, direct, spos, out, table, values = refs[11:]
     z, s = lax.axis_index("tgt"), lax.axis_index("src")
     side = (s % 2) ^ flip
     sources = spos.shape[1]
@@ -255,8 +261,7 @@
         turned = (mixed + same * direct[here, lanes]).T
         for x in range(2):
             row = jnp.where(s // 2 == x, block, 0)
-            kept = pattern[2 * x + side, origin_of(z, k)].astype(F32)
-            out[aligned(row, block), here] = turned[x * block : (x + 1) * block, :] * kept
+            out[aligned(row, block), here] = turned[x * block : (x + 1) * block, :]
 
 
 def resident(
@@ -281,16 +286,17 @@
         front_kernel,
         (shape(rows + 4 * sub, part),)
         + (shape(rows + sub, part),) * 3
-        + (shape(heads * queries + 16, sources),),
-        [target_rows, decoder_rows, attention, spots, target_pos[None, :]],
+        + (shape(heads * queries + 16, sources), shape(1, targets, dtype=F32)),
+        [target_rows, decoder_rows, attention, spots, target_pos[None, :], tile_pattern],
         2 * attention.size * sources,
         target_rows.size * 4,
         [
             pltpu.VMEM(attention.shape, BF16),
             pltpu.VMEM((2, 1, sources), jnp.int32),
-            pltpu.SemaphoreType.DMA((14,)),
+            pltpu.VMEM(tile_pattern.shape, jnp.int32),
+            pltpu.SemaphoreType.DMA((15,)),
         ],
-        hbm=(0, 1, 2, 3, 4),
+        hbm=(0, 1, 2, 3, 4, 5),
     )
     own, far, core, cross = [cut[0]], [], [], []
     for k in range(1, blocks):
@@ -337,11 +343,10 @@
         return kernel_call(
             functools.partial(edges_kernel, heads, queries, flip),
             shape(sources // 2, blocks * targets, dtype=F32),
-            [home, *rightward[1:], *leftward[1:], *values, reads, direct, spots, tile_pattern],
+            [home, *rightward[1:], *leftward[1:], *values, reads, direct, spots],
             2 * 2 * blocks * targets * sources * heads * head_dim,
             1 << 22,
             [pltpu.VMEM((4,) + home.shape, BF16), pltpu.VMEM((sources, groups * head_dim), BF16)],
-            smem=(14,),
         )
 
     away = swapped(edges(1), "src", 1)
@@ -353,7 +358,7 @@
     result = parts[0]
     for value in landed:
         result = result + value.astype(F32)
-    return result.astype(BF16)
+    return (result * cut[5]).astype(BF16)
 
 
 def ring(

time: 80.4 us -> 79.2 us (0.985)
  Pallas kernels: 12.4 us -> 11.3 us
    pallas_call x5, Pallas kernels: 12.4 us -> 11.3 us  [kernel_call(): pl.pallas_call(body, out_shape=outs, in_specs=[pl.BlockSpec(memory_space=...]
  transfers between devices with their start and end apart: 29 -> 29, of which waited for: 12 -> 13; matrix products, arithmetic and copies ran while one was open for 0% -> 0% of each run, Pallas kernels for 11% -> 10%
where the time goes in v2:
time: 79.2 us; the launch traced here: 79 us
  waiting for transfers between devices  37.6 us (47%)
  starting transfers between devices  29.1 us (37%)
  Pallas kernels  11.3 us (14%)
    ppermute x9, waiting for transfers between devices, passed_along(): return lax.ppermute(value, axis, pairs)  15.4 us
    ppermute x9, starting transfers between devices, passed_along(): return lax.ppermute(value, axis, pairs)  15 us
    ppermute x3, waiting for transfers between devices, resident(): leftward.append(lax.ppermute(leftward[-1], 'tgt', down))  12.5 us
    pallas_call x5, Pallas kernels, kernel_call(): pl.pallas_call(body, out_shape=outs, in_specs=[pl.BlockSpec(memory_space=...  11.3 us
    ppermute x14, waiting for transfers between devices, swapped(): return lax.ppermute(value, axis, pairs)  9.72 us
    ppermute x14, starting transfers between devices, swapped(): return lax.ppermute(value, axis, pairs)  6.92 us
    ppermute x3, starting transfers between devices, resident(): leftward.append(lax.ppermute(leftward[-1], 'tgt', down))  3.85 us
    ppermute x3, starting transfers between devices, resident(): rightward.append(lax.ppermute(rightward[-1], 'tgt', up))  3.33 us
  transfers between devices with their start and end apart: 29, of which 13 were waited for; matrix products, arithmetic and copies ran while one was open for 0% of the time, Pallas kernels for 10%

profile of v2, /device:TPU:0, one launch (start us, length us, event | category | flops | bytes accessed | tf_op | source)
XLA Modules:
  0.0 79.0 jit_solution(13335734805448211063)
XLA Ops:
  0.0 1.4 %shard_map.82 = (bf16[128,1152]{1,0:T(8,128)(2,1)S(1)}, bf16[80,1152]{1,0:T(8,128)(2,1)S(1)}, bf16[80,1152]{1,0:T(8,128)(2,1)S(1)}, bf16[80,1152]{1,0:T(8,128)(2...) custom-call(bf16[64,4608]{1,0:T(8,128)(2,1)} %targets.1, bf16[16,4608]{1,0:T(8,128)(2,1)} %sources.1, ...), custom_call_target="tpu_custom_call" | custom-call | flops 67108864 | bytes 1179648 | tf_op jit(solution)/shard_map/pallas_call | solution.py:28
  1.4 3.1 %collective-permute-start.12 = (bf16[80,1152]{1,0:T(8,128)(2,1)S(1)}, bf16[80,1152]{1,0:T(8,128)(2,1)S(1)}, u32[]{:S(2)}, u32[]{:S(2)}) collective-permute-start(bf16[80,1152]{1,0:T(8,128)(2,1)S(1)} %get-tuple-element.15), channel_id=1, source_target_pairs={{0,4},{4,8},{8,12},{12,0},{1,5},{5,9},{9,13},{13,1},{2,6},{6,10},{... | collective-permute-start | bytes 552968 | tf_op jit(solution)/shard_map/ppermute | solution.py:19
  4.5 2.6 %collective-permute-start.16 = (bf16[80,1152]{1,0:T(8,128)(2,1)S(1)}, bf16[80,1152]{1,0:T(8,128)(2,1)S(1)}, u32[]{:S(2)}, u32[]{:S(2)}) collective-permute-start(bf16[80,1152]{1,0:T(8,128)(2,1)S(1)} %get-tuple-element.16), channel_id=1, source_target_pairs={{0,8},{4,12},{8,0},{12,4},{1,9},{5,13},{9,1},{13,5},{2,10},{6,14},... | collective-permute-start | bytes 552968 | tf_op jit(solution)/shard_map/ppermute | solution.py:19
  7.1 2.0 %collective-permute-start = (bf16[528,256]{1,0:T(8,128)(2,1)S(1)}, bf16[528,256]{1,0:T(8,128)(2,1)S(1)}, u32[]{:S(2)}, u32[]{:S(2)}) collective-permute-start(bf16[528,256]{1,0:T(8,128)(2,1)S(1)} %get-tuple-element.13.refs_0_), channel_id=1, source_target_pairs={{0,4},{4,8},{8,12},{1,5},{5,9},{9,13},{2,6},{6,10},{10,14},{3,7},{... | collective-permute-start | bytes 811016 | tf_op jit(solution)/shard_map/ppermute | solution.py:314
  9.1 1.7 %collective-permute-start.7 = (bf16[128,1152]{1,0:T(8,128)(2,1)S(1)}, bf16[128,1152]{1,0:T(8,128)(2,1)S(1)}, u32[]{:S(2)}, u32[]{:S(2)}) collective-permute-start(bf16[128,1152]{1,0:T(8,128)(2,1)S(1)} %get-tuple-element.14.own.refs_0_), channel_id=1, source_target_pairs={{0,2},{1,3},{2,0},{3,1},{4,6},{5,7},{6,4},{7,5},{8,10},{9,11},{10,... | collective-permute-start | bytes 884744 | tf_op jit(solution)/shard_map/ppermute | solution.py:24
  10.8 1.3 %collective-permute-done.12.refs_4_ = bf16[80,1152]{1,0:T(8,128)(2,1)S(1)} collective-permute-done((bf16[80,1152]{1,0:T(8,128)(2,1)S(1)}, bf16[80,1152]{1,0:T(8,128)(2,1)S(1)}, u32[]{:S(2)}, u32[]{:S(2)}) %collective-permute-start.12) | collective-permute-done | bytes 184352 | tf_op jit(solution)/shard_map/ppermute | solution.py:19
  12.1 2.2 %collective-permute-start.20 = (bf16[80,1152]{1,0:T(8,128)(2,1)S(1)}, bf16[80,1152]{1,0:T(8,128)(2,1)S(1)}, u32[]{:S(2)}, u32[]{:S(2)}) collective-permute-start(bf16[80,1152]{1,0:T(8,128)(2,1)S(1)} %get-tuple-element.17), channel_id=1, source_target_pairs={{0,12},{4,0},{8,4},{12,8},{1,13},{5,1},{9,5},{13,9},{2,14},{6,2},{... | collective-permute-start | bytes 552968 | tf_op jit(solution)/shard_map/ppermute | solution.py:19
  14.3 4.9 %collective-permute-done.16.refs_8_ = bf16[80,1152]{1,0:T(8,128)(2,1)S(1)} collective-permute-done((bf16[80,1152]{1,0:T(8,128)(2,1)S(1)}, bf16[80,1152]{1,0:T(8,128)(2,1)S(1)}, u32[]{:S(2)}, u32[]{:S(2)}) %collective-permute-start.16) | collective-permute-done | bytes 184352 | tf_op jit(solution)/shard_map/ppermute | solution.py:19
  19.2 1.3 %collective-permute-start.3 = (bf16[528,256]{1,0:T(8,128)(2,1)S(1)}, bf16[528,256]{1,0:T(8,128)(2,1)S(1)}, u32[]{:S(2)}, u32[]{:S(2)}) collective-permute-start(bf16[528,256]{1,0:T(8,128)(2,1)S(1)} %get-tuple-element.13.refs_0_), channel_id=1, source_target_pairs={{12,8},{8,4},{4,0},{13,9},{9,5},{5,1},{14,10},{10,6},{6,2},{15,11}... | collective-permute-start | bytes 811016 | tf_op jit(solution)/shard_map/ppermute | solution.py:315
  20.5 1.7 %collective-permute-done.20.refs_12_ = bf16[80,1152]{1,0:T(8,128)(2,1)S(1)} collective-permute-done((bf16[80,1152]{1,0:T(8,128)(2,1)S(1)}, bf16[80,1152]{1,0:T(8,128)(2,1)S(1)}, u32[]{:S(2)}, u32[]{:S(2)}) %collective-permute-start.20) | collective-permute-done | bytes 184352 | tf_op jit(solution)/shard_map/ppermute | solution.py:19
  22.2 1.5 %collective-permute-start.14 = (bf16[80,1152]{1,0:T(8,128)(2,1)S(1)}, bf16[80,1152]{1,0:T(8,128)(2,1)S(1)}, u32[]{:S(2)}, u32[]{:S(2)}) collective-permute-start(bf16[80,1152]{1,0:T(8,128)(2,1)S(1)} %collective-permute-done.12.refs_4_), channel_id=1, source_target_pairs={{0,2},{1,3},{2,0},{3,1},{4,6},{5,7},{6,4},{7,5},{8,10},{9,11},{10,... | collective-permute-start | bytes 552968 | tf_op jit(solution)/shard_map/ppermute | solution.py:24
  24.2 5.2 %collective-permute-done.3.refs_4_ = bf16[528,256]{1,0:T(8,128)(2,1)S(1)} collective-permute-done((bf16[528,256]{1,0:T(8,128)(2,1)S(1)}, bf16[528,256]{1,0:T(8,128)(2,1)S(1)}, u32[]{:S(2)}, u32[]{:S(2)}) %collective-permute-start.3) | collective-permute-done | bytes 270368 | tf_op jit(solution)/shard_map/ppermute | solution.py:315
  29.4 1.5 %collective-permute-start.22 = (bf16[80,1152]{1,0:T(8,128)(2,1)S(1)}, bf16[80,1152]{1,0:T(8,128)(2,1)S(1)}, u32[]{:S(2)}, u32[]{:S(2)}) collective-permute-start(bf16[80,1152]{1,0:T(8,128)(2,1)S(1)} %collective-permute-done.20.refs_12_), channel_id=1, source_target_pairs={{0,2},{1,3},{2,0},{3,1},{4,6},{5,7},{6,4},{7,5},{8,10},{9,11},{10,... | collective-permute-start | bytes 552968 | tf_op jit(solution)/shard_map/ppermute | solution.py:24
  31.4 0.9 %collective-permute-done.18.refs_10_ = bf16[80,1152]{1,0:T(8,128)(2,1)S(1)} collective-permute-done((bf16[80,1152]{1,0:T(8,128)(2,1)S(1)}, bf16[80,1152]{1,0:T(8,128)(2,1)S(1)}, u32[]{:S(2)}, u32[]{:S(2)}) %collective-permute-start.18) | collective-permute-done | bytes 184352 | tf_op jit(solution)/shard_map/ppermute | solution.py:24
  32.3 3.3 %collective-permute-done.22.refs_14_ = bf16[80,1152]{1,0:T(8,128)(2,1)S(1)} collective-permute-done((bf16[80,1152]{1,0:T(8,128)(2,1)S(1)}, bf16[80,1152]{1,0:T(8,128)(2,1)S(1)}, u32[]{:S(2)}, u32[]{:S(2)}) %collective-permute-start.22) | collective-permute-done | bytes 184352 | tf_op jit(solution)/shard_map/ppermute | solution.py:24
  36.3 1.3 %collective-permute-start.4 = (bf16[528,256]{1,0:T(8,128)(2,1)S(1)}, bf16[528,256]{1,0:T(8,128)(2,1)S(1)}, u32[]{:S(2)}, u32[]{:S(2)}) collective-permute-start(bf16[528,256]{1,0:T(8,128)(2,1)S(1)} %collective-permute-done.3.refs_4_), channel_id=1, source_target_pairs={{8,4},{4,0},{9,5},{5,1},{10,6},{6,2},{11,7},{7,3},{24,20},{20,16},... | collective-permute-start | bytes 811016 | tf_op jit(solution)/shard_map/ppermute | solution.py:315
  38.3 2.7 %shard_map.83.refs_7_ = bf16[64,512]{1,0:T(8,128)(2,1)S(1)} custom-call(bf16[128,1152]{1,0:T(8,128)(2,1)S(1)} %get-tuple-element.14.own.refs_0_, bf16[128,1152]{1,0:T(8,128)(2,1)S(1)} %collective-permute-done.6.core.refs_1_, bf16[128,1152]{1,0:T(8,128)(2,1)S(1)} %collective-permute-done.7.far.refs_2_, ...), custom_call_target="tpu_custom_call" | custom-call | flops 301989888 | bytes 4718592 | tf_op jit(solution)/shard_map/pallas_call | solution.py:28
  41.0 0.7 collective-permute-start.2
  41.7 7.3 %collective-permute-done.4.refs_5_ = bf16[528,256]{1,0:T(8,128)(2,1)S(1)} collective-permute-done((bf16[528,256]{1,0:T(8,128)(2,1)S(1)}, bf16[528,256]{1,0:T(8,128)(2,1)S(1)}, u32[]{:S(2)}, u32[]{:S(2)}) %collective-permute-start.4) | collective-permute-done | bytes 270368 | tf_op jit(solution)/shard_map/ppermute | solution.py:315
  49.0 1.3 %collective-permute-start.5 = (bf16[528,256]{1,0:T(8,128)(2,1)S(1)}, bf16[528,256]{1,0:T(8,128)(2,1)S(1)}, u32[]{:S(2)}, u32[]{:S(2)}) collective-permute-start(bf16[528,256]{1,0:T(8,128)(2,1)S(1)} %collective-permute-done.4.refs_5_), channel_id=1, source_target_pairs={{4,0},{5,1},{6,2},{7,3},{20,16},{21,17},{22,18},{23,19}} | collective-permute-start | bytes 811016 | tf_op jit(solution)/shard_map/ppermute | solution.py:315
  50.3 1.6 %collective-permute-start.10 = (bf16[64,512]{1,0:T(8,128)(2,1)S(1)}, bf16[64,512]{1,0:T(8,128)(2,1)S(1)}, u32[]{:S(2)}, u32[]{:S(2)}) collective-permute-start(bf16[64,512]{1,0:T(8,128)(2,1)S(1)} %shard_map.83.refs_7_), channel_id=1, source_target_pairs={{0,8},{4,12},{8,0},{12,4},{1,9},{5,13},{9,1},{13,5},{2,10},{6,14},... | collective-permute-start | bytes 196616 | tf_op jit(solution)/shard_map/ppermute | solution.py:19
  52.0 3.4 %collective-permute-start.11 = (bf16[64,512]{1,0:T(8,128)(2,1)S(1)}, bf16[64,512]{1,0:T(8,128)(2,1)S(1)}, u32[]{:S(2)}, u32[]{:S(2)}) collective-permute-start(bf16[64,512]{1,0:T(8,128)(2,1)S(1)} %shard_map.83.refs_7_), channel_id=1, source_target_pairs={{0,12},{4,0},{8,4},{12,8},{1,13},{5,1},{9,5},{13,9},{2,14},{6,2},{... | collective-permute-start | bytes 196616 | tf_op jit(solution)/shard_map/ppermute | solution.py:19
  55.4 3.7 %shard_map.84 = (bf16[1024,1024]{1,0:T(8,128)(2,1)S(1)}, f32[1024,256]{1,0:T(8,128)S(1)}) custom-call(bf16[128,1152]{1,0:T(8,128)(2,1)S(1)} %get-tuple-element.14.own.refs_0_, bf16[128,1152]{1,0:T(8,128)(2,1)S(1)} %collective-permute-done.6.core.refs_1_, bf16[128,1152]{1,0:T(8,128)(2,1)S(1)} %collective-permute-done.7.far.refs_2_, ...), custom_call_target="tpu_custom_call" | custom-call | flops 3019898880 | bytes 2359296 | tf_op jit(solution)/shard_map/pallas_call | solution.py:28
  59.2 2.6 %collective-permute-done.11.refs_10_ = bf16[64,512]{1,0:T(8,128)(2,1)S(1)} collective-permute-done((bf16[64,512]{1,0:T(8,128)(2,1)S(1)}, bf16[64,512]{1,0:T(8,128)(2,1)S(1)}, u32[]{:S(2)}, u32[]{:S(2)}) %collective-permute-start.11) | collective-permute-done | bytes 65568 | tf_op jit(solution)/shard_map/ppermute | solution.py:19
  61.9 1.7 %shard_map.86 = f32[128,1024]{1,0:T(8,128)S(1)} custom-call(bf16[528,256]{1,0:T(8,128)(2,1)S(1)} %get-tuple-element.13.refs_0_, bf16[528,256]{1,0:T(8,128)(2,1)S(1)} %collective-permute-done.refs_1_, bf16[528,256]{1,0:T(8,128)(2,1)S(1)} %collective-permute-done.1.refs_2_, bf16[528,256]{1,0:T(8,128)(2,1)S(1)} %collective-permute-done.2.refs_3_, ...), custom_call_target="tpu_custom_call" | custom-call | flops 1073741824 | bytes 4194304 | tf_op jit(solution)/shard_map/pallas_call | solution.py:28
  63.6 1.7 %shard_map.85 = f32[128,1024]{1,0:T(8,128)S(1)} custom-call(bf16[528,256]{1,0:T(8,128)(2,1)S(1)} %get-tuple-element.13.refs_0_, bf16[528,256]{1,0:T(8,128)(2,1)S(1)} %collective-permute-done.refs_1_, bf16[528,256]{1,0:T(8,128)(2,1)S(1)} %collective-permute-done.1.refs_2_, bf16[528,256]{1,0:T(8,128)(2,1)S(1)} %collective-permute-done.2.refs_3_, ...), custom_call_target="tpu_custom_call" | custom-call | flops 1073741824 | bytes 4194304 | tf_op jit(solution)/shard_map/pallas_call | solution.py:28
  66.0 5.3 %collective-permute-done.25 = bf16[64,1024]{1,0:T(8,128)(2,1)S(1)} collective-permute-done((bf16[64,1024]{1,0:T(8,128)(2,1)S(1)}, bf16[64,1024]{1,0:T(8,128)(2,1)S(1)}, u32[]{:S(2)}, u32[]{:S(2)}) %collective-permute-start.25) | collective-permute-done | bytes 131104 | tf_op jit(solution)/shard_map/ppermute | solution.py:24
  71.4 1.2 %collective-permute-start.26 = (bf16[64,256]{1,0:T(8,128)(2,1)S(1)}, bf16[64,256]{1,0:T(8,128)(2,1)S(1)}, u32[]{:S(2)}, u32[]{:S(2)}) collective-permute-start(bf16[64,256]{1,0:T(8,128)(2,1)S(1)} %get-tuple-element.23), channel_id=1, source_target_pairs={{0,12},{4,0},{8,4},{12,8},{1,13},{5,1},{9,5},{13,9},{2,14},{6,2},{... | collective-permute-start | bytes 98312 | tf_op jit(solution)/shard_map/ppermute | solution.py:19
  72.7 0.9 %collective-permute-start.28 = (bf16[64,256]{1,0:T(8,128)(2,1)S(1)}, bf16[64,256]{1,0:T(8,128)(2,1)S(1)}, u32[]{:S(2)}, u32[]{:S(2)}) collective-permute-start(bf16[64,256]{1,0:T(8,128)(2,1)S(1)} %get-tuple-element.24), channel_id=1, source_target_pairs={{0,4},{4,8},{8,12},{12,0},{1,5},{5,9},{9,13},{13,1},{2,6},{6,10},{... | collective-permute-start | bytes 98312 | tf_op jit(solution)/shard_map/ppermute | solution.py:19
  73.5 1.9 %collective-permute-done.26 = bf16[64,256]{1,0:T(8,128)(2,1)S(1)} collective-permute-done((bf16[64,256]{1,0:T(8,128)(2,1)S(1)}, bf16[64,256]{1,0:T(8,128)(2,1)S(1)}, u32[]{:S(2)}, u32[]{:S(2)}) %collective-permute-start.26) | collective-permute-done | bytes 32800 | tf_op jit(solution)/shard_map/ppermute | solution.py:19
  75.4 2.1 %collective-permute-done.27 = bf16[64,256]{1,0:T(8,128)(2,1)S(1)} collective-permute-done((bf16[64,256]{1,0:T(8,128)(2,1)S(1)}, bf16[64,256]{1,0:T(8,128)(2,1)S(1)}, u32[]{:S(2)}, u32[]{:S(2)}) %collective-permute-start.27) | collective-permute-done | bytes 32800 | tf_op jit(solution)/shard_map/ppermute | solution.py:19
  77.5 0.9 %collective-permute-done.28 = bf16[64,256]{1,0:T(8,128)(2,1)S(1)} collective-permute-done((bf16[64,256]{1,0:T(8,128)(2,1)S(1)}, bf16[64,256]{1,0:T(8,128)(2,1)S(1)}, u32[]{:S(2)}, u32[]{:S(2)}) %collective-permute-start.28) | collective-permute-done | bytes 32800 | tf_op jit(solution)/shard_map/ppermute | solution.py:19
  (39 shorter events, 3.9 us)
Async XLA Ops:
  1.4 10.7 %collective-permute-start.12 = (bf16[80,1152]{1,0:T(8,128)(2,1)S(1)}, bf16[80,1152]{1,0:T(8,128)(2,1)S(1)}, u32[]{:S(2)}, u32[]{:S(2)}) collective-permute-start(bf16[80,1152]{1,0:T(8,128)(2,1)S(1)} %get-tuple-element.15), channel_id=1, source_target_pairs={{0,4},{4,8},{8,12},{12,0},{1,5},{5,9},{9,13},{13,1},{2,6},{6,10},{... | collective-permute-start | bytes 552968 | tf_op jit(solution)/shard_map/ppermute | solution.py:19
  4.5 14.7 %collective-permute-start.16 = (bf16[80,1152]{1,0:T(8,128)(2,1)S(1)}, bf16[80,1152]{1,0:T(8,128)(2,1)S(1)}, u32[]{:S(2)}, u32[]{:S(2)}) collective-permute-start(bf16[80,1152]{1,0:T(8,128)(2,1)S(1)} %get-tuple-element.16), channel_id=1, source_target_pairs={{0,8},{4,12},{8,0},{12,4},{1,9},{5,13},{9,1},{13,5},{2,10},{6,14},... | collective-permute-start | bytes 552968 | tf_op jit(solution)/shard_map/ppermute | solution.py:19
  7.1 16.6 %collective-permute-start = (bf16[528,256]{1,0:T(8,128)(2,1)S(1)}, bf16[528,256]{1,0:T(8,128)(2,1)S(1)}, u32[]{:S(2)}, u32[]{:S(2)}) collective-permute-start(bf16[528,256]{1,0:T(8,128)(2,1)S(1)} %get-tuple-element.13.refs_0_), channel_id=1, source_target_pairs={{0,4},{4,8},{8,12},{1,5},{5,9},{9,13},{2,6},{6,10},{10,14},{3,7},{... | collective-permute-start | bytes 811016 | tf_op jit(solution)/shard_map/ppermute | solution.py:314
  9.1 15.1 %collective-permute-start.7 = (bf16[128,1152]{1,0:T(8,128)(2,1)S(1)}, bf16[128,1152]{1,0:T(8,128)(2,1)S(1)}, u32[]{:S(2)}, u32[]{:S(2)}) collective-permute-start(bf16[128,1152]{1,0:T(8,128)(2,1)S(1)} %get-tuple-element.14.own.refs_0_), channel_id=1, source_target_pairs={{0,2},{1,3},{2,0},{3,1},{4,6},{5,7},{6,4},{7,5},{8,10},{9,11},{10,... | collective-permute-start | bytes 884744 | tf_op jit(solution)/shard_map/ppermute | solution.py:24
  10.8 20.1 %collective-permute-start.6 = (bf16[128,1152]{1,0:T(8,128)(2,1)S(1)}, bf16[128,1152]{1,0:T(8,128)(2,1)S(1)}, u32[]{:S(2)}, u32[]{:S(2)}) collective-permute-start(bf16[128,1152]{1,0:T(8,128)(2,1)S(1)} %get-tuple-element.14.own.refs_0_), channel_id=1, source_target_pairs={{0,1},{1,0},{2,3},{3,2},{4,5},{5,4},{6,7},{7,6},{8,9},{9,8},{10,11... | collective-permute-start | bytes 884744 | tf_op jit(solution)/shard_map/ppermute | solution.py:24
  12.1 43.3 %copy-start.1 = (bf16[8,1152,128]{2,1,0:T(8,128)(2,1)S(1)}, bf16[8,1152,128]{2,1,0:T(8,128)(2,1)}, u32[]{:S(2)}) copy-start(bf16[8,1152,128]{2,1,0:T(8,128)(2,1)} %refs_16_.1) | copy-start | bytes 7077892
  12.1 10.1 %collective-permute-start.20 = (bf16[80,1152]{1,0:T(8,128)(2,1)S(1)}, bf16[80,1152]{1,0:T(8,128)(2,1)S(1)}, u32[]{:S(2)}, u32[]{:S(2)}) collective-permute-start(bf16[80,1152]{1,0:T(8,128)(2,1)S(1)} %get-tuple-element.17), channel_id=1, source_target_pairs={{0,12},{4,0},{8,4},{12,8},{1,13},{5,1},{9,5},{13,9},{2,14},{6,2},{... | collective-permute-start | bytes 552968 | tf_op jit(solution)/shard_map/ppermute | solution.py:19
  19.2 10.2 %collective-permute-start.3 = (bf16[528,256]{1,0:T(8,128)(2,1)S(1)}, bf16[528,256]{1,0:T(8,128)(2,1)S(1)}, u32[]{:S(2)}, u32[]{:S(2)}) collective-permute-start(bf16[528,256]{1,0:T(8,128)(2,1)S(1)} %get-tuple-element.13.refs_0_), channel_id=1, source_target_pairs={{12,8},{8,4},{4,0},{13,9},{9,5},{5,1},{14,10},{10,6},{6,2},{15,11}... | collective-permute-start | bytes 811016 | tf_op jit(solution)/shard_map/ppermute | solution.py:315
  22.2 8.7 %collective-permute-start.14 = (bf16[80,1152]{1,0:T(8,128)(2,1)S(1)}, bf16[80,1152]{1,0:T(8,128)(2,1)S(1)}, u32[]{:S(2)}, u32[]{:S(2)}) collective-permute-start(bf16[80,1152]{1,0:T(8,128)(2,1)S(1)} %collective-permute-done.12.refs_4_), channel_id=1, source_target_pairs={{0,2},{1,3},{2,0},{3,1},{4,6},{5,7},{6,4},{7,5},{8,10},{9,11},{10,... | collective-permute-start | bytes 552968 | tf_op jit(solution)/shard_map/ppermute | solution.py:24
  23.7 8.6 %collective-permute-start.18 = (bf16[80,1152]{1,0:T(8,128)(2,1)S(1)}, bf16[80,1152]{1,0:T(8,128)(2,1)S(1)}, u32[]{:S(2)}, u32[]{:S(2)}) collective-permute-start(bf16[80,1152]{1,0:T(8,128)(2,1)S(1)} %collective-permute-done.16.refs_8_), channel_id=1, source_target_pairs={{0,2},{1,3},{2,0},{3,1},{4,6},{5,7},{6,4},{7,5},{8,10},{9,11},{10,... | collective-permute-start | bytes 552968 | tf_op jit(solution)/shard_map/ppermute | solution.py:24
  24.2 14.0 %collective-permute-start.8 = (bf16[128,1152]{1,0:T(8,128)(2,1)S(1)}, bf16[128,1152]{1,0:T(8,128)(2,1)S(1)}, u32[]{:S(2)}, u32[]{:S(2)}) collective-permute-start(bf16[128,1152]{1,0:T(8,128)(2,1)S(1)} %collective-permute-done.7.far.refs_2_), channel_id=1, source_target_pairs={{0,1},{1,0},{2,3},{3,2},{4,5},{5,4},{6,7},{7,6},{8,9},{9,8},{10,11... | collective-permute-start | bytes 884744 | tf_op jit(solution)/shard_map/ppermute | solution.py:24
  29.4 6.2 %collective-permute-start.22 = (bf16[80,1152]{1,0:T(8,128)(2,1)S(1)}, bf16[80,1152]{1,0:T(8,128)(2,1)S(1)}, u32[]{:S(2)}, u32[]{:S(2)}) collective-permute-start(bf16[80,1152]{1,0:T(8,128)(2,1)S(1)} %collective-permute-done.20.refs_12_), channel_id=1, source_target_pairs={{0,2},{1,3},{2,0},{3,1},{4,6},{5,7},{6,4},{7,5},{8,10},{9,11},{10,... | collective-permute-start | bytes 552968 | tf_op jit(solution)/shard_map/ppermute | solution.py:24
  30.9 5.4 %collective-permute-start.13 = (bf16[80,1152]{1,0:T(8,128)(2,1)S(1)}, bf16[80,1152]{1,0:T(8,128)(2,1)S(1)}, u32[]{:S(2)}, u32[]{:S(2)}) collective-permute-start(bf16[80,1152]{1,0:T(8,128)(2,1)S(1)} %collective-permute-done.12.refs_4_), channel_id=1, source_target_pairs={{0,1},{1,0},{2,3},{3,2},{4,5},{5,4},{6,7},{7,6},{8,9},{9,8},{10,11... | collective-permute-start | bytes 552968 | tf_op jit(solution)/shard_map/ppermute | solution.py:24
  30.9 6.7 %collective-permute-start.17 = (bf16[80,1152]{1,0:T(8,128)(2,1)S(1)}, bf16[80,1152]{1,0:T(8,128)(2,1)S(1)}, u32[]{:S(2)}, u32[]{:S(2)}) collective-permute-start(bf16[80,1152]{1,0:T(8,128)(2,1)S(1)} %collective-permute-done.16.refs_8_), channel_id=1, source_target_pairs={{0,1},{1,0},{2,3},{3,2},{4,5},{5,4},{6,7},{7,6},{8,9},{9,8},{10,11... | collective-permute-start | bytes 552968 | tf_op jit(solution)/shard_map/ppermute | solution.py:24
  32.3 5.4 %collective-permute-start.21 = (bf16[80,1152]{1,0:T(8,128)(2,1)S(1)}, bf16[80,1152]{1,0:T(8,128)(2,1)S(1)}, u32[]{:S(2)}, u32[]{:S(2)}) collective-permute-start(bf16[80,1152]{1,0:T(8,128)(2,1)S(1)} %collective-permute-done.20.refs_12_), channel_id=1, source_target_pairs={{0,1},{1,0},{2,3},{3,2},{4,5},{5,4},{6,7},{7,6},{8,9},{9,8},{10,11... | collective-permute-start | bytes 552968 | tf_op jit(solution)/shard_map/ppermute | solution.py:24
  35.6 5.4 %collective-permute-start.1 = (bf16[528,256]{1,0:T(8,128)(2,1)S(1)}, bf16[528,256]{1,0:T(8,128)(2,1)S(1)}, u32[]{:S(2)}, u32[]{:S(2)}) collective-permute-start(bf16[528,256]{1,0:T(8,128)(2,1)S(1)} %collective-permute-done.refs_1_), channel_id=1, source_target_pairs={{4,8},{8,12},{5,9},{9,13},{6,10},{10,14},{7,11},{11,15},{20,24},{2... | collective-permute-start | bytes 811016 | tf_op jit(solution)/shard_map/ppermute | solution.py:314
  36.3 12.7 %collective-permute-start.4 = (bf16[528,256]{1,0:T(8,128)(2,1)S(1)}, bf16[528,256]{1,0:T(8,128)(2,1)S(1)}, u32[]{:S(2)}, u32[]{:S(2)}) collective-permute-start(bf16[528,256]{1,0:T(8,128)(2,1)S(1)} %collective-permute-done.3.refs_4_), channel_id=1, source_target_pairs={{8,4},{4,0},{9,5},{5,1},{10,6},{6,2},{11,7},{7,3},{24,20},{20,16},... | collective-permute-start | bytes 811016 | tf_op jit(solution)/shard_map/ppermute | solution.py:315
  37.6 12.7 %collective-permute-start.15 = (bf16[80,1152]{1,0:T(8,128)(2,1)S(1)}, bf16[80,1152]{1,0:T(8,128)(2,1)S(1)}, u32[]{:S(2)}, u32[]{:S(2)}) collective-permute-start(bf16[80,1152]{1,0:T(8,128)(2,1)S(1)} %collective-permute-done.14.refs_6_), channel_id=1, source_target_pairs={{0,1},{1,0},{2,3},{3,2},{4,5},{5,4},{6,7},{7,6},{8,9},{9,8},{10,11... | collective-permute-start | bytes 552968 | tf_op jit(solution)/shard_map/ppermute | solution.py:24
  37.7 14.3 %collective-permute-start.19 = (bf16[80,1152]{1,0:T(8,128)(2,1)S(1)}, bf16[80,1152]{1,0:T(8,128)(2,1)S(1)}, u32[]{:S(2)}, u32[]{:S(2)}) collective-permute-start(bf16[80,1152]{1,0:T(8,128)(2,1)S(1)} %collective-permute-done.18.refs_10_), channel_id=1, source_target_pairs={{0,1},{1,0},{2,3},{3,2},{4,5},{5,4},{6,7},{7,6},{8,9},{9,8},{10,11... | collective-permute-start | bytes 552968 | tf_op jit(solution)/shard_map/ppermute | solution.py:24
  38.2 17.2 %collective-permute-start.23 = (bf16[80,1152]{1,0:T(8,128)(2,1)S(1)}, bf16[80,1152]{1,0:T(8,128)(2,1)S(1)}, u32[]{:S(2)}, u32[]{:S(2)}) collective-permute-start(bf16[80,1152]{1,0:T(8,128)(2,1)S(1)} %collective-permute-done.22.refs_14_), channel_id=1, source_target_pairs={{0,1},{1,0},{2,3},{3,2},{4,5},{5,4},{6,7},{7,6},{8,9},{9,8},{10,11... | collective-permute-start | bytes 552968 | tf_op jit(solution)/shard_map/ppermute | solution.py:24
  41.0 20.8 %copy-start = (s32[256]{0:T(256)S(1)}, s32[256]{0:T(256)}, u32[]{:S(2)}) copy-start(s32[256]{0:T(256)} %param.11) | copy-start | bytes 3076
  41.0 20.8 %collective-permute-start.2 = (bf16[528,256]{1,0:T(8,128)(2,1)S(1)}, bf16[528,256]{1,0:T(8,128)(2,1)S(1)}, u32[]{:S(2)}, u32[]{:S(2)}) collective-permute-start(bf16[528,256]{1,0:T(8,128)(2,1)S(1)} %collective-permute-done.1.refs_2_), channel_id=1, source_target_pairs={{8,12},{9,13},{10,14},{11,15},{24,28},{25,29},{26,30},{27,31}} | collective-permute-start | bytes 811016 | tf_op jit(solution)/shard_map/ppermute | solution.py:314
  49.0 12.8 %collective-permute-start.5 = (bf16[528,256]{1,0:T(8,128)(2,1)S(1)}, bf16[528,256]{1,0:T(8,128)(2,1)S(1)}, u32[]{:S(2)}, u32[]{:S(2)}) collective-permute-start(bf16[528,256]{1,0:T(8,128)(2,1)S(1)} %collective-permute-done.4.refs_5_), channel_id=1, source_target_pairs={{4,0},{5,1},{6,2},{7,3},{20,16},{21,17},{22,18},{23,19}} | collective-permute-start | bytes 811016 | tf_op jit(solution)/shard_map/ppermute | solution.py:315
  50.3 8.8 %collective-permute-start.10 = (bf16[64,512]{1,0:T(8,128)(2,1)S(1)}, bf16[64,512]{1,0:T(8,128)(2,1)S(1)}, u32[]{:S(2)}, u32[]{:S(2)}) collective-permute-start(bf16[64,512]{1,0:T(8,128)(2,1)S(1)} %shard_map.83.refs_7_), channel_id=1, source_target_pairs={{0,8},{4,12},{8,0},{12,4},{1,9},{5,13},{9,1},{13,5},{2,10},{6,14},... | collective-permute-start | bytes 196616 | tf_op jit(solution)/shard_map/ppermute | solution.py:19
  52.0 9.9 %collective-permute-start.11 = (bf16[64,512]{1,0:T(8,128)(2,1)S(1)}, bf16[64,512]{1,0:T(8,128)(2,1)S(1)}, u32[]{:S(2)}, u32[]{:S(2)}) collective-permute-start(bf16[64,512]{1,0:T(8,128)(2,1)S(1)} %shard_map.83.refs_7_), channel_id=1, source_target_pairs={{0,12},{4,0},{8,4},{12,8},{1,13},{5,1},{9,5},{13,9},{2,14},{6,2},{... | collective-permute-start | bytes 196616 | tf_op jit(solution)/shard_map/ppermute | solution.py:19
  55.4 6.4 %collective-permute-start.9 = (bf16[64,512]{1,0:T(8,128)(2,1)S(1)}, bf16[64,512]{1,0:T(8,128)(2,1)S(1)}, u32[]{:S(2)}, u32[]{:S(2)}) collective-permute-start(bf16[64,512]{1,0:T(8,128)(2,1)S(1)} %shard_map.83.refs_7_), channel_id=1, source_target_pairs={{0,4},{4,8},{8,12},{12,0},{1,5},{5,9},{9,13},{13,1},{2,6},{6,10},{... | collective-permute-start | bytes 196616 | tf_op jit(solution)/shard_map/ppermute | solution.py:19
  63.6 2.0 %collective-permute-start.24 = (f32[128,1024]{1,0:T(8,128)S(1)}, f32[128,1024]{1,0:T(8,128)S(1)}, u32[]{:S(2)}, u32[]{:S(2)}) collective-permute-start(f32[128,1024]{1,0:T(8,128)S(1)} %shard_map.86), channel_id=1, source_target_pairs={{0,1},{1,0},{2,3},{3,2},{4,5},{5,4},{6,7},{7,6},{8,9},{9,8},{10,11... | collective-permute-start | bytes 1572872 | tf_op jit(solution)/shard_map/ppermute | solution.py:24
  65.6 5.8 %collective-permute-start.25 = (bf16[64,1024]{1,0:T(8,128)(2,1)S(1)}, bf16[64,1024]{1,0:T(8,128)(2,1)S(1)}, u32[]{:S(2)}, u32[]{:S(2)}) collective-permute-start(bf16[64,1024]{1,0:T(8,128)(2,1)S(1)} %fusion), channel_id=1, source_target_pairs={{0,2},{1,3},{2,0},{3,1},{4,6},{5,7},{6,4},{7,5},{8,10},{9,11},{10,... | collective-permute-start | bytes 393224 | tf_op jit(solution)/shard_map/ppermute | solution.py:24
  71.4 4.0 %collective-permute-start.26 = (bf16[64,256]{1,0:T(8,128)(2,1)S(1)}, bf16[64,256]{1,0:T(8,128)(2,1)S(1)}, u32[]{:S(2)}, u32[]{:S(2)}) collective-permute-start(bf16[64,256]{1,0:T(8,128)(2,1)S(1)} %get-tuple-element.23), channel_id=1, source_target_pairs={{0,12},{4,0},{8,4},{12,8},{1,13},{5,1},{9,5},{13,9},{2,14},{6,2},{... | collective-permute-start | bytes 98312 | tf_op jit(solution)/shard_map/ppermute | solution.py:19
  72.7 4.8 %collective-permute-start.27 = (bf16[64,256]{1,0:T(8,128)(2,1)S(1)}, bf16[64,256]{1,0:T(8,128)(2,1)S(1)}, u32[]{:S(2)}, u32[]{:S(2)}) collective-permute-start(bf16[64,256]{1,0:T(8,128)(2,1)S(1)} %get-tuple-element.25), channel_id=1, source_target_pairs={{0,8},{4,12},{8,0},{12,4},{1,9},{5,13},{9,1},{13,5},{2,10},{6,14},... | collective-permute-start | bytes 98312 | tf_op jit(solution)/shard_map/ppermute | solution.py:19
  72.7 5.7 %collective-permute-start.28 = (bf16[64,256]{1,0:T(8,128)(2,1)S(1)}, bf16[64,256]{1,0:T(8,128)(2,1)S(1)}, u32[]{:S(2)}, u32[]{:S(2)}) collective-permute-start(bf16[64,256]{1,0:T(8,128)(2,1)S(1)} %get-tuple-element.24), channel_id=1, source_target_pairs={{0,4},{4,8},{8,12},{12,0},{1,5},{5,9},{9,13},{13,1},{2,6},{6,10},{... | collective-permute-start | bytes 98312 | tf_op jit(solution)/shard_map/ppermute | solution.py:19

commit v3 on v2

--- a/solution.py
+++ b/solution.py
@@ -54,12 +54,8 @@
     return jnp.concatenate([ref[first, rows, :], ref[first + 1, rows, :]], axis=-1)
 
 
-def origin_of(z, k):
-    return jnp.where(z >= k, z - k, z - k + 4)
-
-
 def source_row(z, k, block):
-    b = origin_of(z, k)
+    b = z ^ k
     return (b % 2) * (2 * block) + (b // 2) * block
 
 
@@ -84,7 +80,7 @@
 
     moves = [(attn, held), (spos, spots.at[0]), (tpos, spots.at[1]), (pattern, flags)]
     for k, out in enumerate((first, second, third), 1):
-        at = columns(jnp.where(z + k >= 4, z + k - 4, z + k))
+        at = columns(z ^ k)
         moves.append((targets.at[:, at], out.at[pl.ds(0, rows)]))
         moves.append((sources.at[:, at], out.at[pl.ds(rows, sub)]))
     moves.append((targets.at[:, columns(z)], own.at[pl.ds(0, rows)]))
@@ -181,87 +177,66 @@
         put(k, direct, slice(0, direct.shape[1]), got)
 
 
-def edges_kernel(heads, queries, flip, *refs):
-    home, right1, right2, right3, left1, left2, left3 = refs[:7]
-    blocks_of_values = refs[7:11]
-    reads, direct, spos, out, table, values = refs[11:]
+def scores_kernel(home, first, second, third, reads, out, values):
+    z = lax.axis_index("tgt")
+    block, width = home.shape
+    heads = out.shape[0]
+    dim = reads.shape[1] // heads
+    for k, ref in enumerate((home, first, second, third)):
+        values[aligned(source_row(z, k, block), block), :] = ref[...]
+    for group in range(width // dim):
+        turned = values[:, group * dim : (group + 1) * dim].astype(F32).T.astype(BF16)
+        for head in (2 * group, 2 * group + 1):
+            out[head] = jnp.dot(
+                reads[:, head * dim : (head + 1) * dim], turned, preferred_element_type=F32
+            )
+
+
+def edges_kernel(heads, queries, shown, home, first, second, third, scores, direct, spos, away, kept):
+    tables = (home, first, second, third)
     z, s = lax.axis_index("tgt"), lax.axis_index("src")
-    side = (s % 2) ^ flip
     sources = spos.shape[1]
     half = sources // 2
+    base = heads * queries
     block = sources // 4
+    core = s % 2
+    sides = (aligned((1 - core) * half, half), aligned(core * half, half))
     ordered = by_core(spos[...])
-    wide = 2 * (reads.shape[1] // heads)
-    dim = wide // 2
-    pairs = heads // 2
-    table[0] = home[...]
-    for k, (near, other) in enumerate(((right1, left3), (right2, left2), (right3, left1)), 1):
-
-        @pl.when(z >= k)
-        def _(k=k, near=near):
-            table[k] = near[...]
-
-        @pl.when(z < k)
-        def _(k=k, other=other):
-            table[k] = other[...]
-
-    for k in range(4):
-        values[aligned(source_row(z, k, block), block), :] = blocks_of_values[k][...]
-    lanes = aligned(side * half, half)
     grid_q = jnp.concatenate(
         [
-            lax.broadcasted_iota(jnp.int32, (queries, sources), 0) + origin_of(z, k) * queries
+            lax.broadcasted_iota(jnp.int32, (queries, sources), 0) + (z ^ k) * queries
             for k in range(4)
         ],
         axis=0,
     )
-    near = ordered[:, :half]
-    near = jnp.where(side == 0, near, ordered[:, half:])
-    picks = (grid_q[:, :half] == near).astype(F32).astype(BF16)
-    blank = jnp.zeros((dim, half), BF16)
-    scorers, tables = [], []
-    for pair in range(pairs):
-        turned = values[lanes, pair * dim : (pair + 1) * dim].astype(F32).T.astype(BF16)
-        scorers.append(
-            jnp.concatenate(
+    turned = jnp.concatenate([ordered[:, half:], ordered[:, :half]], axis=1)
+    picks = (grid_q == jnp.where(core == 0, turned, ordered)).astype(F32).astype(BF16)
+    for i, k in enumerate(shown):
+        tpos = tables[k][base : base + 16, :].astype(F32)[0:1].astype(jnp.int32)
+        hot = (grid_q == tpos).astype(F32).T.astype(BF16)
+        here = slice(k * sources, (k + 1) * sources)
+        same = jnp.dot(hot, picks, preferred_element_type=F32)
+        mixed = [
+            same[:, j * half : (j + 1) * half] * direct[here, lanes] for j, lanes in enumerate(sides)
+        ]
+        for h in range(heads):
+            table = jnp.concatenate(
                 [
-                    jnp.concatenate([turned, blank], axis=1),
-                    jnp.concatenate([blank, turned], axis=1),
-                ],
-                axis=0,
-            )
-        )
-        tables.append(
-            jnp.concatenate(
-                [
-                    jnp.concatenate(
-                        [table[k, h * queries : (h + 1) * queries, lanes] for k in range(4)], axis=0
-                    )
-                    for h in (2 * pair, 2 * pair + 1)
+                    jnp.concatenate([t[h * queries : (h + 1) * queries, lanes] for t in tables], axis=0)
+                    for lanes in sides
                 ],
                 axis=1,
             )
-        )
-    for k in range(4):
-        tpos = table[k, table.shape[1] - 16 : table.shape[1], :].astype(F32)[0:1].astype(jnp.int32)
-        hot = (grid_q == tpos).astype(F32).T.astype(BF16)
-        here = slice(k * sources, (k + 1) * sources)
-        running = None
-        for pair in range(pairs):
-            weights = jnp.dot(hot, tables[pair], preferred_element_type=F32)
-            scores = jnp.dot(
-                reads[here, pair * wide : (pair + 1) * wide],
-                scorers[pair],
-                preferred_element_type=F32,
-            )
-            term = weights * scores
-            running = term if running is None else running + term
-        mixed = running[:, :half] + running[:, half:]
-        same = jnp.dot(hot, picks, preferred_element_type=F32)
-        turned = (mixed + same * direct[here, lanes]).T
-        for x in range(2):
-            row = jnp.where(s // 2 == x, block, 0)
-            out[aligned(row, block), here] = turned[x * block : (x + 1) * block, :]
+            weights = jnp.dot(hot, table, preferred_element_type=F32)
+            for j, lanes in enumerate(sides):
+                mixed[j] = mixed[j] + weights[:, j * half : (j + 1) * half] * scores[h, here, lanes]
+        for out, value in zip((away, kept), mixed):
+            value = value.T
+            for x in range(2):
+                row = jnp.where(s // 2 == x, block, 0)
+                out[aligned(row, block), i * sources : (i + 1) * sources] = value[
+                    x * block : (x + 1) * block, :
+                ]
 
 
 def resident(
@@ -298,67 +273,65 @@
         ],
         hbm=(0, 1, 2, 3, 4, 5),
     )
-    own, far, core, cross = [cut[0]], [], [], []
-    for k in range(1, blocks):
-        own.append(passed_along(cut[k], "tgt", k))
-    for k in range(blocks):
-        far.append(swapped(own[k], "src", 2))
-        core.append(swapped(own[k], "src", 1))
-        cross.append(swapped(far[k], "src", 1))
-
-    home = cut[4]
-    rightward, leftward = [home], [home]
-    for step in range(1, blocks):
-        up = [(i, i + 1) for i in range(step - 1, blocks - 1)]
-        down = [(blocks - 1 - i, blocks - 2 - i) for i in range(step - 1, blocks - 1)]
-        rightward.append(lax.ppermute(rightward[-1], "tgt", up))
-        leftward.append(lax.ppermute(leftward[-1], "tgt", down))
-    values = [
-        kernel_call(
-            functools.partial(values_kernel, rows),
-            shape(block, groups * head_dim),
-            [own[0], core[0], far[0], cross[0], value_proj],
-            2 * block * depth * groups * head_dim,
-            value_proj.size * 2,
-            [pltpu.VMEM(value_proj.shape, BF16), pltpu.SemaphoreType.DMA((4,))],
-            hbm=(4,),
-        )
-    ]
-    for k in range(1, blocks):
-        values.append(passed_along(values[0], "tgt", k))
+
+    def doubled(value):
+        second = swapped(value, "tgt", 2)
+        return [value, swapped(value, "tgt", 1), second, swapped(second, "tgt", 1)]
+
+    own = [cut[0]] + [swapped(cut[k], "tgt", k) for k in range(1, blocks)]
+    far = [swapped(own[k], "src", 2) for k in range(blocks)]
+    core = [swapped(own[k], "src", 1) for k in range(blocks)]
+    cross = [swapped(far[k], "src", 1) for k in range(blocks)]
+    tables = doubled(cut[4])
+    values = kernel_call(
+        functools.partial(values_kernel, rows),
+        shape(block, groups * head_dim),
+        [own[0], core[0], far[0], cross[0], value_proj],
+        2 * block * depth * groups * head_dim,
+        value_proj.size * 2,
+        [pltpu.VMEM(value_proj.shape, BF16), pltpu.SemaphoreType.DMA((4,))],
+        hbm=(4,),
+    )
+    values = doubled(values)
 
     reads, direct = kernel_call(
         functools.partial(reads_kernel, rows),
-        (
-            shape(blocks * targets, heads * head_dim),
-            shape(blocks * targets, sources, dtype=F32),
-        ),
+        (shape(blocks * targets, heads * head_dim), shape(blocks * targets, sources, dtype=F32)),
         [a[k] for k in range(blocks) for a in (own, core, far, cross)] + [out_proj],
         2 * blocks * targets * part * (heads * head_dim + sources),
         out_proj.size * 2,
         [pltpu.VMEM((sources, part), BF16)],
     )
-
-    def edges(flip):
-        return kernel_call(
-            functools.partial(edges_kernel, heads, queries, flip),
-            shape(sources // 2, blocks * targets, dtype=F32),
-            [home, *rightward[1:], *leftward[1:], *values, reads, direct, spots],
-            2 * 2 * blocks * targets * sources * heads * head_dim,
+    scores = kernel_call(
+        scores_kernel,
+        shape(heads, blocks * targets, sources, dtype=F32),
+        [*values, reads],
+        2 * blocks * targets * sources * heads * head_dim,
+        1 << 22,
+        [pltpu.VMEM((sources, groups * head_dim), BF16)],
+    )
+
+    def edges(shown):
+        away, kept = kernel_call(
+            functools.partial(edges_kernel, heads, queries, shown),
+            (shape(2 * block, len(shown) * targets, dtype=F32),) * 2,
+            [*tables, scores, direct, spots],
+            len(shown) * targets * sources * sources * heads * 2,
             1 << 22,
-            [pltpu.VMEM((4,) + home.shape, BF16), pltpu.VMEM((sources, groups * head_dim), BF16)],
-        )
-
-    away = swapped(edges(1), "src", 1)
-    kept = edges(0)
-    back = swapped((kept[:block] + away[:block]).astype(BF16), "src", 2)
-    mine = kept[block:] + away[block:] + back.astype(F32)
-    parts = [mine[:, k * targets : (k + 1) * targets] for k in range(blocks)]
-    landed = [passed_along(parts[k].astype(BF16), "tgt", -k) for k in range(1, blocks)]
-    result = parts[0]
-    for value in landed:
-        result = result + value.astype(F32)
-    return (result * cut[5]).astype(BF16)
+        )
+        away = swapped(away, "src", 1)
+        back = swapped((kept[:block] + away[:block]).astype(BF16), "src", 2)
+        return kept[block:] + away[block:] + back.astype(F32)
+
+    distant = edges((2, 3))
+    closer = edges((0, 1))
+    second = swapped(distant[:, :targets].astype(BF16), "tgt", 2)
+    third = swapped(distant[:, targets:].astype(BF16), "tgt", 3)
+    first = swapped(closer[:, targets:].astype(BF16), "tgt", 1)
+    total = closer[:, :targets]
+    for value in (first, second, third):
+        total = total + value.astype(F32)
+    return (total * cut[5]).astype(BF16)
 
 
 def ring(

time: 79.2 us -> 87.6 us (1.11)
  waiting for transfers between devices: 37.6 us -> 49.8 us
  starting transfers between devices: 29.1 us -> 25.1 us
    ppermute x14 -> x28, waiting for transfers between devices: 9.72 us -> 49.8 us  [swapped(): return lax.ppermute(value, axis, pairs)]
    ppermute x15 -> x0, waiting for transfers between devices: 27.9 us -> none  [the longest x9 15.4 us: passed_along(): return lax.ppermute(value, axis, pairs)]
    ppermute x15 -> x0, starting transfers between devices: 22.2 us -> none  [the longest x9 15 us: passed_along(): return lax.ppermute(value, axis, pairs)]
    ppermute x14 -> x28, starting transfers between devices: 6.92 us -> 25.1 us  [swapped(): return lax.ppermute(value, axis, pairs)]
    pallas_call x5 -> x6, Pallas kernels: 11.3 us -> 11.6 us  [kernel_call(): pl.pallas_call(body, out_shape=outs, in_specs=[pl.BlockSpec(memory_space=...]
  transfers between devices with their start and end apart: 29 -> 28, of which waited for: 13 -> 13; matrix products, arithmetic and copies ran while one was open for 0% -> 0% of each run, Pallas kernels for 10% -> 10%
where the time goes in v3:
time: 87.6 us; the launch traced here: 87.4 us
  waiting for transfers between devices  49.8 us (57%)
  starting transfers between devices  25.1 us (29%)
  Pallas kernels  11.6 us (13%)
    ppermute x28, waiting for transfers between devices, swapped(): return lax.ppermute(value, axis, pairs)  49.8 us
    ppermute x28, starting transfers between devices, swapped(): return lax.ppermute(value, axis, pairs)  25.1 us
    pallas_call x6, Pallas kernels, kernel_call(): pl.pallas_call(body, out_shape=outs, in_specs=[pl.BlockSpec(memory_space=...  11.6 us
  transfers between devices with their start and end apart: 28, of which 13 were waited for; matrix products, arithmetic and copies ran while one was open for 0% of the time, Pallas kernels for 10%

profile of v3, /device:TPU:0, one launch (start us, length us, event | category | flops | bytes accessed | tf_op | source)
XLA Modules:
  0.0 87.4 jit_solution(18041438227861523727)
XLA Ops:
  0.0 1.6 %shard_map.82 = (bf16[128,1152]{1,0:T(8,128)(2,1)S(1)}, bf16[80,1152]{1,0:T(8,128)(2,1)S(1)}, bf16[80,1152]{1,0:T(8,128)(2,1)S(1)}, bf16[80,1152]{1,0:T(8,128)(2...) custom-call(bf16[64,4608]{1,0:T(8,128)(2,1)} %targets.1, bf16[16,4608]{1,0:T(8,128)(2,1)} %sources.1, ...), custom_call_target="tpu_custom_call" | custom-call | flops 67108864 | bytes 1179648 | tf_op jit(solution)/shard_map/pallas_call | solution.py:28
  1.6 3.0 %collective-permute-start.4 = (bf16[128,1152]{1,0:T(8,128)(2,1)S(1)}, bf16[128,1152]{1,0:T(8,128)(2,1)S(1)}, u32[]{:S(2)}, u32[]{:S(2)}) collective-permute-start(bf16[128,1152]{1,0:T(8,128)(2,1)S(1)} %get-tuple-element.18.own.refs_0_), channel_id=1, source_target_pairs={{0,2},{1,3},{2,0},{3,1},{4,6},{5,7},{6,4},{7,5},{8,10},{9,11},{10,... | collective-permute-start | bytes 884744 | tf_op jit(solution)/shard_map/ppermute | solution.py:24
  4.6 1.6 %collective-permute-start.9 = (bf16[80,1152]{1,0:T(8,128)(2,1)S(1)}, bf16[80,1152]{1,0:T(8,128)(2,1)S(1)}, u32[]{:S(2)}, u32[]{:S(2)}) collective-permute-start(bf16[80,1152]{1,0:T(8,128)(2,1)S(1)} %get-tuple-element.19), channel_id=1, source_target_pairs={{0,4},{4,0},{8,12},{12,8},{1,5},{5,1},{9,13},{13,9},{2,6},{6,2},{1... | collective-permute-start | bytes 552968 | tf_op jit(solution)/shard_map/ppermute | solution.py:24
  6.2 2.6 %collective-permute-start.1 = (bf16[528,256]{1,0:T(8,128)(2,1)S(1)}, bf16[528,256]{1,0:T(8,128)(2,1)S(1)}, u32[]{:S(2)}, u32[]{:S(2)}) collective-permute-start(bf16[528,256]{1,0:T(8,128)(2,1)S(1)} %get-tuple-element.17.home), channel_id=1, source_target_pairs={{0,8},{4,12},{8,0},{12,4},{1,9},{5,13},{9,1},{13,5},{2,10},{6,14},... | collective-permute-start | bytes 811016 | tf_op jit(solution)/shard_map/ppermute | solution.py:24
  9.1 3.1 %collective-permute-done.9.refs_4_ = bf16[80,1152]{1,0:T(8,128)(2,1)S(1)} collective-permute-done((bf16[80,1152]{1,0:T(8,128)(2,1)S(1)}, bf16[80,1152]{1,0:T(8,128)(2,1)S(1)}, u32[]{:S(2)}, u32[]{:S(2)}) %collective-permute-start.9) | collective-permute-done | bytes 184352 | tf_op jit(solution)/shard_map/ppermute | solution.py:24
  12.2 3.4 %collective-permute-start.17 = (bf16[80,1152]{1,0:T(8,128)(2,1)S(1)}, bf16[80,1152]{1,0:T(8,128)(2,1)S(1)}, u32[]{:S(2)}, u32[]{:S(2)}) collective-permute-start(bf16[80,1152]{1,0:T(8,128)(2,1)S(1)} %get-tuple-element.21), channel_id=1, source_target_pairs={{0,12},{4,8},{8,4},{12,0},{1,13},{5,9},{9,5},{13,1},{2,14},{6,10},... | collective-permute-start | bytes 552968 | tf_op jit(solution)/shard_map/ppermute | solution.py:24
  15.7 18.5 %collective-permute-done.13.refs_8_ = bf16[80,1152]{1,0:T(8,128)(2,1)S(1)} collective-permute-done((bf16[80,1152]{1,0:T(8,128)(2,1)S(1)}, bf16[80,1152]{1,0:T(8,128)(2,1)S(1)}, u32[]{:S(2)}, u32[]{:S(2)}) %collective-permute-start.13) | collective-permute-done | bytes 184352 | tf_op jit(solution)/shard_map/ppermute | solution.py:24
  34.7 1.5 %collective-permute-start.15 = (bf16[80,1152]{1,0:T(8,128)(2,1)S(1)}, bf16[80,1152]{1,0:T(8,128)(2,1)S(1)}, u32[]{:S(2)}, u32[]{:S(2)}) collective-permute-start(bf16[80,1152]{1,0:T(8,128)(2,1)S(1)} %collective-permute-done.13.refs_8_), channel_id=1, source_target_pairs={{0,2},{1,3},{2,0},{3,1},{4,6},{5,7},{6,4},{7,5},{8,10},{9,11},{10,... | collective-permute-start | bytes 552968 | tf_op jit(solution)/shard_map/ppermute | solution.py:24
  36.7 4.9 %collective-permute-done.11.refs_6_ = bf16[80,1152]{1,0:T(8,128)(2,1)S(1)} collective-permute-done((bf16[80,1152]{1,0:T(8,128)(2,1)S(1)}, bf16[80,1152]{1,0:T(8,128)(2,1)S(1)}, u32[]{:S(2)}, u32[]{:S(2)}) %collective-permute-start.11) | collective-permute-done | bytes 184352 | tf_op jit(solution)/shard_map/ppermute | solution.py:24
  41.6 3.9 %collective-permute-done.15.refs_10_ = bf16[80,1152]{1,0:T(8,128)(2,1)S(1)} collective-permute-done((bf16[80,1152]{1,0:T(8,128)(2,1)S(1)}, bf16[80,1152]{1,0:T(8,128)(2,1)S(1)}, u32[]{:S(2)}, u32[]{:S(2)}) %collective-permute-start.15) | collective-permute-done | bytes 184352 | tf_op jit(solution)/shard_map/ppermute | solution.py:24
  45.6 2.2 %collective-permute-done.19.refs_14_ = bf16[80,1152]{1,0:T(8,128)(2,1)S(1)} collective-permute-done((bf16[80,1152]{1,0:T(8,128)(2,1)S(1)}, bf16[80,1152]{1,0:T(8,128)(2,1)S(1)}, u32[]{:S(2)}, u32[]{:S(2)}) %collective-permute-start.19) | collective-permute-done | bytes 184352 | tf_op jit(solution)/shard_map/ppermute | solution.py:24
  48.3 2.7 %shard_map.83.home = bf16[64,512]{1,0:T(8,128)(2,1)S(1)} custom-call(bf16[128,1152]{1,0:T(8,128)(2,1)S(1)} %get-tuple-element.18.own.refs_0_, bf16[128,1152]{1,0:T(8,128)(2,1)S(1)} %collective-permute-done.3.core.refs_1_, bf16[128,1152]{1,0:T(8,128)(2,1)S(1)} %collective-permute-done.4.far.refs_2_, ...), custom_call_target="tpu_custom_call" | custom-call | flops 301989888 | bytes 4718592 | tf_op jit(solution)/shard_map/pallas_call | solution.py:28
  51.1 1.6 %collective-permute-start.7 = (bf16[64,512]{1,0:T(8,128)(2,1)S(1)}, bf16[64,512]{1,0:T(8,128)(2,1)S(1)}, u32[]{:S(2)}, u32[]{:S(2)}) collective-permute-start(bf16[64,512]{1,0:T(8,128)(2,1)S(1)} %shard_map.83.home), channel_id=1, source_target_pairs={{0,8},{4,12},{8,0},{12,4},{1,9},{5,13},{9,1},{13,5},{2,10},{6,14},... | collective-permute-start | bytes 196616 | tf_op jit(solution)/shard_map/ppermute | solution.py:24
  52.7 1.5 %collective-permute-start = (bf16[528,256]{1,0:T(8,128)(2,1)S(1)}, bf16[528,256]{1,0:T(8,128)(2,1)S(1)}, u32[]{:S(2)}, u32[]{:S(2)}) collective-permute-start(bf16[528,256]{1,0:T(8,128)(2,1)S(1)} %get-tuple-element.17.home), channel_id=1, source_target_pairs={{0,4},{4,0},{8,12},{12,8},{1,5},{5,1},{9,13},{13,9},{2,6},{6,2},{1... | collective-permute-start | bytes 811016 | tf_op jit(solution)/shard_map/ppermute | solution.py:24
  54.7 1.5 %collective-permute-start.6 = (bf16[64,512]{1,0:T(8,128)(2,1)S(1)}, bf16[64,512]{1,0:T(8,128)(2,1)S(1)}, u32[]{:S(2)}, u32[]{:S(2)}) collective-permute-start(bf16[64,512]{1,0:T(8,128)(2,1)S(1)} %shard_map.83.home), channel_id=1, source_target_pairs={{0,4},{4,0},{8,12},{12,8},{1,5},{5,1},{9,13},{13,9},{2,6},{6,2},{1... | collective-permute-start | bytes 196616 | tf_op jit(solution)/shard_map/ppermute | solution.py:24
  56.2 1.8 %collective-permute-done.7.second = bf16[64,512]{1,0:T(8,128)(2,1)S(1)} collective-permute-done((bf16[64,512]{1,0:T(8,128)(2,1)S(1)}, bf16[64,512]{1,0:T(8,128)(2,1)S(1)}, u32[]{:S(2)}, u32[]{:S(2)}) %collective-permute-start.7) | collective-permute-done | bytes 65568 | tf_op jit(solution)/shard_map/ppermute | solution.py:24
  58.0 3.8 %shard_map.84 = (bf16[1024,1024]{1,0:T(8,128)(2,1)S(1)}, f32[1024,256]{1,0:T(8,128)S(1)}) custom-call(bf16[128,1152]{1,0:T(8,128)(2,1)S(1)} %get-tuple-element.18.own.refs_0_, bf16[128,1152]{1,0:T(8,128)(2,1)S(1)} %collective-permute-done.3.core.refs_1_, bf16[128,1152]{1,0:T(8,128)(2,1)S(1)} %collective-permute-done.4.far.refs_2_, ...), custom_call_target="tpu_custom_call" | custom-call | flops 3019898880 | bytes 2359296 | tf_op jit(solution)/shard_map/pallas_call | solution.py:28
  61.8 8.7 %collective-permute-done.6.first = bf16[64,512]{1,0:T(8,128)(2,1)S(1)} collective-permute-done((bf16[64,512]{1,0:T(8,128)(2,1)S(1)}, bf16[64,512]{1,0:T(8,128)(2,1)S(1)}, u32[]{:S(2)}, u32[]{:S(2)}) %collective-permute-start.6) | collective-permute-done | bytes 65568 | tf_op jit(solution)/shard_map/ppermute | solution.py:24
  70.5 0.7 collective-permute-done.8.third
  71.2 1.4 %shard_map.85.scores = f32[8,1024,256]{2,1,0:T(8,128)S(1)} custom-call(bf16[64,512]{1,0:T(8,128)(2,1)S(1)} %shard_map.83.home, bf16[64,512]{1,0:T(8,128)(2,1)S(1)} %collective-permute-done.6.first, bf16[64,512]{1,0:T(8,128)(2,1)S(1)} %collective-permute-done.7.second, bf16[64,512]{1,0:T(8,128)(2,1)S(1)} %collective-permute-done.8.third, ...), custom_call_target="tpu_custom_call" | custom-call | flops 536870912 | bytes 4194304 | tf_op jit(solution)/shard_map/pallas_call | solution.py:28
  72.5 1.1 %shard_map.87 = (f32[128,512]{1,0:T(8,128)S(1)}, f32[128,512]{1,0:T(8,128)S(1)}) custom-call(bf16[528,256]{1,0:T(8,128)(2,1)S(1)} %get-tuple-element.17.home, bf16[528,256]{1,0:T(8,128)(2,1)S(1)} %collective-permute-done.first, bf16[528,256]{1,0:T(8,128)(2,1)S(1)} %collective-permute-done.1.second, bf16[528,256]{1,0:T(8,128)(2,1)S(1)} %collective-permute-done.2.third, ...), custom_call_target="tpu_custom_call" | custom-call | flops 536870912 | bytes 4194304 | tf_op jit(solution)/shard_map/pallas_call | solution.py:28
  73.7 1.1 %shard_map.86 = (f32[128,512]{1,0:T(8,128)S(1)}, f32[128,512]{1,0:T(8,128)S(1)}) custom-call(bf16[528,256]{1,0:T(8,128)(2,1)S(1)} %get-tuple-element.17.home, bf16[528,256]{1,0:T(8,128)(2,1)S(1)} %collective-permute-done.first, bf16[528,256]{1,0:T(8,128)(2,1)S(1)} %collective-permute-done.1.second, bf16[528,256]{1,0:T(8,128)(2,1)S(1)} %collective-permute-done.2.third, ...), custom_call_target="tpu_custom_call" | custom-call | flops 536870912 | bytes 4194304 | tf_op jit(solution)/shard_map/pallas_call | solution.py:28
  74.9 0.6 collective-permute-start.21
  75.4 0.6 collective-permute-start.25
  76.6 1.0 %collective-permute-start.22 = (bf16[64,512]{1,0:T(8,128)(2,1)S(1)}, bf16[64,512]{1,0:T(8,128)(2,1)S(1)}, u32[]{:S(2)}, u32[]{:S(2)}) collective-permute-start(bf16[64,512]{1,0:T(8,128)(2,1)S(1)} %fusion.3), channel_id=1, source_target_pairs={{0,2},{1,3},{2,0},{3,1},{4,6},{5,7},{6,4},{7,5},{8,10},{9,11},{10,... | collective-permute-start | bytes 196616 | tf_op jit(solution)/shard_map/ppermute | solution.py:24
  77.6 2.3 %collective-permute-done.25 = bf16[64,512]{1,0:T(8,128)(2,1)S(1)} collective-permute-done((bf16[64,512]{1,0:T(8,128)(2,1)S(1)}, bf16[64,512]{1,0:T(8,128)(2,1)S(1)}, u32[]{:S(2)}, u32[]{:S(2)}) %collective-permute-start.25) | collective-permute-done | bytes 65568 | tf_op jit(solution)/shard_map/ppermute | solution.py:24
  80.3 2.4 %collective-permute-start.27 = (bf16[64,256]{1,0:T(8,128)(2,1)S(1)}, bf16[64,256]{1,0:T(8,128)(2,1)S(1)}, u32[]{:S(2)}, u32[]{:S(2)}) collective-permute-start(bf16[64,256]{1,0:T(8,128)(2,1)S(1)} %get-tuple-element.30), channel_id=1, source_target_pairs={{0,12},{4,8},{8,4},{12,0},{1,13},{5,9},{9,5},{13,1},{2,14},{6,10},... | collective-permute-start | bytes 98312 | tf_op jit(solution)/shard_map/ppermute | solution.py:24
  82.8 0.8 collective-permute-start.23
  83.6 1.4 %collective-permute-done.26 = bf16[64,256]{1,0:T(8,128)(2,1)S(1)} collective-permute-done((bf16[64,256]{1,0:T(8,128)(2,1)S(1)}, bf16[64,256]{1,0:T(8,128)(2,1)S(1)}, u32[]{:S(2)}, u32[]{:S(2)}) %collective-permute-start.26) | collective-permute-done | bytes 32800 | tf_op jit(solution)/shard_map/ppermute | solution.py:24
  85.0 1.1 %collective-permute-done.27 = bf16[64,256]{1,0:T(8,128)(2,1)S(1)} collective-permute-done((bf16[64,256]{1,0:T(8,128)(2,1)S(1)}, bf16[64,256]{1,0:T(8,128)(2,1)S(1)}, u32[]{:S(2)}, u32[]{:S(2)}) %collective-permute-start.27) | collective-permute-done | bytes 32800 | tf_op jit(solution)/shard_map/ppermute | solution.py:24
  86.1 0.7 collective-permute-done.23
  86.8 0.6 fusion.8
  (41 shorter events, 3.7 us)
Async XLA Ops:
  0.0 58.0 %copy-start.1 = (bf16[8,1152,128]{2,1,0:T(8,128)(2,1)S(1)}, bf16[8,1152,128]{2,1,0:T(8,128)(2,1)}, u32[]{:S(2)}) copy-start(bf16[8,1152,128]{2,1,0:T(8,128)(2,1)} %refs_16_.1) | copy-start | bytes 7077892
  1.6 14.1 %collective-permute-start.4 = (bf16[128,1152]{1,0:T(8,128)(2,1)S(1)}, bf16[128,1152]{1,0:T(8,128)(2,1)S(1)}, u32[]{:S(2)}, u32[]{:S(2)}) collective-permute-start(bf16[128,1152]{1,0:T(8,128)(2,1)S(1)} %get-tuple-element.18.own.refs_0_), channel_id=1, source_target_pairs={{0,2},{1,3},{2,0},{3,1},{4,6},{5,7},{6,4},{7,5},{8,10},{9,11},{10,... | collective-permute-start | bytes 884744 | tf_op jit(solution)/shard_map/ppermute | solution.py:24
  4.6 7.6 %collective-permute-start.9 = (bf16[80,1152]{1,0:T(8,128)(2,1)S(1)}, bf16[80,1152]{1,0:T(8,128)(2,1)S(1)}, u32[]{:S(2)}, u32[]{:S(2)}) collective-permute-start(bf16[80,1152]{1,0:T(8,128)(2,1)S(1)} %get-tuple-element.19), channel_id=1, source_target_pairs={{0,4},{4,0},{8,12},{12,8},{1,5},{5,1},{9,13},{13,9},{2,6},{6,2},{1... | collective-permute-start | bytes 552968 | tf_op jit(solution)/shard_map/ppermute | solution.py:24
  6.2 30.5 %collective-permute-start.3 = (bf16[128,1152]{1,0:T(8,128)(2,1)S(1)}, bf16[128,1152]{1,0:T(8,128)(2,1)S(1)}, u32[]{:S(2)}, u32[]{:S(2)}) collective-permute-start(bf16[128,1152]{1,0:T(8,128)(2,1)S(1)} %get-tuple-element.18.own.refs_0_), channel_id=1, source_target_pairs={{0,1},{1,0},{2,3},{3,2},{4,5},{5,4},{6,7},{7,6},{8,9},{9,8},{10,11... | collective-permute-start | bytes 884744 | tf_op jit(solution)/shard_map/ppermute | solution.py:24
  6.2 30.0 %collective-permute-start.1 = (bf16[528,256]{1,0:T(8,128)(2,1)S(1)}, bf16[528,256]{1,0:T(8,128)(2,1)S(1)}, u32[]{:S(2)}, u32[]{:S(2)}) collective-permute-start(bf16[528,256]{1,0:T(8,128)(2,1)S(1)} %get-tuple-element.17.home), channel_id=1, source_target_pairs={{0,8},{4,12},{8,0},{12,4},{1,9},{5,13},{9,1},{13,5},{2,10},{6,14},... | collective-permute-start | bytes 811016 | tf_op jit(solution)/shard_map/ppermute | solution.py:24
  8.8 25.4 %collective-permute-start.13 = (bf16[80,1152]{1,0:T(8,128)(2,1)S(1)}, bf16[80,1152]{1,0:T(8,128)(2,1)S(1)}, u32[]{:S(2)}, u32[]{:S(2)}) collective-permute-start(bf16[80,1152]{1,0:T(8,128)(2,1)S(1)} %get-tuple-element.20), channel_id=1, source_target_pairs={{0,8},{4,12},{8,0},{12,4},{1,9},{5,13},{9,1},{13,5},{2,10},{6,14},... | collective-permute-start | bytes 552968 | tf_op jit(solution)/shard_map/ppermute | solution.py:24
  12.2 22.4 %collective-permute-start.17 = (bf16[80,1152]{1,0:T(8,128)(2,1)S(1)}, bf16[80,1152]{1,0:T(8,128)(2,1)S(1)}, u32[]{:S(2)}, u32[]{:S(2)}) collective-permute-start(bf16[80,1152]{1,0:T(8,128)(2,1)S(1)} %get-tuple-element.21), channel_id=1, source_target_pairs={{0,12},{4,8},{8,4},{12,0},{1,13},{5,9},{9,5},{13,1},{2,14},{6,10},... | collective-permute-start | bytes 552968 | tf_op jit(solution)/shard_map/ppermute | solution.py:24
  15.7 32.6 %collective-permute-start.5 = (bf16[128,1152]{1,0:T(8,128)(2,1)S(1)}, bf16[128,1152]{1,0:T(8,128)(2,1)S(1)}, u32[]{:S(2)}, u32[]{:S(2)}) collective-permute-start(bf16[128,1152]{1,0:T(8,128)(2,1)S(1)} %collective-permute-done.4.far.refs_2_), channel_id=1, source_target_pairs={{0,1},{1,0},{2,3},{3,2},{4,5},{5,4},{6,7},{7,6},{8,9},{9,8},{10,11... | collective-permute-start | bytes 884744 | tf_op jit(solution)/shard_map/ppermute | solution.py:24
  34.1 7.5 %collective-permute-start.11 = (bf16[80,1152]{1,0:T(8,128)(2,1)S(1)}, bf16[80,1152]{1,0:T(8,128)(2,1)S(1)}, u32[]{:S(2)}, u32[]{:S(2)}) collective-permute-start(bf16[80,1152]{1,0:T(8,128)(2,1)S(1)} %collective-permute-done.9.refs_4_), channel_id=1, source_target_pairs={{0,2},{1,3},{2,0},{3,1},{4,6},{5,7},{6,4},{7,5},{8,10},{9,11},{10,... | collective-permute-start | bytes 552968 | tf_op jit(solution)/shard_map/ppermute | solution.py:24
  34.7 10.9 %collective-permute-start.15 = (bf16[80,1152]{1,0:T(8,128)(2,1)S(1)}, bf16[80,1152]{1,0:T(8,128)(2,1)S(1)}, u32[]{:S(2)}, u32[]{:S(2)}) collective-permute-start(bf16[80,1152]{1,0:T(8,128)(2,1)S(1)} %collective-permute-done.13.refs_8_), channel_id=1, source_target_pairs={{0,2},{1,3},{2,0},{3,1},{4,6},{5,7},{6,4},{7,5},{8,10},{9,11},{10,... | collective-permute-start | bytes 552968 | tf_op jit(solution)/shard_map/ppermute | solution.py:24
  36.2 11.6 %collective-permute-start.19 = (bf16[80,1152]{1,0:T(8,128)(2,1)S(1)}, bf16[80,1152]{1,0:T(8,128)(2,1)S(1)}, u32[]{:S(2)}, u32[]{:S(2)}) collective-permute-start(bf16[80,1152]{1,0:T(8,128)(2,1)S(1)} %collective-permute-done.17.refs_12_), channel_id=1, source_target_pairs={{0,2},{1,3},{2,0},{3,1},{4,6},{5,7},{6,4},{7,5},{8,10},{9,11},{10,... | collective-permute-start | bytes 552968 | tf_op jit(solution)/shard_map/ppermute | solution.py:24
  36.7 11.1 %collective-permute-start.10 = (bf16[80,1152]{1,0:T(8,128)(2,1)S(1)}, bf16[80,1152]{1,0:T(8,128)(2,1)S(1)}, u32[]{:S(2)}, u32[]{:S(2)}) collective-permute-start(bf16[80,1152]{1,0:T(8,128)(2,1)S(1)} %collective-permute-done.9.refs_4_), channel_id=1, source_target_pairs={{0,1},{1,0},{2,3},{3,2},{4,5},{5,4},{6,7},{7,6},{8,9},{9,8},{10,11... | collective-permute-start | bytes 552968 | tf_op jit(solution)/shard_map/ppermute | solution.py:24
  41.6 9.4 %collective-permute-start.14 = (bf16[80,1152]{1,0:T(8,128)(2,1)S(1)}, bf16[80,1152]{1,0:T(8,128)(2,1)S(1)}, u32[]{:S(2)}, u32[]{:S(2)}) collective-permute-start(bf16[80,1152]{1,0:T(8,128)(2,1)S(1)} %collective-permute-done.13.refs_8_), channel_id=1, source_target_pairs={{0,1},{1,0},{2,3},{3,2},{4,5},{5,4},{6,7},{7,6},{8,9},{9,8},{10,11... | collective-permute-start | bytes 552968 | tf_op jit(solution)/shard_map/ppermute | solution.py:24
  45.6 7.1 %collective-permute-start.18 = (bf16[80,1152]{1,0:T(8,128)(2,1)S(1)}, bf16[80,1152]{1,0:T(8,128)(2,1)S(1)}, u32[]{:S(2)}, u32[]{:S(2)}) collective-permute-start(bf16[80,1152]{1,0:T(8,128)(2,1)S(1)} %collective-permute-done.17.refs_12_), channel_id=1, source_target_pairs={{0,1},{1,0},{2,3},{3,2},{4,5},{5,4},{6,7},{7,6},{8,9},{9,8},{10,11... | collective-permute-start | bytes 552968 | tf_op jit(solution)/shard_map/ppermute | solution.py:24
  47.8 6.4 %collective-permute-start.12 = (bf16[80,1152]{1,0:T(8,128)(2,1)S(1)}, bf16[80,1152]{1,0:T(8,128)(2,1)S(1)}, u32[]{:S(2)}, u32[]{:S(2)}) collective-permute-start(bf16[80,1152]{1,0:T(8,128)(2,1)S(1)} %collective-permute-done.11.refs_6_), channel_id=1, source_target_pairs={{0,1},{1,0},{2,3},{3,2},{4,5},{5,4},{6,7},{7,6},{8,9},{9,8},{10,11... | collective-permute-start | bytes 552968 | tf_op jit(solution)/shard_map/ppermute | solution.py:24
  47.8 7.0 %collective-permute-start.16 = (bf16[80,1152]{1,0:T(8,128)(2,1)S(1)}, bf16[80,1152]{1,0:T(8,128)(2,1)S(1)}, u32[]{:S(2)}, u32[]{:S(2)}) collective-permute-start(bf16[80,1152]{1,0:T(8,128)(2,1)S(1)} %collective-permute-done.15.refs_10_), channel_id=1, source_target_pairs={{0,1},{1,0},{2,3},{3,2},{4,5},{5,4},{6,7},{7,6},{8,9},{9,8},{10,11... | collective-permute-start | bytes 552968 | tf_op jit(solution)/shard_map/ppermute | solution.py:24
  48.3 9.7 %collective-permute-start.20 = (bf16[80,1152]{1,0:T(8,128)(2,1)S(1)}, bf16[80,1152]{1,0:T(8,128)(2,1)S(1)}, u32[]{:S(2)}, u32[]{:S(2)}) collective-permute-start(bf16[80,1152]{1,0:T(8,128)(2,1)S(1)} %collective-permute-done.19.refs_14_), channel_id=1, source_target_pairs={{0,1},{1,0},{2,3},{3,2},{4,5},{5,4},{6,7},{7,6},{8,9},{9,8},{10,11... | collective-permute-start | bytes 552968 | tf_op jit(solution)/shard_map/ppermute | solution.py:24
  51.1 6.9 %collective-permute-start.7 = (bf16[64,512]{1,0:T(8,128)(2,1)S(1)}, bf16[64,512]{1,0:T(8,128)(2,1)S(1)}, u32[]{:S(2)}, u32[]{:S(2)}) collective-permute-start(bf16[64,512]{1,0:T(8,128)(2,1)S(1)} %shard_map.83.home), channel_id=1, source_target_pairs={{0,8},{4,12},{8,0},{12,4},{1,9},{5,13},{9,1},{13,5},{2,10},{6,14},... | collective-permute-start | bytes 196616 | tf_op jit(solution)/shard_map/ppermute | solution.py:24
  52.7 19.8 %collective-permute-start = (bf16[528,256]{1,0:T(8,128)(2,1)S(1)}, bf16[528,256]{1,0:T(8,128)(2,1)S(1)}, u32[]{:S(2)}, u32[]{:S(2)}) collective-permute-start(bf16[528,256]{1,0:T(8,128)(2,1)S(1)} %get-tuple-element.17.home), channel_id=1, source_target_pairs={{0,4},{4,0},{8,12},{12,8},{1,5},{5,1},{9,13},{13,9},{2,6},{6,2},{1... | collective-permute-start | bytes 811016 | tf_op jit(solution)/shard_map/ppermute | solution.py:24
  54.2 18.4 %collective-permute-start.2 = (bf16[528,256]{1,0:T(8,128)(2,1)S(1)}, bf16[528,256]{1,0:T(8,128)(2,1)S(1)}, u32[]{:S(2)}, u32[]{:S(2)}) collective-permute-start(bf16[528,256]{1,0:T(8,128)(2,1)S(1)} %collective-permute-done.1.second), channel_id=1, source_target_pairs={{0,4},{4,0},{8,12},{12,8},{1,5},{5,1},{9,13},{13,9},{2,6},{6,2},{1... | collective-permute-start | bytes 811016 | tf_op jit(solution)/shard_map/ppermute | solution.py:24
  54.7 15.7 %collective-permute-start.6 = (bf16[64,512]{1,0:T(8,128)(2,1)S(1)}, bf16[64,512]{1,0:T(8,128)(2,1)S(1)}, u32[]{:S(2)}, u32[]{:S(2)}) collective-permute-start(bf16[64,512]{1,0:T(8,128)(2,1)S(1)} %shard_map.83.home), channel_id=1, source_target_pairs={{0,4},{4,0},{8,12},{12,8},{1,5},{5,1},{9,13},{13,9},{2,6},{6,2},{1... | collective-permute-start | bytes 196616 | tf_op jit(solution)/shard_map/ppermute | solution.py:24
  58.0 13.2 %collective-permute-start.8 = (bf16[64,512]{1,0:T(8,128)(2,1)S(1)}, bf16[64,512]{1,0:T(8,128)(2,1)S(1)}, u32[]{:S(2)}, u32[]{:S(2)}) collective-permute-start(bf16[64,512]{1,0:T(8,128)(2,1)S(1)} %collective-permute-done.7.second), channel_id=1, source_target_pairs={{0,4},{4,0},{8,12},{12,8},{1,5},{5,1},{9,13},{13,9},{2,6},{6,2},{1... | collective-permute-start | bytes 196616 | tf_op jit(solution)/shard_map/ppermute | solution.py:24
  71.2 1.4 %copy-start = (s32[256]{0:T(256)S(1)}, s32[256]{0:T(256)}, u32[]{:S(2)}) copy-start(s32[256]{0:T(256)} %param.11) | copy-start | bytes 3076
  73.7 1.8 %collective-permute-start.24 = (f32[128,512]{1,0:T(8,128)S(1)}, f32[128,512]{1,0:T(8,128)S(1)}, u32[]{:S(2)}, u32[]{:S(2)}) collective-permute-start(f32[128,512]{1,0:T(8,128)S(1)} %get-tuple-element.27), channel_id=1, source_target_pairs={{0,1},{1,0},{2,3},{3,2},{4,5},{5,4},{6,7},{7,6},{8,9},{9,8},{10,11... | collective-permute-start | bytes 786440 | tf_op jit(solution)/shard_map/ppermute | solution.py:24
  74.9 1.7 %collective-permute-start.21 = (f32[128,512]{1,0:T(8,128)S(1)}, f32[128,512]{1,0:T(8,128)S(1)}, u32[]{:S(2)}, u32[]{:S(2)}) collective-permute-start(f32[128,512]{1,0:T(8,128)S(1)} %get-tuple-element.25), channel_id=1, source_target_pairs={{0,1},{1,0},{2,3},{3,2},{4,5},{5,4},{6,7},{7,6},{8,9},{9,8},{10,11... | collective-permute-start | bytes 786440 | tf_op jit(solution)/shard_map/ppermute | solution.py:24
  75.4 4.5 %collective-permute-start.25 = (bf16[64,512]{1,0:T(8,128)(2,1)S(1)}, bf16[64,512]{1,0:T(8,128)(2,1)S(1)}, u32[]{:S(2)}, u32[]{:S(2)}) collective-permute-start(bf16[64,512]{1,0:T(8,128)(2,1)S(1)} %fusion), channel_id=1, source_target_pairs={{0,2},{1,3},{2,0},{3,1},{4,6},{5,7},{6,4},{7,5},{8,10},{9,11},{10,... | collective-permute-start | bytes 196616 | tf_op jit(solution)/shard_map/ppermute | solution.py:24
  76.6 6.2 %collective-permute-start.22 = (bf16[64,512]{1,0:T(8,128)(2,1)S(1)}, bf16[64,512]{1,0:T(8,128)(2,1)S(1)}, u32[]{:S(2)}, u32[]{:S(2)}) collective-permute-start(bf16[64,512]{1,0:T(8,128)(2,1)S(1)} %fusion.3), channel_id=1, source_target_pairs={{0,2},{1,3},{2,0},{3,1},{4,6},{5,7},{6,4},{7,5},{8,10},{9,11},{10,... | collective-permute-start | bytes 196616 | tf_op jit(solution)/shard_map/ppermute | solution.py:24
  80.0 5.0 %collective-permute-start.26 = (bf16[64,256]{1,0:T(8,128)(2,1)S(1)}, bf16[64,256]{1,0:T(8,128)(2,1)S(1)}, u32[]{:S(2)}, u32[]{:S(2)}) collective-permute-start(bf16[64,256]{1,0:T(8,128)(2,1)S(1)} %get-tuple-element.29), channel_id=1, source_target_pairs={{0,8},{4,12},{8,0},{12,4},{1,9},{5,13},{9,1},{13,5},{2,10},{6,14},... | collective-permute-start | bytes 98312 | tf_op jit(solution)/shard_map/ppermute | solution.py:24
  80.3 5.7 %collective-permute-start.27 = (bf16[64,256]{1,0:T(8,128)(2,1)S(1)}, bf16[64,256]{1,0:T(8,128)(2,1)S(1)}, u32[]{:S(2)}, u32[]{:S(2)}) collective-permute-start(bf16[64,256]{1,0:T(8,128)(2,1)S(1)} %get-tuple-element.30), channel_id=1, source_target_pairs={{0,12},{4,8},{8,4},{12,0},{1,13},{5,9},{9,5},{13,1},{2,14},{6,10},... | collective-permute-start | bytes 98312 | tf_op jit(solution)/shard_map/ppermute | solution.py:24
  82.8 4.0 %collective-permute-start.23 = (bf16[64,256]{1,0:T(8,128)(2,1)S(1)}, bf16[64,256]{1,0:T(8,128)(2,1)S(1)}, u32[]{:S(2)}, u32[]{:S(2)}) collective-permute-start(bf16[64,256]{1,0:T(8,128)(2,1)S(1)} %slice.87), channel_id=1, source_target_pairs={{0,4},{4,0},{8,12},{12,8},{1,5},{5,1},{9,13},{13,9},{2,6},{6,2},{1... | collective-permute-start | bytes 98312 | tf_op jit(solution)/shard_map/ppermute | solution.py:24

commit v4 on v3

--- a/solution.py
+++ b/solution.py
@@ -67,7 +67,7 @@
 
 
 def front_kernel(
-    targets, sources, attn, spos, tpos, pattern, own, first, second, third, table, kept, held, spots, flags, done
+    targets, sources, attn, spos, tpos, pattern, own, first, second, third, upper, lower, kept, held, spots, flags, done
 ):
     z = lax.axis_index("tgt")
     rows, sub = targets.shape[0], sources.shape[0]
@@ -93,11 +93,12 @@
         copy.wait()
     picks = lax.broadcasted_iota(jnp.int32, (keys, spos.shape[1]), 0) == by_core(spots[0])
     picks = picks.astype(F32).astype(BF16)
-    table[0:base, :] = jnp.dot(
-        held[...].reshape(base, keys), picks, preferred_element_type=F32
-    ).astype(BF16)
-    table[base:, :] = jnp.broadcast_to(
-        spots[1].astype(F32), (table.shape[0] - base, tpos.shape[1])
+    table = jnp.dot(held[...].reshape(base, keys), picks, preferred_element_type=F32).astype(BF16)
+    cut = lower.shape[0]
+    lower[...] = table[base - cut :]
+    upper[0 : base - cut, :] = table[: base - cut]
+    upper[base - cut :, :] = jnp.broadcast_to(
+        spots[1].astype(F32), (upper.shape[0] + cut - base, tpos.shape[1])
     ).astype(BF16)
     across = lax.broadcasted_iota(jnp.int32, pattern.shape, 0) == lax.axis_index("src")
     down = lax.broadcasted_iota(jnp.int32, pattern.shape, 1) == z
@@ -140,7 +141,33 @@
             ].astype(BF16)
 
 
-def reads_kernel(rows, *refs):
+def stacked(rows, pieces):
+    return jnp.concatenate([ref[0:rows, :] for ref in pieces], axis=0)
+
+
+def put(rows, target, start, cols, value):
+    s = lax.axis_index("src")
+    for j in range(4):
+        target[aligned(start + (s ^ j) * rows, rows), cols] = value[
+            j * rows : (j + 1) * rows
+        ].astype(target.dtype)
+
+
+def put_reads(rows, lefts, weight, reads):
+    width = 2 * weight.shape[2]
+    for pair in range(weight.shape[0] // 2):
+        right = pair_of(weight, 2 * pair)
+        for i, left in enumerate(lefts):
+            got = jnp.dot(left, right, preferred_element_type=F32)
+            put(rows, reads, 4 * i * rows, slice(pair * width, (pair + 1) * width), got)
+
+
+def near_kernel(rows, *refs):
+    pieces, weight, reads = refs[:8], refs[8], refs[9]
+    put_reads(rows, [stacked(rows, pieces[4 * i : 4 * i + 4]) for i in range(2)], weight, reads)
+
+
+def far_kernel(rows, *refs):
     pieces, weight, reads, direct, dec = refs[:16], refs[16], refs[17], refs[18], refs[19]
     z, s = lax.axis_index("tgt"), lax.axis_index("src")
     sub = pieces[4].shape[0] - rows
@@ -152,29 +179,13 @@
         else:
             piece = pieces[0][aligned(rows + sub * z, sub), :]
         dec[aligned(source_row(z, k, block) + sub * s, sub), :] = piece
-    width = 2 * weight.shape[2]
-    group = 4 * rows
-
-    def put(k, target, cols, value):
-        for j in range(4):
-            target[aligned(k * group + (s ^ j) * rows, rows), cols] = value[
-                j * rows : (j + 1) * rows
-            ].astype(target.dtype)
-
-    lefts = [
-        jnp.concatenate([ref[0:rows, :] for ref in pieces[4 * k : 4 * k + 4]], axis=0)
-        for k in range(4)
-    ]
-    for pair in range(weight.shape[0] // 2):
-        right = pair_of(weight, 2 * pair)
-        for k in range(4):
-            got = jnp.dot(lefts[k], right, preferred_element_type=F32)
-            put(k, reads, slice(pair * width, (pair + 1) * width), got)
+    lefts = [stacked(rows, pieces[4 * k : 4 * k + 4]) for k in range(4)]
+    put_reads(rows, lefts[2:], weight, reads)
     for k in range(4):
         got = lax.dot_general(
             lefts[k], dec[...], (((1,), (1,)), ((), ())), preferred_element_type=F32
         )
-        put(k, direct, slice(0, direct.shape[1]), got)
+        put(rows, direct, 4 * k * rows, slice(0, direct.shape[1]), got)
 
 
 def scores_kernel(home, first, second, third, reads, out, values):
@@ -192,12 +203,13 @@
             )
 
 
-def edges_kernel(heads, queries, shown, home, first, second, third, scores, direct, spos, away, kept):
-    tables = (home, first, second, third)
+def edges_kernel(heads, queries, shown, *refs):
+    uppers, lowers = refs[0:4], refs[4:8]
+    scores, direct, spos, away, kept = refs[8:]
     z, s = lax.axis_index("tgt"), lax.axis_index("src")
     sources = spos.shape[1]
     half = sources // 2
-    base = heads * queries
+    base = heads // 2 * queries
     block = sources // 4
     core = s % 2
     sides = (aligned((1 - core) * half, half), aligned(core * half, half))
@@ -212,24 +224,27 @@
     turned = jnp.concatenate([ordered[:, half:], ordered[:, :half]], axis=1)
     picks = (grid_q == jnp.where(core == 0, turned, ordered)).astype(F32).astype(BF16)
     for i, k in enumerate(shown):
-        tpos = tables[k][base : base + 16, :].astype(F32)[0:1].astype(jnp.int32)
+        tpos = uppers[k][base : base + 16, :].astype(F32)[0:1].astype(jnp.int32)
         hot = (grid_q == tpos).astype(F32).T.astype(BF16)
         here = slice(k * sources, (k + 1) * sources)
+        there = slice(i * sources, (i + 1) * sources)
         same = jnp.dot(hot, picks, preferred_element_type=F32)
         mixed = [
             same[:, j * half : (j + 1) * half] * direct[here, lanes] for j, lanes in enumerate(sides)
         ]
         for h in range(heads):
+            tables = uppers if h < heads // 2 else lowers
+            at = h % (heads // 2) * queries
             table = jnp.concatenate(
                 [
-                    jnp.concatenate([t[h * queries : (h + 1) * queries, lanes] for t in tables], axis=0)
+                    jnp.concatenate([t[at : at + queries, lanes] for t in tables], axis=0)
                     for lanes in sides
                 ],
                 axis=1,
             )
             weights = jnp.dot(hot, table, preferred_element_type=F32)
             for j, lanes in enumerate(sides):
-                mixed[j] = mixed[j] + weights[:, j * half : (j + 1) * half] * scores[h, here, lanes]
+                mixed[j] = mixed[j] + weights[:, j * half : (j + 1) * half] * scores[h, there, lanes]
         for out, value in zip((away, kept), mixed):
             value = value.T
             for x in range(2):
@@ -261,7 +276,11 @@
         front_kernel,
         (shape(rows + 4 * sub, part),)
         + (shape(rows + sub, part),) * 3
-        + (shape(heads * queries + 16, sources), shape(1, targets, dtype=F32)),
+        + (
+            shape(heads // 2 * queries + 16, sources),
+            shape(heads // 2 * queries, sources),
+            shape(1, targets, dtype=F32),
+        ),
         [target_rows, decoder_rows, attention, spots, target_pos[None, :], tile_pattern],
         2 * attention.size * sources,
         target_rows.size * 4,
@@ -282,7 +301,7 @@
     far = [swapped(own[k], "src", 2) for k in range(blocks)]
     core = [swapped(own[k], "src", 1) for k in range(blocks)]
     cross = [swapped(far[k], "src", 1) for k in range(blocks)]
-    tables = doubled(cut[4])
+    tables = doubled(cut[4]) + doubled(cut[5])
     values = kernel_call(
         functools.partial(values_kernel, rows),
         shape(block, groups * head_dim),
@@ -294,28 +313,41 @@
     )
     values = doubled(values)
 
-    reads, direct = kernel_call(
-        functools.partial(reads_kernel, rows),
-        (shape(blocks * targets, heads * head_dim), shape(blocks * targets, sources, dtype=F32)),
-        [a[k] for k in range(blocks) for a in (own, core, far, cross)] + [out_proj],
-        2 * blocks * targets * part * (heads * head_dim + sources),
+    groups_of = [a[k] for k in range(blocks) for a in (own, core, far, cross)]
+    wide = heads * head_dim
+    near = kernel_call(
+        functools.partial(near_kernel, rows),
+        shape(2 * targets, wide),
+        [*groups_of[:8], out_proj],
+        4 * targets * part * wide,
+        out_proj.size * 2,
+    )
+    distant, direct = kernel_call(
+        functools.partial(far_kernel, rows),
+        (shape(2 * targets, wide), shape(blocks * targets, sources, dtype=F32)),
+        [*groups_of, out_proj],
+        4 * targets * part * (wide + 2 * sources),
         out_proj.size * 2,
         [pltpu.VMEM((sources, part), BF16)],
     )
-    scores = kernel_call(
-        scores_kernel,
-        shape(heads, blocks * targets, sources, dtype=F32),
-        [*values, reads],
-        2 * blocks * targets * sources * heads * head_dim,
-        1 << 22,
-        [pltpu.VMEM((sources, groups * head_dim), BF16)],
-    )
-
-    def edges(shown):
+
+    def scored(reads):
+        return kernel_call(
+            scores_kernel,
+            shape(heads, 2 * targets, sources, dtype=F32),
+            [*values, reads],
+            4 * targets * sources * heads * head_dim,
+            1 << 21,
+            [pltpu.VMEM((sources, groups * head_dim), BF16)],
+        )
+
+    scores = {"a": scored(distant), "b": scored(near)}
+
+    def edges(name, shown):
         away, kept = kernel_call(
             functools.partial(edges_kernel, heads, queries, shown),
             (shape(2 * block, len(shown) * targets, dtype=F32),) * 2,
-            [*tables, scores, direct, spots],
+            [*tables, scores[name], direct, spots],
             len(shown) * targets * sources * sources * heads * 2,
             1 << 22,
         )
@@ -323,15 +355,15 @@
         back = swapped((kept[:block] + away[:block]).astype(BF16), "src", 2)
         return kept[block:] + away[block:] + back.astype(F32)
 
-    distant = edges((2, 3))
-    closer = edges((0, 1))
-    second = swapped(distant[:, :targets].astype(BF16), "tgt", 2)
-    third = swapped(distant[:, targets:].astype(BF16), "tgt", 3)
+    outer = edges("a", (2, 3))
+    closer = edges("b", (0, 1))
+    second = swapped(outer[:, :targets].astype(BF16), "tgt", 2)
+    third = swapped(outer[:, targets:].astype(BF16), "tgt", 3)
     first = swapped(closer[:, targets:].astype(BF16), "tgt", 1)
     total = closer[:, :targets]
     for value in (first, second, third):
         total = total + value.astype(F32)
-    return (total * cut[5]).astype(BF16)
+    return (total * cut[6]).astype(BF16)
 
 
 def ring(

time: 87.6 us -> 87.8 us (level)
  waiting for transfers between devices: 49.8 us -> 40.8 us
  starting transfers between devices: 25.1 us -> 33.9 us
    ppermute x28 -> x31, waiting for transfers between devices: 49.8 us -> 40.8 us  [swapped(): return lax.ppermute(value, axis, pairs)]
    ppermute x28 -> x31, starting transfers between devices: 25.1 us -> 33.9 us  [swapped(): return lax.ppermute(value, axis, pairs)]
    pallas_call x6 -> x8, Pallas kernels: 11.6 us -> 12 us  [kernel_call(): pl.pallas_call(body, out_shape=outs, in_specs=[pl.BlockSpec(memory_space=...]
  transfers between devices with their start and end apart: 28 -> 31, of which waited for: 13 -> 12; matrix products, arithmetic and copies ran while one was open for 0% -> 0% of each run, Pallas kernels for 10% -> 11%
where the time goes in v4:
time: 87.8 us; the launch traced here: 87.6 us
  waiting for transfers between devices  40.8 us (46%)
  starting transfers between devices  33.9 us (39%)
  Pallas kernels  12 us (14%)
    ppermute x31, waiting for transfers between devices, swapped(): return lax.ppermute(value, axis, pairs)  40.8 us
    ppermute x31, starting transfers between devices, swapped(): return lax.ppermute(value, axis, pairs)  33.9 us
    pallas_call x8, Pallas kernels, kernel_call(): pl.pallas_call(body, out_shape=outs, in_specs=[pl.BlockSpec(memory_space=...  12 us
  transfers between devices with their start and end apart: 31, of which 12 were waited for; matrix products, arithmetic and copies ran while one was open for 0% of the time, Pallas kernels for 11%

profile of v4, /device:TPU:0, one launch (start us, length us, event | category | flops | bytes accessed | tf_op | source)
XLA Modules:
  0.0 87.6 jit_solution(2909027350762623762)
XLA Ops:
  0.0 1.6 %shard_map.82 = (bf16[128,1152]{1,0:T(8,128)(2,1)S(1)}, bf16[80,1152]{1,0:T(8,128)(2,1)S(1)}, bf16[80,1152]{1,0:T(8,128)(2,1)S(1)}, bf16[80,1152]{1,0:T(8,128)(2...) custom-call(bf16[64,4608]{1,0:T(8,128)(2,1)} %targets.1, ...), custom_call_target="tpu_custom_call" | custom-call | flops 67108864 | bytes 1179648 | tf_op jit(solution)/shard_map/pallas_call | solution.py:28
  1.6 3.0 %collective-permute-start.7 = (bf16[128,1152]{1,0:T(8,128)(2,1)S(1)}, bf16[128,1152]{1,0:T(8,128)(2,1)S(1)}, u32[]{:S(2)}, u32[]{:S(2)}) collective-permute-start(bf16[128,1152]{1,0:T(8,128)(2,1)S(1)} %get-tuple-element.20.own.refs_0_), channel_id=1, source_target_pairs={{0,2},{1,3},{2,0},{3,1},{4,6},{5,7},{6,4},{7,5},{8,10},{9,11},{10,... | collective-permute-start | bytes 884744 | tf_op jit(solution)/shard_map/ppermute | solution.py:24
  4.6 2.6 %collective-permute-start.4 = (bf16[256,256]{1,0:T(8,128)(2,1)S(1)}, bf16[256,256]{1,0:T(8,128)(2,1)S(1)}, u32[]{:S(2)}, u32[]{:S(2)}) collective-permute-start(bf16[256,256]{1,0:T(8,128)(2,1)S(1)} %get-tuple-element.19.refs_4_), channel_id=1, source_target_pairs={{0,8},{4,12},{8,0},{12,4},{1,9},{5,13},{9,1},{13,5},{2,10},{6,14},... | collective-permute-start | bytes 393224 | tf_op jit(solution)/shard_map/ppermute | solution.py:24
  7.5 1.6 %collective-permute-start.12 = (bf16[80,1152]{1,0:T(8,128)(2,1)S(1)}, bf16[80,1152]{1,0:T(8,128)(2,1)S(1)}, u32[]{:S(2)}, u32[]{:S(2)}) collective-permute-start(bf16[80,1152]{1,0:T(8,128)(2,1)S(1)} %get-tuple-element.21), channel_id=1, source_target_pairs={{0,4},{4,0},{8,12},{12,8},{1,5},{5,1},{9,13},{13,9},{2,6},{6,2},{1... | collective-permute-start | bytes 552968 | tf_op jit(solution)/shard_map/ppermute | solution.py:24
  9.1 8.3 %collective-permute-done.4.refs_6_ = bf16[256,256]{1,0:T(8,128)(2,1)S(1)} collective-permute-done((bf16[256,256]{1,0:T(8,128)(2,1)S(1)}, bf16[256,256]{1,0:T(8,128)(2,1)S(1)}, u32[]{:S(2)}, u32[]{:S(2)}) %collective-permute-start.4) | collective-permute-done | bytes 131104 | tf_op jit(solution)/shard_map/ppermute | solution.py:24
  17.4 2.9 %collective-permute-done.1.refs_2_ = bf16[272,256]{1,0:T(8,128)(2,1)S(1)} collective-permute-done((bf16[272,256]{1,0:T(8,128)(2,1)S(1)}, bf16[272,256]{1,0:T(8,128)(2,1)S(1)}, u32[]{:S(2)}, u32[]{:S(2)}) %collective-permute-start.1) | collective-permute-done | bytes 139296 | tf_op jit(solution)/shard_map/ppermute | solution.py:24
  20.3 6.6 %collective-permute-start.20 = (bf16[80,1152]{1,0:T(8,128)(2,1)S(1)}, bf16[80,1152]{1,0:T(8,128)(2,1)S(1)}, u32[]{:S(2)}, u32[]{:S(2)}) collective-permute-start(bf16[80,1152]{1,0:T(8,128)(2,1)S(1)} %get-tuple-element.23), channel_id=1, source_target_pairs={{0,12},{4,8},{8,4},{12,0},{1,13},{5,9},{9,5},{13,1},{2,14},{6,10},... | collective-permute-start | bytes 552968 | tf_op jit(solution)/shard_map/ppermute | solution.py:24
  26.8 0.6 collective-permute-start.14
  27.4 4.9 %collective-permute-done.16.refs_8_ = bf16[80,1152]{1,0:T(8,128)(2,1)S(1)} collective-permute-done((bf16[80,1152]{1,0:T(8,128)(2,1)S(1)}, bf16[80,1152]{1,0:T(8,128)(2,1)S(1)}, u32[]{:S(2)}, u32[]{:S(2)}) %collective-permute-start.16) | collective-permute-done | bytes 184352 | tf_op jit(solution)/shard_map/ppermute | solution.py:24
  32.7 1.6 %collective-permute-start.22 = (bf16[80,1152]{1,0:T(8,128)(2,1)S(1)}, bf16[80,1152]{1,0:T(8,128)(2,1)S(1)}, u32[]{:S(2)}, u32[]{:S(2)}) collective-permute-start(bf16[80,1152]{1,0:T(8,128)(2,1)S(1)} %collective-permute-done.20.refs_12_), channel_id=1, source_target_pairs={{0,2},{1,3},{2,0},{3,1},{4,6},{5,7},{6,4},{7,5},{8,10},{9,11},{10,... | collective-permute-start | bytes 552968 | tf_op jit(solution)/shard_map/ppermute | solution.py:24
  34.8 5.0 %collective-permute-done.18.refs_10_ = bf16[80,1152]{1,0:T(8,128)(2,1)S(1)} collective-permute-done((bf16[80,1152]{1,0:T(8,128)(2,1)S(1)}, bf16[80,1152]{1,0:T(8,128)(2,1)S(1)}, u32[]{:S(2)}, u32[]{:S(2)}) %collective-permute-start.18) | collective-permute-done | bytes 184352 | tf_op jit(solution)/shard_map/ppermute | solution.py:24
  39.8 3.5 %collective-permute-done.22.refs_14_ = bf16[80,1152]{1,0:T(8,128)(2,1)S(1)} collective-permute-done((bf16[80,1152]{1,0:T(8,128)(2,1)S(1)}, bf16[80,1152]{1,0:T(8,128)(2,1)S(1)}, u32[]{:S(2)}, u32[]{:S(2)}) %collective-permute-start.22) | collective-permute-done | bytes 184352 | tf_op jit(solution)/shard_map/ppermute | solution.py:24
  43.8 2.7 %shard_map.83.home = bf16[64,512]{1,0:T(8,128)(2,1)S(1)} custom-call(bf16[128,1152]{1,0:T(8,128)(2,1)S(1)} %get-tuple-element.20.own.refs_0_, bf16[128,1152]{1,0:T(8,128)(2,1)S(1)} %collective-permute-done.6.core.refs_1_, bf16[128,1152]{1,0:T(8,128)(2,1)S(1)} %collective-permute-done.7.far.refs_2_, ...), custom_call_target="tpu_custom_call" | custom-call | flops 301989888 | bytes 4718592 | tf_op jit(solution)/shard_map/pallas_call | solution.py:28
  46.5 5.0 %collective-permute-start.10 = (bf16[64,512]{1,0:T(8,128)(2,1)S(1)}, bf16[64,512]{1,0:T(8,128)(2,1)S(1)}, u32[]{:S(2)}, u32[]{:S(2)}) collective-permute-start(bf16[64,512]{1,0:T(8,128)(2,1)S(1)} %shard_map.83.home), channel_id=1, source_target_pairs={{0,8},{4,12},{8,0},{12,4},{1,9},{5,13},{9,1},{13,5},{2,10},{6,14},... | collective-permute-start | bytes 196616 | tf_op jit(solution)/shard_map/ppermute | solution.py:24
  51.5 2.0 %collective-permute-start.3 = (bf16[256,256]{1,0:T(8,128)(2,1)S(1)}, bf16[256,256]{1,0:T(8,128)(2,1)S(1)}, u32[]{:S(2)}, u32[]{:S(2)}) collective-permute-start(bf16[256,256]{1,0:T(8,128)(2,1)S(1)} %get-tuple-element.19.refs_4_), channel_id=1, source_target_pairs={{0,4},{4,0},{8,12},{12,8},{1,5},{5,1},{9,13},{13,9},{2,6},{6,2},{1... | collective-permute-start | bytes 393224 | tf_op jit(solution)/shard_map/ppermute | solution.py:24
  53.6 2.0 %collective-permute-start.5 = (bf16[256,256]{1,0:T(8,128)(2,1)S(1)}, bf16[256,256]{1,0:T(8,128)(2,1)S(1)}, u32[]{:S(2)}, u32[]{:S(2)}) collective-permute-start(bf16[256,256]{1,0:T(8,128)(2,1)S(1)} %collective-permute-done.4.refs_6_), channel_id=1, source_target_pairs={{0,4},{4,0},{8,12},{12,8},{1,5},{5,1},{9,13},{13,9},{2,6},{6,2},{1... | collective-permute-start | bytes 393224 | tf_op jit(solution)/shard_map/ppermute | solution.py:24
  55.6 1.0 %collective-permute-done.9.first = bf16[64,512]{1,0:T(8,128)(2,1)S(1)} collective-permute-done((bf16[64,512]{1,0:T(8,128)(2,1)S(1)}, bf16[64,512]{1,0:T(8,128)(2,1)S(1)}, u32[]{:S(2)}, u32[]{:S(2)}) %collective-permute-start.9) | collective-permute-done | bytes 65568 | tf_op jit(solution)/shard_map/ppermute | solution.py:24
  56.6 1.2 %collective-permute-start.11 = (bf16[64,512]{1,0:T(8,128)(2,1)S(1)}, bf16[64,512]{1,0:T(8,128)(2,1)S(1)}, u32[]{:S(2)}, u32[]{:S(2)}) collective-permute-start(bf16[64,512]{1,0:T(8,128)(2,1)S(1)} %collective-permute-done.10.second), channel_id=1, source_target_pairs={{0,4},{4,0},{8,12},{12,8},{1,5},{5,1},{9,13},{13,9},{2,6},{6,2},{1... | collective-permute-start | bytes 196616 | tf_op jit(solution)/shard_map/ppermute | solution.py:24
  57.8 2.3 %shard_map.86 = (bf16[512,1024]{1,0:T(8,128)(2,1)S(1)}, f32[1024,256]{1,0:T(8,128)S(1)}) custom-call(bf16[128,1152]{1,0:T(8,128)(2,1)S(1)} %get-tuple-element.20.own.refs_0_, bf16[128,1152]{1,0:T(8,128)(2,1)S(1)} %collective-permute-done.6.core.refs_1_, bf16[128,1152]{1,0:T(8,128)(2,1)S(1)} %collective-permute-done.7.far.refs_2_, ...), custom_call_target="tpu_custom_call" | custom-call | flops 1811939328 | bytes 2359296 | tf_op jit(solution)/shard_map/pallas_call | solution.py:28
  60.2 8.9 %collective-permute-done.11.third = bf16[64,512]{1,0:T(8,128)(2,1)S(1)} collective-permute-done((bf16[64,512]{1,0:T(8,128)(2,1)S(1)}, bf16[64,512]{1,0:T(8,128)(2,1)S(1)}, u32[]{:S(2)}, u32[]{:S(2)}) %collective-permute-start.11) | collective-permute-done | bytes 65568 | tf_op jit(solution)/shard_map/ppermute | solution.py:24
  69.1 0.8 shard_map.88.refs_8_
  69.9 1.1 %shard_map.89 = (f32[128,512]{1,0:T(8,128)S(1)}, f32[128,512]{1,0:T(8,128)S(1)}) custom-call(bf16[272,256]{1,0:T(8,128)(2,1)S(1)} %get-tuple-element.18.refs_0_, bf16[272,256]{1,0:T(8,128)(2,1)S(1)} %collective-permute-done.refs_1_, bf16[272,256]{1,0:T(8,128)(2,1)S(1)} %collective-permute-done.1.refs_2_, ...), custom_call_target="tpu_custom_call" | custom-call | flops 536870912 | bytes 4194304 | tf_op jit(solution)/shard_map/pallas_call | solution.py:28
  71.1 1.6 %shard_map.84.reads = bf16[512,1024]{1,0:T(8,128)(2,1)S(1)} custom-call(bf16[128,1152]{1,0:T(8,128)(2,1)S(1)} %get-tuple-element.20.own.refs_0_, bf16[128,1152]{1,0:T(8,128)(2,1)S(1)} %collective-permute-done.6.core.refs_1_, bf16[128,1152]{1,0:T(8,128)(2,1)S(1)} %collective-permute-done.7.far.refs_2_, ...), custom_call_target="tpu_custom_call" | custom-call | flops 1207959552 | bytes 2359296 | tf_op jit(solution)/shard_map/pallas_call | solution.py:28
  72.7 0.8 shard_map.85.refs_8_
  73.5 1.1 %shard_map.87 = (f32[128,512]{1,0:T(8,128)S(1)}, f32[128,512]{1,0:T(8,128)S(1)}) custom-call(bf16[272,256]{1,0:T(8,128)(2,1)S(1)} %get-tuple-element.18.refs_0_, bf16[272,256]{1,0:T(8,128)(2,1)S(1)} %collective-permute-done.refs_1_, bf16[272,256]{1,0:T(8,128)(2,1)S(1)} %collective-permute-done.1.refs_2_, ...), custom_call_target="tpu_custom_call" | custom-call | flops 536870912 | bytes 4194304 | tf_op jit(solution)/shard_map/pallas_call | solution.py:28
  76.4 1.0 %collective-permute-start.25 = (bf16[64,512]{1,0:T(8,128)(2,1)S(1)}, bf16[64,512]{1,0:T(8,128)(2,1)S(1)}, u32[]{:S(2)}, u32[]{:S(2)}) collective-permute-start(bf16[64,512]{1,0:T(8,128)(2,1)S(1)} %fusion.3), channel_id=1, source_target_pairs={{0,2},{1,3},{2,0},{3,1},{4,6},{5,7},{6,4},{7,5},{8,10},{9,11},{10,... | collective-permute-start | bytes 196616 | tf_op jit(solution)/shard_map/ppermute | solution.py:24
  77.4 2.3 %collective-permute-done.28 = bf16[64,512]{1,0:T(8,128)(2,1)S(1)} collective-permute-done((bf16[64,512]{1,0:T(8,128)(2,1)S(1)}, bf16[64,512]{1,0:T(8,128)(2,1)S(1)}, u32[]{:S(2)}, u32[]{:S(2)}) %collective-permute-start.28) | collective-permute-done | bytes 65568 | tf_op jit(solution)/shard_map/ppermute | solution.py:24
  79.9 3.1 %collective-permute-start.30 = (bf16[64,256]{1,0:T(8,128)(2,1)S(1)}, bf16[64,256]{1,0:T(8,128)(2,1)S(1)}, u32[]{:S(2)}, u32[]{:S(2)}) collective-permute-start(bf16[64,256]{1,0:T(8,128)(2,1)S(1)} %get-tuple-element.32), channel_id=1, source_target_pairs={{0,12},{4,8},{8,4},{12,0},{1,13},{5,9},{9,5},{13,1},{2,14},{6,10},... | collective-permute-start | bytes 98312 | tf_op jit(solution)/shard_map/ppermute | solution.py:24
  83.4 1.6 %collective-permute-done.29 = bf16[64,256]{1,0:T(8,128)(2,1)S(1)} collective-permute-done((bf16[64,256]{1,0:T(8,128)(2,1)S(1)}, bf16[64,256]{1,0:T(8,128)(2,1)S(1)}, u32[]{:S(2)}, u32[]{:S(2)}) %collective-permute-start.29) | collective-permute-done | bytes 32800 | tf_op jit(solution)/shard_map/ppermute | solution.py:24
  85.0 0.6 collective-permute-done.30
  85.6 1.4 %collective-permute-done.26 = bf16[64,256]{1,0:T(8,128)(2,1)S(1)} collective-permute-done((bf16[64,256]{1,0:T(8,128)(2,1)S(1)}, bf16[64,256]{1,0:T(8,128)(2,1)S(1)}, u32[]{:S(2)}, u32[]{:S(2)}) %collective-permute-start.26) | collective-permute-done | bytes 32800 | tf_op jit(solution)/shard_map/ppermute | solution.py:24
  87.0 0.6 fusion.8
  (49 shorter events, 4.4 us)
Async XLA Ops:
  0.0 57.8 %copy-start = (bf16[8,1152,128]{2,1,0:T(8,128)(2,1)S(1)}, bf16[8,1152,128]{2,1,0:T(8,128)(2,1)}, u32[]{:S(2)}) copy-start(bf16[8,1152,128]{2,1,0:T(8,128)(2,1)} %refs_16_.1) | copy-start | bytes 7077892
  1.6 25.2 %collective-permute-start.7 = (bf16[128,1152]{1,0:T(8,128)(2,1)S(1)}, bf16[128,1152]{1,0:T(8,128)(2,1)S(1)}, u32[]{:S(2)}, u32[]{:S(2)}) collective-permute-start(bf16[128,1152]{1,0:T(8,128)(2,1)S(1)} %get-tuple-element.20.own.refs_0_), channel_id=1, source_target_pairs={{0,2},{1,3},{2,0},{3,1},{4,6},{5,7},{6,4},{7,5},{8,10},{9,11},{10,... | collective-permute-start | bytes 884744 | tf_op jit(solution)/shard_map/ppermute | solution.py:24
  4.6 12.8 %collective-permute-start.4 = (bf16[256,256]{1,0:T(8,128)(2,1)S(1)}, bf16[256,256]{1,0:T(8,128)(2,1)S(1)}, u32[]{:S(2)}, u32[]{:S(2)}) collective-permute-start(bf16[256,256]{1,0:T(8,128)(2,1)S(1)} %get-tuple-element.19.refs_4_), channel_id=1, source_target_pairs={{0,8},{4,12},{8,0},{12,4},{1,9},{5,13},{9,1},{13,5},{2,10},{6,14},... | collective-permute-start | bytes 393224 | tf_op jit(solution)/shard_map/ppermute | solution.py:24
  7.2 13.1 %collective-permute-start.1 = (bf16[272,256]{1,0:T(8,128)(2,1)S(1)}, bf16[272,256]{1,0:T(8,128)(2,1)S(1)}, u32[]{:S(2)}, u32[]{:S(2)}) collective-permute-start(bf16[272,256]{1,0:T(8,128)(2,1)S(1)} %get-tuple-element.18.refs_0_), channel_id=1, source_target_pairs={{0,8},{4,12},{8,0},{12,4},{1,9},{5,13},{9,1},{13,5},{2,10},{6,14},... | collective-permute-start | bytes 417800 | tf_op jit(solution)/shard_map/ppermute | solution.py:24
  7.5 25.2 %collective-permute-start.6 = (bf16[128,1152]{1,0:T(8,128)(2,1)S(1)}, bf16[128,1152]{1,0:T(8,128)(2,1)S(1)}, u32[]{:S(2)}, u32[]{:S(2)}) collective-permute-start(bf16[128,1152]{1,0:T(8,128)(2,1)S(1)} %get-tuple-element.20.own.refs_0_), channel_id=1, source_target_pairs={{0,1},{1,0},{2,3},{3,2},{4,5},{5,4},{6,7},{7,6},{8,9},{9,8},{10,11... | collective-permute-start | bytes 884744 | tf_op jit(solution)/shard_map/ppermute | solution.py:24
  7.5 19.3 %collective-permute-start.12 = (bf16[80,1152]{1,0:T(8,128)(2,1)S(1)}, bf16[80,1152]{1,0:T(8,128)(2,1)S(1)}, u32[]{:S(2)}, u32[]{:S(2)}) collective-permute-start(bf16[80,1152]{1,0:T(8,128)(2,1)S(1)} %get-tuple-element.21), channel_id=1, source_target_pairs={{0,4},{4,0},{8,12},{12,8},{1,5},{5,1},{9,13},{13,9},{2,6},{6,2},{1... | collective-permute-start | bytes 552968 | tf_op jit(solution)/shard_map/ppermute | solution.py:24
  17.4 14.9 %collective-permute-start.16 = (bf16[80,1152]{1,0:T(8,128)(2,1)S(1)}, bf16[80,1152]{1,0:T(8,128)(2,1)S(1)}, u32[]{:S(2)}, u32[]{:S(2)}) collective-permute-start(bf16[80,1152]{1,0:T(8,128)(2,1)S(1)} %get-tuple-element.22), channel_id=1, source_target_pairs={{0,8},{4,12},{8,0},{12,4},{1,9},{5,13},{9,1},{13,5},{2,10},{6,14},... | collective-permute-start | bytes 552968 | tf_op jit(solution)/shard_map/ppermute | solution.py:24
  20.3 12.0 %collective-permute-start.20 = (bf16[80,1152]{1,0:T(8,128)(2,1)S(1)}, bf16[80,1152]{1,0:T(8,128)(2,1)S(1)}, u32[]{:S(2)}, u32[]{:S(2)}) collective-permute-start(bf16[80,1152]{1,0:T(8,128)(2,1)S(1)} %get-tuple-element.23), channel_id=1, source_target_pairs={{0,12},{4,8},{8,4},{12,0},{1,13},{5,9},{9,5},{13,1},{2,14},{6,10},... | collective-permute-start | bytes 552968 | tf_op jit(solution)/shard_map/ppermute | solution.py:24
  26.8 16.5 %collective-permute-start.8 = (bf16[128,1152]{1,0:T(8,128)(2,1)S(1)}, bf16[128,1152]{1,0:T(8,128)(2,1)S(1)}, u32[]{:S(2)}, u32[]{:S(2)}) collective-permute-start(bf16[128,1152]{1,0:T(8,128)(2,1)S(1)} %collective-permute-done.7.far.refs_2_), channel_id=1, source_target_pairs={{0,1},{1,0},{2,3},{3,2},{4,5},{5,4},{6,7},{7,6},{8,9},{9,8},{10,11... | collective-permute-start | bytes 884744 | tf_op jit(solution)/shard_map/ppermute | solution.py:24
  26.8 7.5 %collective-permute-start.14 = (bf16[80,1152]{1,0:T(8,128)(2,1)S(1)}, bf16[80,1152]{1,0:T(8,128)(2,1)S(1)}, u32[]{:S(2)}, u32[]{:S(2)}) collective-permute-start(bf16[80,1152]{1,0:T(8,128)(2,1)S(1)} %collective-permute-done.12.refs_4_), channel_id=1, source_target_pairs={{0,2},{1,3},{2,0},{3,1},{4,6},{5,7},{6,4},{7,5},{8,10},{9,11},{10,... | collective-permute-start | bytes 552968 | tf_op jit(solution)/shard_map/ppermute | solution.py:24
  32.3 2.0 %collective-permute-start.13 = (bf16[80,1152]{1,0:T(8,128)(2,1)S(1)}, bf16[80,1152]{1,0:T(8,128)(2,1)S(1)}, u32[]{:S(2)}, u32[]{:S(2)}) collective-permute-start(bf16[80,1152]{1,0:T(8,128)(2,1)S(1)} %collective-permute-done.12.refs_4_), channel_id=1, source_target_pairs={{0,1},{1,0},{2,3},{3,2},{4,5},{5,4},{6,7},{7,6},{8,9},{9,8},{10,11... | collective-permute-start | bytes 552968 | tf_op jit(solution)/shard_map/ppermute | solution.py:24
  32.3 7.5 %collective-permute-start.18 = (bf16[80,1152]{1,0:T(8,128)(2,1)S(1)}, bf16[80,1152]{1,0:T(8,128)(2,1)S(1)}, u32[]{:S(2)}, u32[]{:S(2)}) collective-permute-start(bf16[80,1152]{1,0:T(8,128)(2,1)S(1)} %collective-permute-done.16.refs_8_), channel_id=1, source_target_pairs={{0,2},{1,3},{2,0},{3,1},{4,6},{5,7},{6,4},{7,5},{8,10},{9,11},{10,... | collective-permute-start | bytes 552968 | tf_op jit(solution)/shard_map/ppermute | solution.py:24
  32.7 10.6 %collective-permute-start.22 = (bf16[80,1152]{1,0:T(8,128)(2,1)S(1)}, bf16[80,1152]{1,0:T(8,128)(2,1)S(1)}, u32[]{:S(2)}, u32[]{:S(2)}) collective-permute-start(bf16[80,1152]{1,0:T(8,128)(2,1)S(1)} %collective-permute-done.20.refs_12_), channel_id=1, source_target_pairs={{0,2},{1,3},{2,0},{3,1},{4,6},{5,7},{6,4},{7,5},{8,10},{9,11},{10,... | collective-permute-start | bytes 552968 | tf_op jit(solution)/shard_map/ppermute | solution.py:24
  34.3 12.2 %collective-permute-start.17 = (bf16[80,1152]{1,0:T(8,128)(2,1)S(1)}, bf16[80,1152]{1,0:T(8,128)(2,1)S(1)}, u32[]{:S(2)}, u32[]{:S(2)}) collective-permute-start(bf16[80,1152]{1,0:T(8,128)(2,1)S(1)} %collective-permute-done.16.refs_8_), channel_id=1, source_target_pairs={{0,1},{1,0},{2,3},{3,2},{4,5},{5,4},{6,7},{7,6},{8,9},{9,8},{10,11... | collective-permute-start | bytes 552968 | tf_op jit(solution)/shard_map/ppermute | solution.py:24
  34.3 17.2 %collective-permute-start.21 = (bf16[80,1152]{1,0:T(8,128)(2,1)S(1)}, bf16[80,1152]{1,0:T(8,128)(2,1)S(1)}, u32[]{:S(2)}, u32[]{:S(2)}) collective-permute-start(bf16[80,1152]{1,0:T(8,128)(2,1)S(1)} %collective-permute-done.20.refs_12_), channel_id=1, source_target_pairs={{0,1},{1,0},{2,3},{3,2},{4,5},{5,4},{6,7},{7,6},{8,9},{9,8},{10,11... | collective-permute-start | bytes 552968 | tf_op jit(solution)/shard_map/ppermute | solution.py:24
  39.8 11.7 %collective-permute-start.15 = (bf16[80,1152]{1,0:T(8,128)(2,1)S(1)}, bf16[80,1152]{1,0:T(8,128)(2,1)S(1)}, u32[]{:S(2)}, u32[]{:S(2)}) collective-permute-start(bf16[80,1152]{1,0:T(8,128)(2,1)S(1)} %collective-permute-done.14.refs_6_), channel_id=1, source_target_pairs={{0,1},{1,0},{2,3},{3,2},{4,5},{5,4},{6,7},{7,6},{8,9},{9,8},{10,11... | collective-permute-start | bytes 552968 | tf_op jit(solution)/shard_map/ppermute | solution.py:24
  43.3 10.2 %collective-permute-start.19 = (bf16[80,1152]{1,0:T(8,128)(2,1)S(1)}, bf16[80,1152]{1,0:T(8,128)(2,1)S(1)}, u32[]{:S(2)}, u32[]{:S(2)}) collective-permute-start(bf16[80,1152]{1,0:T(8,128)(2,1)S(1)} %collective-permute-done.18.refs_10_), channel_id=1, source_target_pairs={{0,1},{1,0},{2,3},{3,2},{4,5},{5,4},{6,7},{7,6},{8,9},{9,8},{10,11... | collective-permute-start | bytes 552968 | tf_op jit(solution)/shard_map/ppermute | solution.py:24
  43.3 10.3 %collective-permute-start.23 = (bf16[80,1152]{1,0:T(8,128)(2,1)S(1)}, bf16[80,1152]{1,0:T(8,128)(2,1)S(1)}, u32[]{:S(2)}, u32[]{:S(2)}) collective-permute-start(bf16[80,1152]{1,0:T(8,128)(2,1)S(1)} %collective-permute-done.22.refs_14_), channel_id=1, source_target_pairs={{0,1},{1,0},{2,3},{3,2},{4,5},{5,4},{6,7},{7,6},{8,9},{9,8},{10,11... | collective-permute-start | bytes 552968 | tf_op jit(solution)/shard_map/ppermute | solution.py:24
  46.5 9.0 %collective-permute-start.10 = (bf16[64,512]{1,0:T(8,128)(2,1)S(1)}, bf16[64,512]{1,0:T(8,128)(2,1)S(1)}, u32[]{:S(2)}, u32[]{:S(2)}) collective-permute-start(bf16[64,512]{1,0:T(8,128)(2,1)S(1)} %shard_map.83.home), channel_id=1, source_target_pairs={{0,8},{4,12},{8,0},{12,4},{1,9},{5,13},{9,1},{13,5},{2,10},{6,14},... | collective-permute-start | bytes 196616 | tf_op jit(solution)/shard_map/ppermute | solution.py:24
  51.5 5.2 %collective-permute-start.9 = (bf16[64,512]{1,0:T(8,128)(2,1)S(1)}, bf16[64,512]{1,0:T(8,128)(2,1)S(1)}, u32[]{:S(2)}, u32[]{:S(2)}) collective-permute-start(bf16[64,512]{1,0:T(8,128)(2,1)S(1)} %shard_map.83.home), channel_id=1, source_target_pairs={{0,4},{4,0},{8,12},{12,8},{1,5},{5,1},{9,13},{13,9},{2,6},{6,2},{1... | collective-permute-start | bytes 196616 | tf_op jit(solution)/shard_map/ppermute | solution.py:24
  51.5 18.4 %collective-permute-start.3 = (bf16[256,256]{1,0:T(8,128)(2,1)S(1)}, bf16[256,256]{1,0:T(8,128)(2,1)S(1)}, u32[]{:S(2)}, u32[]{:S(2)}) collective-permute-start(bf16[256,256]{1,0:T(8,128)(2,1)S(1)} %get-tuple-element.19.refs_4_), channel_id=1, source_target_pairs={{0,4},{4,0},{8,12},{12,8},{1,5},{5,1},{9,13},{13,9},{2,6},{6,2},{1... | collective-permute-start | bytes 393224 | tf_op jit(solution)/shard_map/ppermute | solution.py:24
  53.5 16.4 %collective-permute-start = (bf16[272,256]{1,0:T(8,128)(2,1)S(1)}, bf16[272,256]{1,0:T(8,128)(2,1)S(1)}, u32[]{:S(2)}, u32[]{:S(2)}) collective-permute-start(bf16[272,256]{1,0:T(8,128)(2,1)S(1)} %get-tuple-element.18.refs_0_), channel_id=1, source_target_pairs={{0,4},{4,0},{8,12},{12,8},{1,5},{5,1},{9,13},{13,9},{2,6},{6,2},{1... | collective-permute-start | bytes 417800 | tf_op jit(solution)/shard_map/ppermute | solution.py:24
  53.6 16.3 %collective-permute-start.5 = (bf16[256,256]{1,0:T(8,128)(2,1)S(1)}, bf16[256,256]{1,0:T(8,128)(2,1)S(1)}, u32[]{:S(2)}, u32[]{:S(2)}) collective-permute-start(bf16[256,256]{1,0:T(8,128)(2,1)S(1)} %collective-permute-done.4.refs_6_), channel_id=1, source_target_pairs={{0,4},{4,0},{8,12},{12,8},{1,5},{5,1},{9,13},{13,9},{2,6},{6,2},{1... | collective-permute-start | bytes 393224 | tf_op jit(solution)/shard_map/ppermute | solution.py:24
  55.5 14.4 %collective-permute-start.2 = (bf16[272,256]{1,0:T(8,128)(2,1)S(1)}, bf16[272,256]{1,0:T(8,128)(2,1)S(1)}, u32[]{:S(2)}, u32[]{:S(2)}) collective-permute-start(bf16[272,256]{1,0:T(8,128)(2,1)S(1)} %collective-permute-done.1.refs_2_), channel_id=1, source_target_pairs={{0,4},{4,0},{8,12},{12,8},{1,5},{5,1},{9,13},{13,9},{2,6},{6,2},{1... | collective-permute-start | bytes 417800 | tf_op jit(solution)/shard_map/ppermute | solution.py:24
  56.6 12.4 %collective-permute-start.11 = (bf16[64,512]{1,0:T(8,128)(2,1)S(1)}, bf16[64,512]{1,0:T(8,128)(2,1)S(1)}, u32[]{:S(2)}, u32[]{:S(2)}) collective-permute-start(bf16[64,512]{1,0:T(8,128)(2,1)S(1)} %collective-permute-done.10.second), channel_id=1, source_target_pairs={{0,4},{4,0},{8,12},{12,8},{1,5},{5,1},{9,13},{13,9},{2,6},{6,2},{1... | collective-permute-start | bytes 196616 | tf_op jit(solution)/shard_map/ppermute | solution.py:24
  71.0 4.2 %collective-permute-start.27 = (f32[128,512]{1,0:T(8,128)S(1)}, f32[128,512]{1,0:T(8,128)S(1)}, u32[]{:S(2)}, u32[]{:S(2)}) collective-permute-start(f32[128,512]{1,0:T(8,128)S(1)} %get-tuple-element.29), channel_id=1, source_target_pairs={{0,1},{1,0},{2,3},{3,2},{4,5},{5,4},{6,7},{7,6},{8,9},{9,8},{10,11... | collective-permute-start | bytes 786440 | tf_op jit(solution)/shard_map/ppermute | solution.py:24
  74.6 1.7 %collective-permute-start.24 = (f32[128,512]{1,0:T(8,128)S(1)}, f32[128,512]{1,0:T(8,128)S(1)}, u32[]{:S(2)}, u32[]{:S(2)}) collective-permute-start(f32[128,512]{1,0:T(8,128)S(1)} %get-tuple-element.26), channel_id=1, source_target_pairs={{0,1},{1,0},{2,3},{3,2},{4,5},{5,4},{6,7},{7,6},{8,9},{9,8},{10,11... | collective-permute-start | bytes 786440 | tf_op jit(solution)/shard_map/ppermute | solution.py:24
  75.2 4.5 %collective-permute-start.28 = (bf16[64,512]{1,0:T(8,128)(2,1)S(1)}, bf16[64,512]{1,0:T(8,128)(2,1)S(1)}, u32[]{:S(2)}, u32[]{:S(2)}) collective-permute-start(bf16[64,512]{1,0:T(8,128)(2,1)S(1)} %fusion), channel_id=1, source_target_pairs={{0,2},{1,3},{2,0},{3,1},{4,6},{5,7},{6,4},{7,5},{8,10},{9,11},{10,... | collective-permute-start | bytes 196616 | tf_op jit(solution)/shard_map/ppermute | solution.py:24
  76.4 6.6 %collective-permute-start.25 = (bf16[64,512]{1,0:T(8,128)(2,1)S(1)}, bf16[64,512]{1,0:T(8,128)(2,1)S(1)}, u32[]{:S(2)}, u32[]{:S(2)}) collective-permute-start(bf16[64,512]{1,0:T(8,128)(2,1)S(1)} %fusion.3), channel_id=1, source_target_pairs={{0,2},{1,3},{2,0},{3,1},{4,6},{5,7},{6,4},{7,5},{8,10},{9,11},{10,... | collective-permute-start | bytes 196616 | tf_op jit(solution)/shard_map/ppermute | solution.py:24
  79.7 5.2 %collective-permute-start.29 = (bf16[64,256]{1,0:T(8,128)(2,1)S(1)}, bf16[64,256]{1,0:T(8,128)(2,1)S(1)}, u32[]{:S(2)}, u32[]{:S(2)}) collective-permute-start(bf16[64,256]{1,0:T(8,128)(2,1)S(1)} %get-tuple-element.31), channel_id=1, source_target_pairs={{0,8},{4,12},{8,0},{12,4},{1,9},{5,13},{9,1},{13,5},{2,10},{6,14},... | collective-permute-start | bytes 98312 | tf_op jit(solution)/shard_map/ppermute | solution.py:24
  79.9 5.7 %collective-permute-start.30 = (bf16[64,256]{1,0:T(8,128)(2,1)S(1)}, bf16[64,256]{1,0:T(8,128)(2,1)S(1)}, u32[]{:S(2)}, u32[]{:S(2)}) collective-permute-start(bf16[64,256]{1,0:T(8,128)(2,1)S(1)} %get-tuple-element.32), channel_id=1, source_target_pairs={{0,12},{4,8},{8,4},{12,0},{1,13},{5,9},{9,5},{13,1},{2,14},{6,10},... | collective-permute-start | bytes 98312 | tf_op jit(solution)/shard_map/ppermute | solution.py:24
  83.0 4.0 %collective-permute-start.26 = (bf16[64,256]{1,0:T(8,128)(2,1)S(1)}, bf16[64,256]{1,0:T(8,128)(2,1)S(1)}, u32[]{:S(2)}, u32[]{:S(2)}) collective-permute-start(bf16[64,256]{1,0:T(8,128)(2,1)S(1)} %slice.87), channel_id=1, source_target_pairs={{0,4},{4,0},{8,12},{12,8},{1,5},{5,1},{9,13},{13,9},{2,6},{6,2},{1... | collective-permute-start | bytes 98312 | tf_op jit(solution)/shard_map/ppermute | solution.py:24
  (1 other events, 9.7 us)

commit v5 on v4

--- a/solution.py
+++ b/solution.py
@@ -353,14 +353,17 @@
         )
         away = swapped(away, "src", 1)
         back = swapped((kept[:block] + away[:block]).astype(BF16), "src", 2)
-        return kept[block:] + away[block:] + back.astype(F32)
+        cuts = [slice(i * targets, (i + 1) * targets) for i in range(len(shown))]
+        return [
+            kept[block:, cut] + away[block:, cut] + back[:, cut].astype(F32) for cut in cuts
+        ]
 
     outer = edges("a", (2, 3))
     closer = edges("b", (0, 1))
-    second = swapped(outer[:, :targets].astype(BF16), "tgt", 2)
-    third = swapped(outer[:, targets:].astype(BF16), "tgt", 3)
-    first = swapped(closer[:, targets:].astype(BF16), "tgt", 1)
-    total = closer[:, :targets]
+    second = swapped(outer[0].astype(BF16), "tgt", 2)
+    third = swapped(outer[1].astype(BF16), "tgt", 3)
+    first = swapped(closer[1].astype(BF16), "tgt", 1)
+    total = closer[0]
     for value in (first, second, third):
         total = total + value.astype(F32)
     return (total * cut[6]).astype(BF16)

time: 87.8 us -> 84 us (0.957)
  waiting for transfers between devices: 40.8 us -> 33.3 us
  starting transfers between devices: 33.9 us -> 37.7 us
    ppermute x31, waiting for transfers between devices: 40.8 us -> 33.3 us  [swapped(): return lax.ppermute(value, axis, pairs)]
    ppermute x31, starting transfers between devices: 33.9 us -> 37.7 us  [swapped(): return lax.ppermute(value, axis, pairs)]
  transfers between devices with their start and end apart: 31 -> 31, of which waited for: 12 -> 10; matrix products, arithmetic and copies ran while one was open for 0% -> 0% of each run, Pallas kernels for 11% -> 11%
where the time goes in v5:
time: 84 us; the launch traced here: 83.9 us
  starting transfers between devices  37.7 us (45%)
  waiting for transfers between devices  33.3 us (40%)
  Pallas kernels  12 us (14%)
    ppermute x31, starting transfers between devices, swapped(): return lax.ppermute(value, axis, pairs)  37.7 us
    ppermute x31, waiting for transfers between devices, swapped(): return lax.ppermute(value, axis, pairs)  33.3 us
    pallas_call x8, Pallas kernels, kernel_call(): pl.pallas_call(body, out_shape=outs, in_specs=[pl.BlockSpec(memory_space=...  12 us
  transfers between devices with their start and end apart: 31, of which 10 were waited for; matrix products, arithmetic and copies ran while one was open for 0% of the time, Pallas kernels for 11%

profile of v5, /device:TPU:0, one launch (start us, length us, event | category | flops | bytes accessed | tf_op | source)
XLA Modules:
  0.0 83.9 jit_solution(15471727230325980807)
XLA Ops:
  0.0 1.6 %shard_map.82 = (bf16[128,1152]{1,0:T(8,128)(2,1)S(1)}, bf16[80,1152]{1,0:T(8,128)(2,1)S(1)}, bf16[80,1152]{1,0:T(8,128)(2,1)S(1)}, bf16[80,1152]{1,0:T(8,128)(2...) custom-call(bf16[64,4608]{1,0:T(8,128)(2,1)} %targets.1, ...), custom_call_target="tpu_custom_call" | custom-call | flops 67108864 | bytes 1179648 | tf_op jit(solution)/shard_map/pallas_call | solution.py:28
  1.6 3.0 %collective-permute-start.7 = (bf16[128,1152]{1,0:T(8,128)(2,1)S(1)}, bf16[128,1152]{1,0:T(8,128)(2,1)S(1)}, u32[]{:S(2)}, u32[]{:S(2)}) collective-permute-start(bf16[128,1152]{1,0:T(8,128)(2,1)S(1)} %get-tuple-element.20.own.refs_0_), channel_id=1, source_target_pairs={{0,2},{1,3},{2,0},{3,1},{4,6},{5,7},{6,4},{7,5},{8,10},{9,11},{10,... | collective-permute-start | bytes 884744 | tf_op jit(solution)/shard_map/ppermute | solution.py:24
  4.6 2.6 %collective-permute-start.1 = (bf16[272,256]{1,0:T(8,128)(2,1)S(1)}, bf16[272,256]{1,0:T(8,128)(2,1)S(1)}, u32[]{:S(2)}, u32[]{:S(2)}) collective-permute-start(bf16[272,256]{1,0:T(8,128)(2,1)S(1)} %get-tuple-element.18.refs_0_), channel_id=1, source_target_pairs={{0,8},{4,12},{8,0},{12,4},{1,9},{5,13},{9,1},{13,5},{2,10},{6,14},... | collective-permute-start | bytes 417800 | tf_op jit(solution)/shard_map/ppermute | solution.py:24
  7.2 1.6 %collective-permute-start.12 = (bf16[80,1152]{1,0:T(8,128)(2,1)S(1)}, bf16[80,1152]{1,0:T(8,128)(2,1)S(1)}, u32[]{:S(2)}, u32[]{:S(2)}) collective-permute-start(bf16[80,1152]{1,0:T(8,128)(2,1)S(1)} %get-tuple-element.21), channel_id=1, source_target_pairs={{0,4},{4,0},{8,12},{12,8},{1,5},{5,1},{9,13},{13,9},{2,6},{6,2},{1... | collective-permute-start | bytes 552968 | tf_op jit(solution)/shard_map/ppermute | solution.py:24
  9.1 5.6 %collective-permute-done.1.refs_2_ = bf16[272,256]{1,0:T(8,128)(2,1)S(1)} collective-permute-done((bf16[272,256]{1,0:T(8,128)(2,1)S(1)}, bf16[272,256]{1,0:T(8,128)(2,1)S(1)}, u32[]{:S(2)}, u32[]{:S(2)}) %collective-permute-start.1) | collective-permute-done | bytes 139296 | tf_op jit(solution)/shard_map/ppermute | solution.py:24
  14.7 2.6 %collective-permute-start.20 = (bf16[80,1152]{1,0:T(8,128)(2,1)S(1)}, bf16[80,1152]{1,0:T(8,128)(2,1)S(1)}, u32[]{:S(2)}, u32[]{:S(2)}) collective-permute-start(bf16[80,1152]{1,0:T(8,128)(2,1)S(1)} %get-tuple-element.23), channel_id=1, source_target_pairs={{0,12},{4,8},{8,4},{12,0},{1,13},{5,9},{9,5},{13,1},{2,14},{6,10},... | collective-permute-start | bytes 552968 | tf_op jit(solution)/shard_map/ppermute | solution.py:24
  17.3 0.9 %collective-permute-done.12.refs_4_ = bf16[80,1152]{1,0:T(8,128)(2,1)S(1)} collective-permute-done((bf16[80,1152]{1,0:T(8,128)(2,1)S(1)}, bf16[80,1152]{1,0:T(8,128)(2,1)S(1)}, u32[]{:S(2)}, u32[]{:S(2)}) %collective-permute-start.12) | collective-permute-done | bytes 184352 | tf_op jit(solution)/shard_map/ppermute | solution.py:24
  18.7 7.6 %collective-permute-done.16.refs_8_ = bf16[80,1152]{1,0:T(8,128)(2,1)S(1)} collective-permute-done((bf16[80,1152]{1,0:T(8,128)(2,1)S(1)}, bf16[80,1152]{1,0:T(8,128)(2,1)S(1)}, u32[]{:S(2)}, u32[]{:S(2)}) %collective-permute-start.16) | collective-permute-done | bytes 184352 | tf_op jit(solution)/shard_map/ppermute | solution.py:24
  26.8 1.6 %collective-permute-start.22 = (bf16[80,1152]{1,0:T(8,128)(2,1)S(1)}, bf16[80,1152]{1,0:T(8,128)(2,1)S(1)}, u32[]{:S(2)}, u32[]{:S(2)}) collective-permute-start(bf16[80,1152]{1,0:T(8,128)(2,1)S(1)} %collective-permute-done.20.refs_12_), channel_id=1, source_target_pairs={{0,2},{1,3},{2,0},{3,1},{4,6},{5,7},{6,4},{7,5},{8,10},{9,11},{10,... | collective-permute-start | bytes 552968 | tf_op jit(solution)/shard_map/ppermute | solution.py:24
  28.9 5.0 %collective-permute-done.18.refs_10_ = bf16[80,1152]{1,0:T(8,128)(2,1)S(1)} collective-permute-done((bf16[80,1152]{1,0:T(8,128)(2,1)S(1)}, bf16[80,1152]{1,0:T(8,128)(2,1)S(1)}, u32[]{:S(2)}, u32[]{:S(2)}) %collective-permute-start.18) | collective-permute-done | bytes 184352 | tf_op jit(solution)/shard_map/ppermute | solution.py:24
  33.9 3.5 %collective-permute-done.22.refs_14_ = bf16[80,1152]{1,0:T(8,128)(2,1)S(1)} collective-permute-done((bf16[80,1152]{1,0:T(8,128)(2,1)S(1)}, bf16[80,1152]{1,0:T(8,128)(2,1)S(1)}, u32[]{:S(2)}, u32[]{:S(2)}) %collective-permute-start.22) | collective-permute-done | bytes 184352 | tf_op jit(solution)/shard_map/ppermute | solution.py:24
  37.9 2.7 %shard_map.83.home = bf16[64,512]{1,0:T(8,128)(2,1)S(1)} custom-call(bf16[128,1152]{1,0:T(8,128)(2,1)S(1)} %get-tuple-element.20.own.refs_0_, bf16[128,1152]{1,0:T(8,128)(2,1)S(1)} %collective-permute-done.6.core.refs_1_, bf16[128,1152]{1,0:T(8,128)(2,1)S(1)} %collective-permute-done.7.far.refs_2_, ...), custom_call_target="tpu_custom_call" | custom-call | flops 301989888 | bytes 4718592 | tf_op jit(solution)/shard_map/pallas_call | solution.py:28
  40.6 3.3 %collective-permute-start = (bf16[272,256]{1,0:T(8,128)(2,1)S(1)}, bf16[272,256]{1,0:T(8,128)(2,1)S(1)}, u32[]{:S(2)}, u32[]{:S(2)}) collective-permute-start(bf16[272,256]{1,0:T(8,128)(2,1)S(1)} %get-tuple-element.18.refs_0_), channel_id=1, source_target_pairs={{0,4},{4,0},{8,12},{12,8},{1,5},{5,1},{9,13},{13,9},{2,6},{6,2},{1... | collective-permute-start | bytes 417800 | tf_op jit(solution)/shard_map/ppermute | solution.py:24
  43.9 2.0 %collective-permute-start.4 = (bf16[256,256]{1,0:T(8,128)(2,1)S(1)}, bf16[256,256]{1,0:T(8,128)(2,1)S(1)}, u32[]{:S(2)}, u32[]{:S(2)}) collective-permute-start(bf16[256,256]{1,0:T(8,128)(2,1)S(1)} %get-tuple-element.19.refs_4_), channel_id=1, source_target_pairs={{0,8},{4,12},{8,0},{12,4},{1,9},{5,13},{9,1},{13,5},{2,10},{6,14},... | collective-permute-start | bytes 393224 | tf_op jit(solution)/shard_map/ppermute | solution.py:24
  45.9 1.9 %collective-permute-start.2 = (bf16[272,256]{1,0:T(8,128)(2,1)S(1)}, bf16[272,256]{1,0:T(8,128)(2,1)S(1)}, u32[]{:S(2)}, u32[]{:S(2)}) collective-permute-start(bf16[272,256]{1,0:T(8,128)(2,1)S(1)} %collective-permute-done.1.refs_2_), channel_id=1, source_target_pairs={{0,4},{4,0},{8,12},{12,8},{1,5},{5,1},{9,13},{13,9},{2,6},{6,2},{1... | collective-permute-start | bytes 417800 | tf_op jit(solution)/shard_map/ppermute | solution.py:24
  48.0 0.9 %collective-permute-start.9 = (bf16[64,512]{1,0:T(8,128)(2,1)S(1)}, bf16[64,512]{1,0:T(8,128)(2,1)S(1)}, u32[]{:S(2)}, u32[]{:S(2)}) collective-permute-start(bf16[64,512]{1,0:T(8,128)(2,1)S(1)} %shard_map.83.home), channel_id=1, source_target_pairs={{0,4},{4,0},{8,12},{12,8},{1,5},{5,1},{9,13},{13,9},{2,6},{6,2},{1... | collective-permute-start | bytes 196616 | tf_op jit(solution)/shard_map/ppermute | solution.py:24
  48.9 2.3 %shard_map.86 = (bf16[512,1024]{1,0:T(8,128)(2,1)S(1)}, f32[1024,256]{1,0:T(8,128)S(1)}) custom-call(bf16[128,1152]{1,0:T(8,128)(2,1)S(1)} %get-tuple-element.20.own.refs_0_, bf16[128,1152]{1,0:T(8,128)(2,1)S(1)} %collective-permute-done.6.core.refs_1_, bf16[128,1152]{1,0:T(8,128)(2,1)S(1)} %collective-permute-done.7.far.refs_2_, ...), custom_call_target="tpu_custom_call" | custom-call | flops 1811939328 | bytes 2359296 | tf_op jit(solution)/shard_map/pallas_call | solution.py:28
  51.3 3.9 %collective-permute-start.3 = (bf16[256,256]{1,0:T(8,128)(2,1)S(1)}, bf16[256,256]{1,0:T(8,128)(2,1)S(1)}, u32[]{:S(2)}, u32[]{:S(2)}) collective-permute-start(bf16[256,256]{1,0:T(8,128)(2,1)S(1)} %get-tuple-element.19.refs_4_), channel_id=1, source_target_pairs={{0,4},{4,0},{8,12},{12,8},{1,5},{5,1},{9,13},{13,9},{2,6},{6,2},{1... | collective-permute-start | bytes 393224 | tf_op jit(solution)/shard_map/ppermute | solution.py:24
  55.2 4.4 %collective-permute-start.5 = (bf16[256,256]{1,0:T(8,128)(2,1)S(1)}, bf16[256,256]{1,0:T(8,128)(2,1)S(1)}, u32[]{:S(2)}, u32[]{:S(2)}) collective-permute-start(bf16[256,256]{1,0:T(8,128)(2,1)S(1)} %collective-permute-done.4.refs_6_), channel_id=1, source_target_pairs={{0,4},{4,0},{8,12},{12,8},{1,5},{5,1},{9,13},{13,9},{2,6},{6,2},{1... | collective-permute-start | bytes 393224 | tf_op jit(solution)/shard_map/ppermute | solution.py:24
  59.6 1.6 %shard_map.84.reads = bf16[512,1024]{1,0:T(8,128)(2,1)S(1)} custom-call(bf16[128,1152]{1,0:T(8,128)(2,1)S(1)} %get-tuple-element.20.own.refs_0_, bf16[128,1152]{1,0:T(8,128)(2,1)S(1)} %collective-permute-done.6.core.refs_1_, bf16[128,1152]{1,0:T(8,128)(2,1)S(1)} %collective-permute-done.7.far.refs_2_, ...), custom_call_target="tpu_custom_call" | custom-call | flops 1207959552 | bytes 2359296 | tf_op jit(solution)/shard_map/pallas_call | solution.py:28
  61.2 2.7 %collective-permute-done.11.third = bf16[64,512]{1,0:T(8,128)(2,1)S(1)} collective-permute-done((bf16[64,512]{1,0:T(8,128)(2,1)S(1)}, bf16[64,512]{1,0:T(8,128)(2,1)S(1)}, u32[]{:S(2)}, u32[]{:S(2)}) %collective-permute-start.11) | collective-permute-done | bytes 65568 | tf_op jit(solution)/shard_map/ppermute | solution.py:24
  63.9 0.8 shard_map.85.refs_8_
  64.7 1.1 %shard_map.87 = (f32[128,512]{1,0:T(8,128)S(1)}, f32[128,512]{1,0:T(8,128)S(1)}) custom-call(bf16[272,256]{1,0:T(8,128)(2,1)S(1)} %get-tuple-element.18.refs_0_, bf16[272,256]{1,0:T(8,128)(2,1)S(1)} %collective-permute-done.refs_1_, bf16[272,256]{1,0:T(8,128)(2,1)S(1)} %collective-permute-done.1.refs_2_, ...), custom_call_target="tpu_custom_call" | custom-call | flops 536870912 | bytes 4194304 | tf_op jit(solution)/shard_map/pallas_call | solution.py:28
  65.9 0.8 shard_map.88.refs_8_
  66.8 1.1 %shard_map.89 = (f32[128,512]{1,0:T(8,128)S(1)}, f32[128,512]{1,0:T(8,128)S(1)}) custom-call(bf16[272,256]{1,0:T(8,128)(2,1)S(1)} %get-tuple-element.18.refs_0_, bf16[272,256]{1,0:T(8,128)(2,1)S(1)} %collective-permute-done.refs_1_, bf16[272,256]{1,0:T(8,128)(2,1)S(1)} %collective-permute-done.1.refs_2_, ...), custom_call_target="tpu_custom_call" | custom-call | flops 536870912 | bytes 4194304 | tf_op jit(solution)/shard_map/pallas_call | solution.py:28
  69.6 1.0 %collective-permute-start.28 = (bf16[64,512]{1,0:T(8,128)(2,1)S(1)}, bf16[64,512]{1,0:T(8,128)(2,1)S(1)}, u32[]{:S(2)}, u32[]{:S(2)}) collective-permute-start(bf16[64,512]{1,0:T(8,128)(2,1)S(1)} %fusion), channel_id=1, source_target_pairs={{0,2},{1,3},{2,0},{3,1},{4,6},{5,7},{6,4},{7,5},{8,10},{9,11},{10,... | collective-permute-start | bytes 196616 | tf_op jit(solution)/shard_map/ppermute | solution.py:24
  70.7 2.3 %collective-permute-done.25 = bf16[64,512]{1,0:T(8,128)(2,1)S(1)} collective-permute-done((bf16[64,512]{1,0:T(8,128)(2,1)S(1)}, bf16[64,512]{1,0:T(8,128)(2,1)S(1)}, u32[]{:S(2)}, u32[]{:S(2)}) %collective-permute-start.25) | collective-permute-done | bytes 65568 | tf_op jit(solution)/shard_map/ppermute | solution.py:24
  73.0 1.5 %collective-permute-start.26 = (bf16[64,256]{1,0:T(8,128)(2,1)S(1)}, bf16[64,256]{1,0:T(8,128)(2,1)S(1)}, u32[]{:S(2)}, u32[]{:S(2)}) collective-permute-start(bf16[64,256]{1,0:T(8,128)(2,1)S(1)} %fusion.7), channel_id=1, source_target_pairs={{0,4},{4,0},{8,12},{12,8},{1,5},{5,1},{9,13},{13,9},{2,6},{6,2},{1... | collective-permute-start | bytes 98312 | tf_op jit(solution)/shard_map/ppermute | solution.py:24
  74.5 3.0 %collective-permute-start.29 = (bf16[64,256]{1,0:T(8,128)(2,1)S(1)}, bf16[64,256]{1,0:T(8,128)(2,1)S(1)}, u32[]{:S(2)}, u32[]{:S(2)}) collective-permute-start(bf16[64,256]{1,0:T(8,128)(2,1)S(1)} %get-tuple-element.31), channel_id=1, source_target_pairs={{0,8},{4,12},{8,0},{12,4},{1,9},{5,13},{9,1},{13,5},{2,10},{6,14},... | collective-permute-start | bytes 98312 | tf_op jit(solution)/shard_map/ppermute | solution.py:24
  78.1 1.5 %collective-permute-done.29 = bf16[64,256]{1,0:T(8,128)(2,1)S(1)} collective-permute-done((bf16[64,256]{1,0:T(8,128)(2,1)S(1)}, bf16[64,256]{1,0:T(8,128)(2,1)S(1)}, u32[]{:S(2)}, u32[]{:S(2)}) %collective-permute-start.29) | collective-permute-done | bytes 32800 | tf_op jit(solution)/shard_map/ppermute | solution.py:24
  79.6 3.6 %collective-permute-done.30 = bf16[64,256]{1,0:T(8,128)(2,1)S(1)} collective-permute-done((bf16[64,256]{1,0:T(8,128)(2,1)S(1)}, bf16[64,256]{1,0:T(8,128)(2,1)S(1)}, u32[]{:S(2)}, u32[]{:S(2)}) %collective-permute-start.30) | collective-permute-done | bytes 32800 | tf_op jit(solution)/shard_map/ppermute | solution.py:24
  83.2 0.6 fusion.13
  (47 shorter events, 4.9 us)
Async XLA Ops:
  0.0 48.9 %copy-start = (bf16[8,1152,128]{2,1,0:T(8,128)(2,1)S(1)}, bf16[8,1152,128]{2,1,0:T(8,128)(2,1)}, u32[]{:S(2)}) copy-start(bf16[8,1152,128]{2,1,0:T(8,128)(2,1)} %refs_16_.1) | copy-start | bytes 7077892
  1.6 15.7 %collective-permute-start.7 = (bf16[128,1152]{1,0:T(8,128)(2,1)S(1)}, bf16[128,1152]{1,0:T(8,128)(2,1)S(1)}, u32[]{:S(2)}, u32[]{:S(2)}) collective-permute-start(bf16[128,1152]{1,0:T(8,128)(2,1)S(1)} %get-tuple-element.20.own.refs_0_), channel_id=1, source_target_pairs={{0,2},{1,3},{2,0},{3,1},{4,6},{5,7},{6,4},{7,5},{8,10},{9,11},{10,... | collective-permute-start | bytes 884744 | tf_op jit(solution)/shard_map/ppermute | solution.py:24
  4.6 10.1 %collective-permute-start.1 = (bf16[272,256]{1,0:T(8,128)(2,1)S(1)}, bf16[272,256]{1,0:T(8,128)(2,1)S(1)}, u32[]{:S(2)}, u32[]{:S(2)}) collective-permute-start(bf16[272,256]{1,0:T(8,128)(2,1)S(1)} %get-tuple-element.18.refs_0_), channel_id=1, source_target_pairs={{0,8},{4,12},{8,0},{12,4},{1,9},{5,13},{9,1},{13,5},{2,10},{6,14},... | collective-permute-start | bytes 417800 | tf_op jit(solution)/shard_map/ppermute | solution.py:24
  7.2 19.6 %collective-permute-start.6 = (bf16[128,1152]{1,0:T(8,128)(2,1)S(1)}, bf16[128,1152]{1,0:T(8,128)(2,1)S(1)}, u32[]{:S(2)}, u32[]{:S(2)}) collective-permute-start(bf16[128,1152]{1,0:T(8,128)(2,1)S(1)} %get-tuple-element.20.own.refs_0_), channel_id=1, source_target_pairs={{0,1},{1,0},{2,3},{3,2},{4,5},{5,4},{6,7},{7,6},{8,9},{9,8},{10,11... | collective-permute-start | bytes 884744 | tf_op jit(solution)/shard_map/ppermute | solution.py:24
  7.2 11.0 %collective-permute-start.12 = (bf16[80,1152]{1,0:T(8,128)(2,1)S(1)}, bf16[80,1152]{1,0:T(8,128)(2,1)S(1)}, u32[]{:S(2)}, u32[]{:S(2)}) collective-permute-start(bf16[80,1152]{1,0:T(8,128)(2,1)S(1)} %get-tuple-element.21), channel_id=1, source_target_pairs={{0,4},{4,0},{8,12},{12,8},{1,5},{5,1},{9,13},{13,9},{2,6},{6,2},{1... | collective-permute-start | bytes 552968 | tf_op jit(solution)/shard_map/ppermute | solution.py:24
  8.8 17.6 %collective-permute-start.16 = (bf16[80,1152]{1,0:T(8,128)(2,1)S(1)}, bf16[80,1152]{1,0:T(8,128)(2,1)S(1)}, u32[]{:S(2)}, u32[]{:S(2)}) collective-permute-start(bf16[80,1152]{1,0:T(8,128)(2,1)S(1)} %get-tuple-element.22), channel_id=1, source_target_pairs={{0,8},{4,12},{8,0},{12,4},{1,9},{5,13},{9,1},{13,5},{2,10},{6,14},... | collective-permute-start | bytes 552968 | tf_op jit(solution)/shard_map/ppermute | solution.py:24
  14.7 11.6 %collective-permute-start.20 = (bf16[80,1152]{1,0:T(8,128)(2,1)S(1)}, bf16[80,1152]{1,0:T(8,128)(2,1)S(1)}, u32[]{:S(2)}, u32[]{:S(2)}) collective-permute-start(bf16[80,1152]{1,0:T(8,128)(2,1)S(1)} %get-tuple-element.23), channel_id=1, source_target_pairs={{0,12},{4,8},{8,4},{12,0},{1,13},{5,9},{9,5},{13,1},{2,14},{6,10},... | collective-permute-start | bytes 552968 | tf_op jit(solution)/shard_map/ppermute | solution.py:24
  17.3 20.1 %collective-permute-start.8 = (bf16[128,1152]{1,0:T(8,128)(2,1)S(1)}, bf16[128,1152]{1,0:T(8,128)(2,1)S(1)}, u32[]{:S(2)}, u32[]{:S(2)}) collective-permute-start(bf16[128,1152]{1,0:T(8,128)(2,1)S(1)} %collective-permute-done.7.far.refs_2_), channel_id=1, source_target_pairs={{0,1},{1,0},{2,3},{3,2},{4,5},{5,4},{6,7},{7,6},{8,9},{9,8},{10,11... | collective-permute-start | bytes 884744 | tf_op jit(solution)/shard_map/ppermute | solution.py:24
  18.2 10.2 %collective-permute-start.14 = (bf16[80,1152]{1,0:T(8,128)(2,1)S(1)}, bf16[80,1152]{1,0:T(8,128)(2,1)S(1)}, u32[]{:S(2)}, u32[]{:S(2)}) collective-permute-start(bf16[80,1152]{1,0:T(8,128)(2,1)S(1)} %collective-permute-done.12.refs_4_), channel_id=1, source_target_pairs={{0,2},{1,3},{2,0},{3,1},{4,6},{5,7},{6,4},{7,5},{8,10},{9,11},{10,... | collective-permute-start | bytes 552968 | tf_op jit(solution)/shard_map/ppermute | solution.py:24
  26.4 2.0 %collective-permute-start.13 = (bf16[80,1152]{1,0:T(8,128)(2,1)S(1)}, bf16[80,1152]{1,0:T(8,128)(2,1)S(1)}, u32[]{:S(2)}, u32[]{:S(2)}) collective-permute-start(bf16[80,1152]{1,0:T(8,128)(2,1)S(1)} %collective-permute-done.12.refs_4_), channel_id=1, source_target_pairs={{0,1},{1,0},{2,3},{3,2},{4,5},{5,4},{6,7},{7,6},{8,9},{9,8},{10,11... | collective-permute-start | bytes 552968 | tf_op jit(solution)/shard_map/ppermute | solution.py:24
  26.4 7.5 %collective-permute-start.18 = (bf16[80,1152]{1,0:T(8,128)(2,1)S(1)}, bf16[80,1152]{1,0:T(8,128)(2,1)S(1)}, u32[]{:S(2)}, u32[]{:S(2)}) collective-permute-start(bf16[80,1152]{1,0:T(8,128)(2,1)S(1)} %collective-permute-done.16.refs_8_), channel_id=1, source_target_pairs={{0,2},{1,3},{2,0},{3,1},{4,6},{5,7},{6,4},{7,5},{8,10},{9,11},{10,... | collective-permute-start | bytes 552968 | tf_op jit(solution)/shard_map/ppermute | solution.py:24
  26.8 10.6 %collective-permute-start.22 = (bf16[80,1152]{1,0:T(8,128)(2,1)S(1)}, bf16[80,1152]{1,0:T(8,128)(2,1)S(1)}, u32[]{:S(2)}, u32[]{:S(2)}) collective-permute-start(bf16[80,1152]{1,0:T(8,128)(2,1)S(1)} %collective-permute-done.20.refs_12_), channel_id=1, source_target_pairs={{0,2},{1,3},{2,0},{3,1},{4,6},{5,7},{6,4},{7,5},{8,10},{9,11},{10,... | collective-permute-start | bytes 552968 | tf_op jit(solution)/shard_map/ppermute | solution.py:24
  28.4 12.2 %collective-permute-start.17 = (bf16[80,1152]{1,0:T(8,128)(2,1)S(1)}, bf16[80,1152]{1,0:T(8,128)(2,1)S(1)}, u32[]{:S(2)}, u32[]{:S(2)}) collective-permute-start(bf16[80,1152]{1,0:T(8,128)(2,1)S(1)} %collective-permute-done.16.refs_8_), channel_id=1, source_target_pairs={{0,1},{1,0},{2,3},{3,2},{4,5},{5,4},{6,7},{7,6},{8,9},{9,8},{10,11... | collective-permute-start | bytes 552968 | tf_op jit(solution)/shard_map/ppermute | solution.py:24
  28.4 15.5 %collective-permute-start.21 = (bf16[80,1152]{1,0:T(8,128)(2,1)S(1)}, bf16[80,1152]{1,0:T(8,128)(2,1)S(1)}, u32[]{:S(2)}, u32[]{:S(2)}) collective-permute-start(bf16[80,1152]{1,0:T(8,128)(2,1)S(1)} %collective-permute-done.20.refs_12_), channel_id=1, source_target_pairs={{0,1},{1,0},{2,3},{3,2},{4,5},{5,4},{6,7},{7,6},{8,9},{9,8},{10,11... | collective-permute-start | bytes 552968 | tf_op jit(solution)/shard_map/ppermute | solution.py:24
  33.9 12.1 %collective-permute-start.15 = (bf16[80,1152]{1,0:T(8,128)(2,1)S(1)}, bf16[80,1152]{1,0:T(8,128)(2,1)S(1)}, u32[]{:S(2)}, u32[]{:S(2)}) collective-permute-start(bf16[80,1152]{1,0:T(8,128)(2,1)S(1)} %collective-permute-done.14.refs_6_), channel_id=1, source_target_pairs={{0,1},{1,0},{2,3},{3,2},{4,5},{5,4},{6,7},{7,6},{8,9},{9,8},{10,11... | collective-permute-start | bytes 552968 | tf_op jit(solution)/shard_map/ppermute | solution.py:24
  37.4 10.5 %collective-permute-start.19 = (bf16[80,1152]{1,0:T(8,128)(2,1)S(1)}, bf16[80,1152]{1,0:T(8,128)(2,1)S(1)}, u32[]{:S(2)}, u32[]{:S(2)}) collective-permute-start(bf16[80,1152]{1,0:T(8,128)(2,1)S(1)} %collective-permute-done.18.refs_10_), channel_id=1, source_target_pairs={{0,1},{1,0},{2,3},{3,2},{4,5},{5,4},{6,7},{7,6},{8,9},{9,8},{10,11... | collective-permute-start | bytes 552968 | tf_op jit(solution)/shard_map/ppermute | solution.py:24
  37.4 10.6 %collective-permute-start.23 = (bf16[80,1152]{1,0:T(8,128)(2,1)S(1)}, bf16[80,1152]{1,0:T(8,128)(2,1)S(1)}, u32[]{:S(2)}, u32[]{:S(2)}) collective-permute-start(bf16[80,1152]{1,0:T(8,128)(2,1)S(1)} %collective-permute-done.22.refs_14_), channel_id=1, source_target_pairs={{0,1},{1,0},{2,3},{3,2},{4,5},{5,4},{6,7},{7,6},{8,9},{9,8},{10,11... | collective-permute-start | bytes 552968 | tf_op jit(solution)/shard_map/ppermute | solution.py:24
  40.6 24.1 %collective-permute-start = (bf16[272,256]{1,0:T(8,128)(2,1)S(1)}, bf16[272,256]{1,0:T(8,128)(2,1)S(1)}, u32[]{:S(2)}, u32[]{:S(2)}) collective-permute-start(bf16[272,256]{1,0:T(8,128)(2,1)S(1)} %get-tuple-element.18.refs_0_), channel_id=1, source_target_pairs={{0,4},{4,0},{8,12},{12,8},{1,5},{5,1},{9,13},{13,9},{2,6},{6,2},{1... | collective-permute-start | bytes 417800 | tf_op jit(solution)/shard_map/ppermute | solution.py:24
  43.9 7.3 %collective-permute-start.4 = (bf16[256,256]{1,0:T(8,128)(2,1)S(1)}, bf16[256,256]{1,0:T(8,128)(2,1)S(1)}, u32[]{:S(2)}, u32[]{:S(2)}) collective-permute-start(bf16[256,256]{1,0:T(8,128)(2,1)S(1)} %get-tuple-element.19.refs_4_), channel_id=1, source_target_pairs={{0,8},{4,12},{8,0},{12,4},{1,9},{5,13},{9,1},{13,5},{2,10},{6,14},... | collective-permute-start | bytes 393224 | tf_op jit(solution)/shard_map/ppermute | solution.py:24
  45.9 18.8 %collective-permute-start.2 = (bf16[272,256]{1,0:T(8,128)(2,1)S(1)}, bf16[272,256]{1,0:T(8,128)(2,1)S(1)}, u32[]{:S(2)}, u32[]{:S(2)}) collective-permute-start(bf16[272,256]{1,0:T(8,128)(2,1)S(1)} %collective-permute-done.1.refs_2_), channel_id=1, source_target_pairs={{0,4},{4,0},{8,12},{12,8},{1,5},{5,1},{9,13},{13,9},{2,6},{6,2},{1... | collective-permute-start | bytes 417800 | tf_op jit(solution)/shard_map/ppermute | solution.py:24
  47.9 7.3 %collective-permute-start.10 = (bf16[64,512]{1,0:T(8,128)(2,1)S(1)}, bf16[64,512]{1,0:T(8,128)(2,1)S(1)}, u32[]{:S(2)}, u32[]{:S(2)}) collective-permute-start(bf16[64,512]{1,0:T(8,128)(2,1)S(1)} %shard_map.83.home), channel_id=1, source_target_pairs={{0,8},{4,12},{8,0},{12,4},{1,9},{5,13},{9,1},{13,5},{2,10},{6,14},... | collective-permute-start | bytes 196616 | tf_op jit(solution)/shard_map/ppermute | solution.py:24
  48.0 11.6 %collective-permute-start.9 = (bf16[64,512]{1,0:T(8,128)(2,1)S(1)}, bf16[64,512]{1,0:T(8,128)(2,1)S(1)}, u32[]{:S(2)}, u32[]{:S(2)}) collective-permute-start(bf16[64,512]{1,0:T(8,128)(2,1)S(1)} %shard_map.83.home), channel_id=1, source_target_pairs={{0,4},{4,0},{8,12},{12,8},{1,5},{5,1},{9,13},{13,9},{2,6},{6,2},{1... | collective-permute-start | bytes 196616 | tf_op jit(solution)/shard_map/ppermute | solution.py:24
  51.3 13.4 %collective-permute-start.3 = (bf16[256,256]{1,0:T(8,128)(2,1)S(1)}, bf16[256,256]{1,0:T(8,128)(2,1)S(1)}, u32[]{:S(2)}, u32[]{:S(2)}) collective-permute-start(bf16[256,256]{1,0:T(8,128)(2,1)S(1)} %get-tuple-element.19.refs_4_), channel_id=1, source_target_pairs={{0,4},{4,0},{8,12},{12,8},{1,5},{5,1},{9,13},{13,9},{2,6},{6,2},{1... | collective-permute-start | bytes 393224 | tf_op jit(solution)/shard_map/ppermute | solution.py:24
  55.2 9.5 %collective-permute-start.5 = (bf16[256,256]{1,0:T(8,128)(2,1)S(1)}, bf16[256,256]{1,0:T(8,128)(2,1)S(1)}, u32[]{:S(2)}, u32[]{:S(2)}) collective-permute-start(bf16[256,256]{1,0:T(8,128)(2,1)S(1)} %collective-permute-done.4.refs_6_), channel_id=1, source_target_pairs={{0,4},{4,0},{8,12},{12,8},{1,5},{5,1},{9,13},{13,9},{2,6},{6,2},{1... | collective-permute-start | bytes 393224 | tf_op jit(solution)/shard_map/ppermute | solution.py:24
  59.6 4.3 %collective-permute-start.11 = (bf16[64,512]{1,0:T(8,128)(2,1)S(1)}, bf16[64,512]{1,0:T(8,128)(2,1)S(1)}, u32[]{:S(2)}, u32[]{:S(2)}) collective-permute-start(bf16[64,512]{1,0:T(8,128)(2,1)S(1)} %collective-permute-done.10.second), channel_id=1, source_target_pairs={{0,4},{4,0},{8,12},{12,8},{1,5},{5,1},{9,13},{13,9},{2,6},{6,2},{1... | collective-permute-start | bytes 196616 | tf_op jit(solution)/shard_map/ppermute | solution.py:24
  65.9 2.6 %collective-permute-start.24 = (f32[128,512]{1,0:T(8,128)S(1)}, f32[128,512]{1,0:T(8,128)S(1)}, u32[]{:S(2)}, u32[]{:S(2)}) collective-permute-start(f32[128,512]{1,0:T(8,128)S(1)} %get-tuple-element.26), channel_id=1, source_target_pairs={{0,1},{1,0},{2,3},{3,2},{4,5},{5,4},{6,7},{7,6},{8,9},{9,8},{10,11... | collective-permute-start | bytes 786440 | tf_op jit(solution)/shard_map/ppermute | solution.py:24
  67.9 1.7 %collective-permute-start.27 = (f32[128,512]{1,0:T(8,128)S(1)}, f32[128,512]{1,0:T(8,128)S(1)}, u32[]{:S(2)}, u32[]{:S(2)}) collective-permute-start(f32[128,512]{1,0:T(8,128)S(1)} %get-tuple-element.29), channel_id=1, source_target_pairs={{0,1},{1,0},{2,3},{3,2},{4,5},{5,4},{6,7},{7,6},{8,9},{9,8},{10,11... | collective-permute-start | bytes 786440 | tf_op jit(solution)/shard_map/ppermute | solution.py:24
  68.5 4.5 %collective-permute-start.25 = (bf16[64,512]{1,0:T(8,128)(2,1)S(1)}, bf16[64,512]{1,0:T(8,128)(2,1)S(1)}, u32[]{:S(2)}, u32[]{:S(2)}) collective-permute-start(bf16[64,512]{1,0:T(8,128)(2,1)S(1)} %fusion.1), channel_id=1, source_target_pairs={{0,2},{1,3},{2,0},{3,1},{4,6},{5,7},{6,4},{7,5},{8,10},{9,11},{10,... | collective-permute-start | bytes 196616 | tf_op jit(solution)/shard_map/ppermute | solution.py:24
  69.6 4.8 %collective-permute-start.28 = (bf16[64,512]{1,0:T(8,128)(2,1)S(1)}, bf16[64,512]{1,0:T(8,128)(2,1)S(1)}, u32[]{:S(2)}, u32[]{:S(2)}) collective-permute-start(bf16[64,512]{1,0:T(8,128)(2,1)S(1)} %fusion), channel_id=1, source_target_pairs={{0,2},{1,3},{2,0},{3,1},{4,6},{5,7},{6,4},{7,5},{8,10},{9,11},{10,... | collective-permute-start | bytes 196616 | tf_op jit(solution)/shard_map/ppermute | solution.py:24
  73.0 5.1 %collective-permute-start.26 = (bf16[64,256]{1,0:T(8,128)(2,1)S(1)}, bf16[64,256]{1,0:T(8,128)(2,1)S(1)}, u32[]{:S(2)}, u32[]{:S(2)}) collective-permute-start(bf16[64,256]{1,0:T(8,128)(2,1)S(1)} %fusion.7), channel_id=1, source_target_pairs={{0,4},{4,0},{8,12},{12,8},{1,5},{5,1},{9,13},{13,9},{2,6},{6,2},{1... | collective-permute-start | bytes 98312 | tf_op jit(solution)/shard_map/ppermute | solution.py:24
  74.5 5.1 %collective-permute-start.29 = (bf16[64,256]{1,0:T(8,128)(2,1)S(1)}, bf16[64,256]{1,0:T(8,128)(2,1)S(1)}, u32[]{:S(2)}, u32[]{:S(2)}) collective-permute-start(bf16[64,256]{1,0:T(8,128)(2,1)S(1)} %get-tuple-element.31), channel_id=1, source_target_pairs={{0,8},{4,12},{8,0},{12,4},{1,9},{5,13},{9,1},{13,5},{2,10},{6,14},... | collective-permute-start | bytes 98312 | tf_op jit(solution)/shard_map/ppermute | solution.py:24
  77.5 5.7 %collective-permute-start.30 = (bf16[64,256]{1,0:T(8,128)(2,1)S(1)}, bf16[64,256]{1,0:T(8,128)(2,1)S(1)}, u32[]{:S(2)}, u32[]{:S(2)}) collective-permute-start(bf16[64,256]{1,0:T(8,128)(2,1)S(1)} %get-tuple-element.32), channel_id=1, source_target_pairs={{0,12},{4,8},{8,4},{12,0},{1,13},{5,9},{9,5},{13,1},{2,14},{6,10},... | collective-permute-start | bytes 98312 | tf_op jit(solution)/shard_map/ppermute | solution.py:24
  (1 other events, 13.5 us)
